TPU v7x, 32 devices: a whole 2x2x4 slice. The times are simulated.
32 devices in a mesh: section: 4 (over z), dp: 8 (over y, x, core).
Axes of the slice: x: 2, y: 2, z: 4, core: 2. Of those that a mesh axis runs over, the one named last changes fastest.
Arguments:
- feed_down: bfloat16 [4, 512, 4096], P('section', 'dp'), may hold values from -6 to 6
- feed_up: bfloat16 [4, 512, 4096], P('section', 'dp'), may hold values from -6 to 6
- cotangent_down: bfloat16 [4, 512, 4096], P('section', 'dp'), may hold values from -6 to 6
- cotangent_up: bfloat16 [4, 512, 4096], P('section', 'dp'), may hold values from -6 to 6
- roster: int32 [4, 2, 2], P('section'), may hold values from 0 to 1, each once within a row
- value_weight: bfloat16 [4, 4096, 512], P('section'), may hold values from -0.09375 to 0.09375
Outputs:
- next_down: bfloat16 [4, 512, 4096], P('section', 'dp')
- next_up: bfloat16 [4, 512, 4096], P('section', 'dp')
- back_down: bfloat16 [4, 512, 4096], P('section', 'dp')
- back_up: bfloat16 [4, 512, 4096], P('section', 'dp')
- grad_weight: float32 [4, 4096, 512], P('section', 'dp')
Inputs may be any that keep to these rules, and one draw needn't show every extreme that they name: roster[s, 0, :] and roster[s, 1, :] are each a permutation of the 2 micro-batches: block j of the cotangents that section index s receives for a leg belongs to micro-batch roster[s, leg, j].
All inputs are finite; a program needn't handle non-finite values.
Results may differ from a plain program's by a relative error of at most 0.005.
Values may be sent and summed in bfloat16 or wider, within the bound.
No kernel may reach another device: no remote copies, remote signals or barrier semaphores. Data moves between devices by JAX's collectives and lax.ppermute only.
A program may use at most 64 MiB of HBM per device.

v0:
```python
import jax
import jax.numpy as jnp
from jax import lax
from jax.sharding import PartitionSpec as P

KVH = 4
HD = 128
GROUPS = 8


EPSILON = 1e-05


def passed_along(shard, axis, by):
    count = lax.axis_size(axis)
    return lax.ppermute(shard, axis, [(i, (i + by) % count) for i in range(count)])


def normalize(inputs):
    values = inputs.astype(jnp.float32)
    inverse = lax.rsqrt(jnp.mean(values * values, axis=-1, keepdims=True) + EPSILON)
    return (values * inverse, inverse)


def arrange(received, roster_row):
    blocks = roster_row.shape[0]
    match_table = (roster_row[:, None] == jnp.arange(blocks, dtype=jnp.int32)[None, :]).astype(
        jnp.bfloat16
    )
    shaped = received.reshape(blocks, -1)
    placed = jnp.einsum("jx,jm->mx", shaped, match_table, preferred_element_type=jnp.float32)
    return placed.astype(jnp.bfloat16).reshape(received.shape)


def one_leg(inputs, grads, weight):
    scaled, inverse = normalize(inputs)
    normed = scaled.astype(jnp.bfloat16)
    values = jnp.dot(normed, weight, preferred_element_type=jnp.float32)
    row_total = inputs.shape[0]
    spread = jnp.broadcast_to(
        values.reshape(row_total, KVH, 1, HD), (row_total, KVH, GROUPS, HD)
    ).reshape(row_total, -1)
    advanced = (inputs.astype(jnp.float32) + spread).astype(jnp.bfloat16)
    grouped = (
        jnp.sum(grads.astype(jnp.float32).reshape(row_total, KVH, GROUPS, HD), axis=2)
        .reshape(row_total, -1)
        .astype(jnp.bfloat16)
    )
    back_norm = lax.dot_general(
        grouped, weight, (((1,), (1,)), ((), ())), preferred_element_type=jnp.float32
    )
    through = inverse * (back_norm - scaled * jnp.mean(back_norm * scaled, axis=-1, keepdims=True))
    behind = (grads.astype(jnp.float32) + through).astype(jnp.bfloat16)
    return (advanced, behind, normed, grouped)


def on_device(feed_down, feed_up, cotangent_down, cotangent_up, roster, value_weight):
    inputs_down, raw_up = passed_along((feed_down[0], cotangent_up[0]), "section", 1)
    inputs_up, raw_down = passed_along((feed_up[0], cotangent_down[0]), "section", -1)
    weight = value_weight[0]
    grads_down = arrange(raw_down, roster[0, 0])
    grads_up = arrange(raw_up, roster[0, 1])
    advanced_down, behind_down, normed_down, grouped_down = one_leg(inputs_down, grads_down, weight)
    advanced_up, behind_up, normed_up, grouped_up = one_leg(inputs_up, grads_up, weight)
    normed_all = jnp.concatenate([normed_down, normed_up], axis=0)
    grouped_all = jnp.concatenate([grouped_down, grouped_up], axis=0)
    local_rows = normed_all.shape[0]
    members = lax.axis_size("dp")
    factor = float(local_rows * members) ** (-0.5)
    slices = lax.all_to_all(normed_all, "dp", split_axis=1, concat_axis=0, tiled=True)
    summed = lax.dot_general(
        slices,
        lax.all_gather(grouped_all, "dp", axis=0, tiled=True),
        (((0,), (0,)), ((), ())),
        preferred_element_type=jnp.float32,
    )
    return (
        advanced_down[None],
        advanced_up[None],
        behind_down[None],
        behind_up[None],
        (summed * factor)[None],
    )


def solution(mesh):
    placed = (
        P("section", "dp", None),
        P("section", "dp", None),
        P("section", "dp", None),
        P("section", "dp", None),
        P("section", None, None),
        P("section", None, None),
    )
    return jax.shard_map(
        on_device,
        mesh=mesh,
        in_specs=placed,
        out_specs=(
            P("section", "dp", None),
            P("section", "dp", None),
            P("section", "dp", None),
            P("section", "dp", None),
            P("section", "dp", None),
        ),
        check_vma=False,
    )
```

profile of v0, /device:TPU:0, one launch (start us, length us, event | category | flops | bytes accessed | tf_op | source)
XLA Modules:
  0.0 110.4 jit_solution(12762359681367115548)
XLA Ops:
  7.2 5.1 %collective-permute-start.2 = (bf16[64,4096]{1,0:T(8,128)(2,1)}, bf16[64,4096]{1,0:T(8,128)(2,1)S(1)}, u32[]{:S(2)}, u32[]{:S(2)}) collective-permute-start(bf16[64,4096]{1,0:T(8,128)(2,1)} %bitcast.84), channel_id=1, source_target_pairs={{0,24},{8,0},{16,8},{24,16},{1,25},{9,1},{17,9},{25,17},{2,26},{10... | collective-permute-start | bytes 1572872 | tf_op jit(solution)/shard_map/ppermute | solution.py:16
  12.3 3.8 %collective-permute-start.1 = (bf16[64,4096]{1,0:T(8,128)(2,1)}, bf16[64,4096]{1,0:T(8,128)(2,1)S(1)}, u32[]{:S(2)}, u32[]{:S(2)}) collective-permute-start(bf16[64,4096]{1,0:T(8,128)(2,1)} %bitcast.87), channel_id=1, source_target_pairs={{0,24},{8,0},{16,8},{24,16},{1,25},{9,1},{17,9},{25,17},{2,26},{10... | collective-permute-start | bytes 1572872 | tf_op jit(solution)/shard_map/ppermute | solution.py:16
  16.2 0.8 slice_bitcast_fusion
  16.9 6.4 %copy.20 = bf16[512,4096]{1,0:T(8,128)(2,1)} copy(bf16[512,4096]{0,1:T(8,128)(2,1)} %bitcast.73) | data formatting | bytes 8388608 | tf_op jit(solution)/shard_map/reshape.37
  23.3 1.6 %collective-permute-done.2 = bf16[64,4096]{1,0:T(8,128)(2,1)S(1)} collective-permute-done((bf16[64,4096]{1,0:T(8,128)(2,1)}, bf16[64,4096]{1,0:T(8,128)(2,1)S(1)}, u32[]{:S(2)}, u32[]{:S(2)}) %collective-permute-start.2) | collective-permute-done | bytes 524320 | tf_op jit(solution)/shard_map/ppermute | solution.py:16
  25.0 0.4 reshape.100
  25.4 1.2 %convolution_convert_fusion.1 = bf16[2,131072]{1,0:T(2,128)(2,1)S(1)} fusion(bf16[2,131072]{1,0:T(2,128)(2,1)S(1)} %reshape.100, s32[2]{0:T(128)S(1)} %get-tuple-element.10), kind=kOutput, calls=%fused_computation.1 | convolution fusion | flops 1310724 | bytes 1048584 | tf_op jit(solution)/shard_map/jx,jm->mx/dot_general | solution.py:31
  26.6 1.2 %convert_element_type.95 = bf16[64,4,8,128]{3,2,1,0:T(8,128)(2,1)} reshape(bf16[2,131072]{1,0:T(2,128)(2,1)S(1)} %convolution_convert_fusion.1) | data formatting | bytes 1048576 | tf_op jit(solution)/shard_map/convert_element_type | solution.py:53
  28.0 9.1 %collective-permute-done.3 = bf16[64,4096]{1,0:T(8,128)(2,1)S(1)} collective-permute-done((bf16[64,4096]{1,0:T(8,128)(2,1)}, bf16[64,4096]{1,0:T(8,128)(2,1)S(1)}, u32[]{:S(2)}, u32[]{:S(2)}) %collective-permute-start.3) | collective-permute-done | bytes 524320 | tf_op jit(solution)/shard_map/ppermute | solution.py:16
  37.1 1.2 %reshape.101 = bf16[2,131072]{1,0:T(2,128)(2,1)} reshape(bf16[64,4096]{1,0:T(8,128)(2,1)S(1)} %collective-permute-done.3) | data formatting | bytes 1048576 | tf_op jit(solution)/shard_map/reshape | solution.py:30
  38.3 2.0 %convolution_convert_fusion = bf16[2,131072]{1,0:T(2,128)(2,1)S(1)} fusion(bf16[2,131072]{1,0:T(2,128)(2,1)} %reshape.101, s32[2]{0:T(128)S(1)} %get-tuple-element.9), kind=kOutput, calls=%fused_computation | convolution fusion | flops 1310724 | bytes 1048584 | tf_op jit(solution)/shard_map/jx,jm->mx/dot_general | solution.py:31
  40.3 0.8 copy-done.2
  41.0 1.2 %convert_element_type.103 = bf16[64,4,8,128]{3,2,1,0:T(8,128)(2,1)} reshape(bf16[2,131072]{1,0:T(2,128)(2,1)S(1)} %convolution_convert_fusion) | data formatting | bytes 1048576 | tf_op jit(solution)/shard_map/convert_element_type | solution.py:53
  42.2 1.3 %reshape.103 = f32[64,4096]{1,0:T(8,128)S(1)} reshape(bf16[2,131072]{1,0:T(2,128)(2,1)} %copy-done.2) | data formatting | bytes 1572864 | tf_op jit(solution)/shard_map/convert_element_type | solution.py:53
  43.5 4.8 %collective-permute-done = bf16[64,4096]{1,0:T(8,128)(2,1)S(1)} collective-permute-done((bf16[64,4096]{1,0:T(8,128)(2,1)}, bf16[64,4096]{1,0:T(8,128)(2,1)S(1)}, u32[]{:S(2)}, u32[]{:S(2)}) %collective-permute-start) | collective-permute-done | bytes 524320 | tf_op jit(solution)/shard_map/ppermute | solution.py:16
  48.5 9.1 %collective-permute-done.1 = bf16[64,4096]{1,0:T(8,128)(2,1)S(1)} collective-permute-done((bf16[64,4096]{1,0:T(8,128)(2,1)}, bf16[64,4096]{1,0:T(8,128)(2,1)S(1)}, u32[]{:S(2)}, u32[]{:S(2)}) %collective-permute-start.1) | collective-permute-done | bytes 524320 | tf_op jit(solution)/shard_map/ppermute | solution.py:16
  57.8 1.4 %reduce = bf16[64,4,128]{2,1,0:T(4,128)(2,1)S(1)} reduce(bf16[64,4,8,128]{3,2,1,0:T(8,128)(2,1)} %convert_element_type.95, bf16[]{:T(256)} %constant.18), dimensions={2}, to_apply=%region_2.0.clone | reduce | flops 229376 | bytes 589826 | tf_op jit(solution)/shard_map/reduce_sum | solution.py:45
  59.2 1.4 %reduce.1 = bf16[64,4,128]{2,1,0:T(4,128)(2,1)S(1)} reduce(bf16[64,4,8,128]{3,2,1,0:T(8,128)(2,1)} %convert_element_type.103, bf16[]{:T(256)} %constant.18), dimensions={2}, to_apply=%region_4.0.clone | reduce | flops 229376 | bytes 589826 | tf_op jit(solution)/shard_map/reduce_sum | solution.py:45
  60.7 3.8 %fusion.16 = (f32[64]{0:T(128)S(1)}, f32[64,4096]{1,0:T(8,128)S(1)}) fusion(bf16[64,4096]{1,0:T(8,128)(2,1)S(1)} %collective-permute-done, f32[64]{0:T(128)S(1)} %add_rsqrt_fusion.1, bf16[1,4096,512]{2,1,0:T(8,128)(2,1)} %param.11, bf16[8,8,4,128]{3,2,1,0:T(4,128)(2,1)S(1)} %bitcast.83), kind=kOutput, calls=%fused_computation.25 | convolution fusion | flops 269483968 | bytes 5833216 | tf_op jit(solution)/shard_map/dot_general | solution.py:49
  64.6 1.5 %fusion.11 = (f32[64]{0:T(128)S(1)}, f32[64,4096]{1,0:T(8,128)S(1)}) fusion(bf16[64,4096]{1,0:T(8,128)(2,1)S(1)} %collective-permute-done.1, f32[64]{0:T(128)S(1)} %add_rsqrt_fusion, bf16[1,4096,512]{2,1,0:T(8,128)(2,1)S(1)} %copy-done, bf16[8,8,4,128]{3,2,1,0:T(4,128)(2,1)S(1)} %bitcast.81), kind=kOutput, calls=%fused_computation.20 | convolution fusion | flops 269483968 | bytes 5833216 | tf_op jit(solution)/shard_map/dot_general | solution.py:49
  66.1 1.1 %fusion.27 = (bf16[1,64,4096]{2,1,0:T(8,128)(2,1)}, bf16[64,4096]{1,0:T(8,128)(2,1)S(1)}) fusion(f32[64,4096]{1,0:T(8,128)S(1)} %reshape.102, f32[64,4096]{1,0:T(8,128)S(1)} %get-tuple-element.12, bf16[64,4096]{1,0:T(8,128)(2,1)S(1)} %collective-permute-done, f32[64]{0:T(128)S(1)} %broadcast_multiply_fusion.1, f32[64]{0:T(128)S(1)} %add_rsqrt_fusion.1), kind=kLoop, calls=%fused_computation.38 | loop fusion | flops 2097152 | bytes 3670528 | tf_op jit(solution)/shard_map/broadcast_in_dim | solution.py:80
  67.2 1.1 %fusion.28 = (bf16[1,64,4096]{2,1,0:T(8,128)(2,1)}, bf16[64,4096]{1,0:T(8,128)(2,1)S(1)}) fusion(f32[64,4096]{1,0:T(8,128)S(1)} %reshape.103, f32[64,4096]{1,0:T(8,128)S(1)} %get-tuple-element.14, bf16[64,4096]{1,0:T(8,128)(2,1)S(1)} %collective-permute-done.1, f32[64]{0:T(128)S(1)} %broadcast_multiply_fusion, f32[64]{0:T(128)S(1)} %add_rsqrt_fusion), kind=kLoop, calls=%fused_computation.39 | loop fusion | flops 2097152 | bytes 3670528 | tf_op jit(solution)/shard_map/broadcast_in_dim | solution.py:81
  68.4 1.4 %fusion.29 = f32[64,4,128]{2,0,1:T(8,128)S(1)} fusion(bf16[4,128,4096]{2,1,0:T(8,128)(2,1)S(1)} %bitcast.74, bf16[64,4096]{1,0:T(8,128)(2,1)S(1)} %get-tuple-element.6), kind=kOutput, calls=%fused_computation.40 | convolution fusion | flops 268435456 | bytes 4849664 | tf_op jit(solution)/shard_map/dot_general | solution.py:38
  69.8 1.4 %fusion.31 = f32[64,4,128]{2,0,1:T(8,128)S(1)} fusion(bf16[4,128,4096]{2,1,0:T(8,128)(2,1)S(1)} %bitcast.75, bf16[64,4096]{1,0:T(8,128)(2,1)S(1)} %get-tuple-element.8), kind=kOutput, calls=%fused_computation.42 | convolution fusion | flops 268435456 | bytes 4849664 | tf_op jit(solution)/shard_map/dot_general | solution.py:38
  71.2 0.7 pad_maximum_fusion.1
  71.9 1.1 copy.41
  73.0 3.7 %all-to-all-start = ((bf16[128,8,512]{2,0,1:T(8,128)(2,1)}), bf16[128,8,512]{2,0,1:T(8,128)(2,1)S(1)}, u32[]{:S(2)}, u32[]{:S(2)}) async-start(bf16[128,8,512]{2,0,1:T(8,128)(2,1)} %bitcast.72), calls=%async_computation | async-start | bytes 2097152 | tf_op jit(solution)/shard_map/all_to_all | solution.py:70
  77.0 1.4 %fusion.25 = bf16[1,64,4096]{2,1,0:T(8,128)(2,1)} fusion(f32[8,8,32,128]{3,2,1,0:T(8,128)S(1)} %bitcast.77, bf16[64,4096]{1,0:T(8,128)(2,1)S(1)} %collective-permute-done.1), kind=kLoop, calls=%fused_computation.36 | loop fusion | flops 786432 | bytes 2097152 | tf_op jit(solution)/shard_map/broadcast_in_dim | solution.py:79
  78.6 1.4 %fusion.26 = bf16[1,64,4096]{2,1,0:T(8,128)(2,1)} fusion(f32[8,8,32,128]{3,2,1,0:T(8,128)S(1)} %bitcast.78, bf16[64,4096]{1,0:T(8,128)(2,1)S(1)} %collective-permute-done), kind=kLoop, calls=%fused_computation.37 | loop fusion | flops 786432 | bytes 2097152 | tf_op jit(solution)/shard_map/broadcast_in_dim | solution.py:78
  80.0 13.5 %all-to-all-done = bf16[128,8,512]{2,0,1:T(8,128)(2,1)S(1)} async-done(((bf16[128,8,512]{2,0,1:T(8,128)(2,1)}), bf16[128,8,512]{2,0,1:T(8,128)(2,1)S(1)}, u32[]{:S(2)}, u32[]{:S(2)}) %all-to-all-start) | async-done | bytes 1048608 | tf_op jit(solution)/shard_map/all_to_all | solution.py:70
  93.4 7.2 %all-gather.2.cloned.1.call-done = bf16[1024,512]{1,0:T(8,128)(2,1)} async-done(((bf16[128,512]{1,0:T(8,128)(2,1)}), bf16[1024,512]{1,0:T(8,128)(2,1)}) %all-gather.2.cloned.1.call-update) | async-done | bytes 1048592 | tf_op jit(solution)/shard_map/all_gather | solution.py:73
  100.6 2.9 %fusion.10 = f32[1,512,512]{2,1,0:T(8,128)} fusion(bf16[1024,512]{1,0:T(8,128)(2,1)S(1)} %bitcast.79, bf16[1024,512]{1,0:T(8,128)(2,1)} %all-gather.2.cloned.1.call-done), kind=kOutput, calls=%fused_computation.19 | convolution fusion | flops 537133056 | bytes 3145728 | tf_op jit(solution)/shard_map/dot_general | solution.py:71
  (22 shorter events, 1.4 us)
Async XLA Ops:
  7.2 93.5 %all-gather.2.cloned.1.call-start = ((), (), s32[]{:S(2)}) async-start(), calls=%async_computation.1 | async-start | bytes 1179648 | tf_op jit(solution)/shard_map/all_gather | solution.py:73
  7.2 17.8 %collective-permute-start.2 = (bf16[64,4096]{1,0:T(8,128)(2,1)}, bf16[64,4096]{1,0:T(8,128)(2,1)S(1)}, u32[]{:S(2)}, u32[]{:S(2)}) collective-permute-start(bf16[64,4096]{1,0:T(8,128)(2,1)} %bitcast.84), channel_id=1, source_target_pairs={{0,24},{8,0},{16,8},{24,16},{1,25},{9,1},{17,9},{25,17},{2,26},{10... | collective-permute-start | bytes 1572872 | tf_op jit(solution)/shard_map/ppermute | solution.py:16
  12.3 24.8 %collective-permute-start.3 = (bf16[64,4096]{1,0:T(8,128)(2,1)}, bf16[64,4096]{1,0:T(8,128)(2,1)S(1)}, u32[]{:S(2)}, u32[]{:S(2)}) collective-permute-start(bf16[64,4096]{1,0:T(8,128)(2,1)} %bitcast.85), channel_id=1, source_target_pairs={{0,8},{8,16},{16,24},{24,0},{1,9},{9,17},{17,25},{25,1},{2,10},{10... | collective-permute-start | bytes 1572872 | tf_op jit(solution)/shard_map/ppermute | solution.py:16
  12.3 35.9 %collective-permute-start = (bf16[64,4096]{1,0:T(8,128)(2,1)}, bf16[64,4096]{1,0:T(8,128)(2,1)S(1)}, u32[]{:S(2)}, u32[]{:S(2)}) collective-permute-start(bf16[64,4096]{1,0:T(8,128)(2,1)} %bitcast.86), channel_id=1, source_target_pairs={{0,8},{8,16},{16,24},{24,0},{1,9},{9,17},{17,25},{25,1},{2,10},{10... | collective-permute-start | bytes 1572872 | tf_op jit(solution)/shard_map/ppermute | solution.py:16
  12.3 45.2 %collective-permute-start.1 = (bf16[64,4096]{1,0:T(8,128)(2,1)}, bf16[64,4096]{1,0:T(8,128)(2,1)S(1)}, u32[]{:S(2)}, u32[]{:S(2)}) collective-permute-start(bf16[64,4096]{1,0:T(8,128)(2,1)} %bitcast.87), channel_id=1, source_target_pairs={{0,24},{8,0},{16,8},{24,16},{1,25},{9,1},{17,9},{25,17},{2,26},{10... | collective-permute-start | bytes 1572872 | tf_op jit(solution)/shard_map/ppermute | solution.py:16
  40.2 0.8 copy-start.2
  60.7 3.9 %copy-start = (bf16[1,4096,512]{2,1,0:T(8,128)(2,1)S(1)}, bf16[1,4096,512]{2,1,0:T(8,128)(2,1)}, u32[]{:S(2)}) copy-start(bf16[1,4096,512]{2,1,0:T(8,128)(2,1)} %param.11) | copy-start | bytes 12582916
  66.0 2.4 %copy-start.1 = (bf16[512,4096]{1,0:T(8,128)(2,1)S(1)}, bf16[512,4096]{1,0:T(8,128)(2,1)}, u32[]{:S(2)}) copy-start(bf16[512,4096]{1,0:T(8,128)(2,1)} %copy.20) | copy-start | bytes 12582916
  73.0 20.5 %all-to-all-start = ((bf16[128,8,512]{2,0,1:T(8,128)(2,1)}), bf16[128,8,512]{2,0,1:T(8,128)(2,1)S(1)}, u32[]{:S(2)}, u32[]{:S(2)}) async-start(bf16[128,8,512]{2,0,1:T(8,128)(2,1)} %bitcast.72), calls=%async_computation | async-start | bytes 2097152 | tf_op jit(solution)/shard_map/all_to_all | solution.py:70
Sparse Core Ops, SparseCore 0:
  72.0 28.5 all-gather.1
where the time goes:
time: 111 us; the launch traced here: 110 us
  waiting for transfers between devices  45.3 us (41%)
  local copies, waits for them, and re-layouts  15 us (14%)
  matrix products  14.2 us (13%)
  between operations  14.2 us (13%)
  starting transfers between devices  12.7 us (11%)
  other arithmetic  9.07 us (8%)
    ppermute x4, waiting for transfers between devices, passed_along(): lax.ppermute(shard, axis, [(i, (i + by) % count) for i in range(count)])  24.6 us
    all_to_all x1, waiting for transfers between devices, on_device(): lax.all_to_all(normed_all, 'dp', split_axis=1, concat_axis=0, tiled=True)  13.5 us
    ppermute x4, starting transfers between devices, passed_along(): lax.ppermute(shard, axis, [(i, (i + by) % count) for i in range(count)])  8.98 us
    all_gather x1, waiting for transfers between devices, on_device(): lax.all_gather(grouped_all, 'dp', axis=0, tiled=True)  7.19 us
    another operation x1, local copies, waits for them, and re-layouts  6.38 us
    dot_general x2, matrix products, one_leg(): lax.dot_general(grouped, weight, (((1,), (1,)), ((), ())), preferred_elem...  5.3 us
    convert_element_type x4, local copies, waits for them, and re-layouts, one_leg(): behind = (grads.astype(jnp.float32) + through).astype(jnp.bfloat16)  3.94 us
    all_to_all x1, starting transfers between devices, on_device(): lax.all_to_all(normed_all, 'dp', split_axis=1, concat_axis=0, tiled=True)  3.73 us
  transfers between devices with their start and end apart: 6, of which 6 were waited for; matrix products, arithmetic and copies ran while one was open for 18% of the time, Pallas kernels for 0%

commit v1 on v0

v1 whole, which is shorter than its diff:
```python
import functools

import jax
import jax.numpy as jnp
from jax import lax
from jax.experimental import pallas as pl
from jax.experimental.pallas import tpu as pltpu
from jax.sharding import PartitionSpec as P


KVH = 4
HD = 128
GROUPS = 8


EPSILON = 1e-05


MIB = 2**20


def passed_along(shard, axis, by):
    count = lax.axis_size(axis)
    return lax.ppermute(shard, axis, [(i, (i + by) % count) for i in range(count)])


def whole_vmem():
    return pl.BlockSpec(memory_space=pltpu.VMEM)


def group_kernel(down_ref, up_ref, down_out, up_out):
    for src, dst in ((down_ref, down_out), (up_ref, up_out)):
        for k in range(KVH):
            total = src[:, k * GROUPS * HD : (k * GROUPS + 1) * HD].astype(jnp.float32)
            for j in range(1, GROUPS):
                at = (k * GROUPS + j) * HD
                total = total + src[:, at : at + HD].astype(jnp.float32)
            dst[:, k * HD : (k + 1) * HD] = total.astype(dst.dtype)


def group_sums(down, up):
    rows, width = down.shape
    step = rows // 2
    wide = pl.BlockSpec((step, width), lambda i: (i, 0))
    narrow = pl.BlockSpec((step, width // GROUPS), lambda i: (i, 0))
    out = jax.ShapeDtypeStruct((rows, width // GROUPS), down.dtype)
    return pl.pallas_call(
        group_kernel,
        grid=(rows // step,),
        in_specs=[wide, wide],
        out_specs=[narrow, narrow],
        out_shape=[out, out],
        name="group_sums",
        compiler_params=pltpu.CompilerParams(vmem_limit_bytes=6 * MIB),
        cost_estimate=pl.CostEstimate(
            flops=2 * rows * width, bytes_accessed=4 * rows * width, transcendentals=0
        ),
    )(down, up)


def normalize_kernel(members, x_ref, out_ref):
    x = x_ref[...].astype(jnp.float32)
    inverse = lax.rsqrt(jnp.mean(x * x, axis=-1, keepdims=True) + EPSILON)
    width = x.shape[1] // members
    for p in range(members):
        part = x_ref[:, p * width : (p + 1) * width].astype(jnp.float32)
        out_ref[p] = (part * inverse).astype(out_ref.dtype)


def normalized_slices(x, members):
    rows, width = x.shape
    return pl.pallas_call(
        functools.partial(normalize_kernel, members),
        in_specs=[whole_vmem()],
        out_specs=whole_vmem(),
        out_shape=jax.ShapeDtypeStruct((members, rows, width // members), x.dtype),
        name="normalized_slices",
        compiler_params=pltpu.CompilerParams(vmem_limit_bytes=4 * MIB),
        cost_estimate=pl.CostEstimate(
            flops=4 * rows * width, bytes_accessed=4 * rows * width, transcendentals=rows
        ),
    )(x)


def span_kernel(
    down_ref, up_ref, grouped_ref, weight_ref,
    next_down, next_up, through_down, through_up,
    scaled, normed, back, values, inner,
):
    step = pl.program_id(0)
    rows = down_ref.shape[0]
    tile = weight_ref.shape[0]

    @pl.when(step == 0)
    def _():
        values[...] = jnp.zeros_like(values)
        inner[...] = jnp.zeros_like(inner)
        for leg, ref in enumerate((down_ref, up_ref)):
            x = ref[...].astype(jnp.float32)
            inverse = lax.rsqrt(jnp.mean(x * x, axis=-1, keepdims=True) + EPSILON)
            own = slice(leg * rows, (leg + 1) * rows)
            scaled[own, :] = x * inverse
            normed[own, :] = (x * inverse).astype(normed.dtype)

    columns = pl.ds(pl.multiple_of(step * tile, tile), tile)
    weight = weight_ref[...]
    values[...] += jnp.dot(normed[:, columns], weight, preferred_element_type=jnp.float32)
    part = lax.dot_general(
        grouped_ref[...], weight, (((1,), (1,)), ((), ())), preferred_element_type=jnp.float32
    )
    back[:, columns] = part
    inner[...] += jnp.sum(part * scaled[:, columns], axis=-1, keepdims=True)

    @pl.when(step == pl.num_programs(0) - 1)
    def _():
        width = down_ref.shape[1]
        for leg, (ref, nxt, thr) in enumerate(
            ((down_ref, next_down, through_down), (up_ref, next_up, through_up))
        ):
            own = slice(leg * rows, (leg + 1) * rows)
            x = ref[...].astype(jnp.float32)
            inverse = lax.rsqrt(jnp.mean(x * x, axis=-1, keepdims=True) + EPSILON)
            mean = inner[own, :] * (1.0 / width)
            for c in range(width // HD):
                at = slice(c * HD, (c + 1) * HD)
                k = c // GROUPS
                nxt[:, at] = (
                    ref[:, at].astype(jnp.float32) + values[own, k * HD : (k + 1) * HD]
                ).astype(nxt.dtype)
                thr[:, at] = inverse * (back[own, at] - scaled[own, at] * mean)


def span(down, up, grouped, weight):
    rows, width = down.shape
    inner = weight.shape[1]
    tile = 512 if width % 512 == 0 else width
    whole = pl.BlockSpec((rows, width), lambda i: (0, 0))
    return pl.pallas_call(
        span_kernel,
        grid=(width // tile,),
        in_specs=[
            whole_vmem(),
            whole_vmem(),
            whole_vmem(),
            pl.BlockSpec((tile, inner), lambda i: (i, 0)),
        ],
        out_specs=[whole, whole, whole_vmem(), whole_vmem()],
        out_shape=[jax.ShapeDtypeStruct((rows, width), down.dtype)] * 2
        + [jax.ShapeDtypeStruct((rows, width), jnp.float32)] * 2,
        scratch_shapes=[
            pltpu.VMEM((2 * rows, width), jnp.float32),
            pltpu.VMEM((2 * rows, width), down.dtype),
            pltpu.VMEM((2 * rows, width), jnp.float32),
            pltpu.VMEM((2 * rows, inner), jnp.float32),
            pltpu.VMEM((2 * rows, 1), jnp.float32),
        ],
        compiler_params=pltpu.CompilerParams(vmem_limit_bytes=24 * MIB),
        name="span",
        cost_estimate=pl.CostEstimate(
            flops=8 * rows * width * inner,
            bytes_accessed=2 * width * inner + 16 * rows * width,
            transcendentals=2 * rows,
        ),
    )(down, up, grouped, weight)


def weight_kernel(factor, me_ref, down_ref, up_ref, own_ref, other_ref, out_ref):
    chips = own_ref.shape[0]
    chip = me_ref[0] // 2
    core = me_ref[0] % 2
    total = jnp.zeros(out_ref.shape, jnp.float32)
    over_tokens = (((0,), (0,)), ((), ()))
    for c in range(chips):
        same = (chip ^ c) * 2 + core
        other = (chip ^ c) * 2 + 1 - core
        normed = jnp.concatenate(
            [down_ref[same], up_ref[same], down_ref[other], up_ref[other]], axis=0
        )
        grouped = jnp.concatenate([own_ref[c], other_ref[c]], axis=0)
        total = total + lax.dot_general(
            normed, grouped, over_tokens, preferred_element_type=jnp.float32
        )
    out_ref[...] = total * factor


def weight_gradient(normed_down, normed_up, own, other, me, factor):
    members, rows, width = normed_down.shape
    inner = own.shape[-1]
    return pl.pallas_call(
        functools.partial(weight_kernel, factor),
        in_specs=[pl.BlockSpec(memory_space=pltpu.SMEM)] + [whole_vmem()] * 4,
        out_specs=whole_vmem(),
        out_shape=jax.ShapeDtypeStruct((width, inner), jnp.float32),
        name="weight_gradient",
        compiler_params=pltpu.CompilerParams(vmem_limit_bytes=16 * MIB),
        cost_estimate=pl.CostEstimate(
            flops=4 * members * rows * width * inner,
            bytes_accessed=4 * members * rows * (width + inner) + 4 * width * inner,
            transcendentals=0,
        ),
    )(me, normed_down, normed_up, own, other)


def chosen_blocks(blocks_ref, match_ref, m):
    chosen = blocks_ref[0].astype(jnp.float32)
    for j in range(1, blocks_ref.shape[0]):
        mine = match_ref[m, j : j + 1, 0:1] != 0
        chosen = jnp.where(mine, blocks_ref[j].astype(jnp.float32), chosen)
    return chosen


def arrange_kernel(match_down, match_up, down_ref, up_ref, out_ref):
    blocks, rows, _ = down_ref.shape
    for leg, (match, ref) in enumerate(((match_down, down_ref), (match_up, up_ref))):
        for m in range(blocks):
            at = (leg * blocks + m) * rows
            out_ref[at : at + rows, :] = chosen_blocks(ref, match, m).astype(out_ref.dtype)


def arranged_sums(down, up, match_down, match_up):
    rows, width = down.shape
    blocks = match_down.shape[0]
    return pl.pallas_call(
        arrange_kernel,
        in_specs=[whole_vmem()] * 4,
        out_specs=whole_vmem(),
        out_shape=jax.ShapeDtypeStruct((2 * rows, width), down.dtype),
        name="arranged_sums",
        compiler_params=pltpu.CompilerParams(vmem_limit_bytes=4 * MIB),
        cost_estimate=pl.CostEstimate(
            flops=4 * rows * width, bytes_accessed=8 * rows * width, transcendentals=0
        ),
    )(
        match_down,
        match_up,
        down.reshape(blocks, rows // blocks, width),
        up.reshape(blocks, rows // blocks, width),
    )


def finish_kernel(match_ref, raw_ref, through_ref, out_ref):
    m = pl.program_id(0)
    total = chosen_blocks(raw_ref, match_ref, m) + through_ref[m]
    out_ref[0] = total.astype(out_ref.dtype)


def finished(raw, match, through):
    rows, width = raw.shape
    blocks = match.shape[0]
    cut = (blocks, rows // blocks, width)
    return pl.pallas_call(
        finish_kernel,
        grid=(blocks,),
        in_specs=[whole_vmem()] * 3,
        out_specs=pl.BlockSpec((1,) + cut[1:], lambda m: (m, 0, 0)),
        out_shape=jax.ShapeDtypeStruct(cut, raw.dtype),
        name="finished",
        compiler_params=pltpu.CompilerParams(vmem_limit_bytes=4 * MIB),
        cost_estimate=pl.CostEstimate(
            flops=2 * rows * width, bytes_accessed=8 * rows * width, transcendentals=0
        ),
    )(match, raw.reshape(cut), through.reshape(cut)).reshape(rows, width)


def matches(roster_row):
    blocks = roster_row.shape[0]
    wanted = jnp.arange(blocks, dtype=jnp.int32)
    equal = (roster_row[None, :] == wanted[:, None]).astype(jnp.int32)
    return jnp.broadcast_to(equal[:, :, None], (blocks, blocks, HD))


def on_device(feed_down, feed_up, cotangent_down, cotangent_up, roster, value_weight):
    members = lax.axis_size("dp")
    chips = members // 2
    me = lax.axis_index("dp")
    weight = value_weight[0]
    rows = feed_down.shape[1]
    sums_down, sums_up = group_sums(cotangent_down[0], cotangent_up[0])

    x_down = passed_along(feed_down[0], "section", 1)
    sums_up = passed_along(sums_up, "section", 1)
    sums_down = passed_along(sums_down, "section", -1)
    x_up = passed_along(feed_up[0], "section", -1)
    raw_up = passed_along(cotangent_up[0], "section", 1)
    raw_down = passed_along(cotangent_down[0], "section", -1)

    match_down = matches(roster[0, 0])
    match_up = matches(roster[0, 1])
    grouped = arranged_sums(sums_down, sums_up, match_down, match_up)

    def exchanged(slices):
        return lax.all_to_all(slices, "dp", split_axis=0, concat_axis=0, tiled=True)

    normed_down = exchanged(normalized_slices(x_down, members))
    normed_up = exchanged(normalized_slices(x_up, members))

    pieces = [grouped]
    for c in range(1, chips):
        pieces.append(
            lax.ppermute(grouped, "dp", [(i, (((i // 2) ^ c) * 2) + i % 2) for i in range(members)])
        )
    own = jnp.stack(pieces)
    other = lax.ppermute(own, "dp", [(i, i ^ 1) for i in range(members)])

    next_down, next_up, through_down, through_up = span(x_down, x_up, grouped, weight)

    factor = float(2 * rows * members) ** (-0.5)
    summed = weight_gradient(
        normed_down, normed_up, own, other, me.reshape(1).astype(jnp.int32), factor
    )

    back_down = finished(raw_down, match_down, through_down)
    back_up = finished(raw_up, match_up, through_up)
    return (
        next_down[None],
        next_up[None],
        back_down[None],
        back_up[None],
        summed[None],
    )


def solution(mesh):
    placed = (
        P("section", "dp", None),
        P("section", "dp", None),
        P("section", "dp", None),
        P("section", "dp", None),
        P("section", None, None),
        P("section", None, None),
    )
    return jax.shard_map(
        on_device,
        mesh=mesh,
        in_specs=placed,
        out_specs=(
            P("section", "dp", None),
            P("section", "dp", None),
            P("section", "dp", None),
            P("section", "dp", None),
            P("section", "dp", None),
        ),
        check_vma=False,
    )
```

time: 111 us -> 60 us (0.54)
  waiting for transfers between devices: 45.3 us -> 15.6 us
  Pallas kernels: 0 us -> 14.3 us
  matrix products: 14.2 us -> 0 us
  between operations: 14.2 us -> 0.71 us
  starting transfers between devices: 12.7 us -> 23.7 us
  local copies, waits for them, and re-layouts: 15 us -> 5.16 us
  other arithmetic: 9.07 us -> 0.08 us
    ppermute x4 -> x6, waiting for transfers between devices: 24.6 us -> 7.22 us  [passed_along(): lax.ppermute(shard, axis, [(i, (i + by) % count) for i in range(count)])]
    pallas_call x0 -> x8, Pallas kernels: none -> 14.3 us  [the longest x1 6.17 us: span(): pl.pallas_call(span_kernel, grid=(width // tile,), in_specs=[whole_vmem()...]
    dot_general x7 -> x0, matrix products: 14.2 us -> none  [the longest x2 5.3 us: one_leg(): lax.dot_general(grouped, weight, (((1,), (1,)), ((), ())), preferred_elem...]
    all_to_all x1 -> x2, waiting for transfers between devices: 13.5 us -> 0.01 us  [exchanged(): return lax.all_to_all(slices, 'dp', split_axis=0, concat_axis=0, tiled=True)]
    ppermute x0 -> x4, waiting for transfers between devices: none -> 8.33 us  [the longest x3 8.32 us: on_device(): lax.ppermute(grouped, 'dp', [(i, (i // 2 ^ c) * 2 + i % 2) for i in range...]
    all_gather x1 -> x0, waiting for transfers between devices: 7.19 us -> none  [on_device(): lax.all_gather(grouped_all, 'dp', axis=0, tiled=True)]
    another operation x1 -> x0, local copies, waits for them, and re-layouts: 6.38 us -> none
    broadcast_in_dim x4 -> x0, other arithmetic: 5.02 us -> none  [the longest x1 1.4 us: on_device(): advanced_down[None]]
  transfers between devices with their start and end apart: 6 -> 12, of which waited for: 6 -> 3; matrix products, arithmetic and copies ran while one was open for 18% -> 2% of each run, Pallas kernels for 0% -> 19%
where the time goes in v1:
time: 60 us; the launch traced here: 59.5 us
  starting transfers between devices  23.7 us (40%)
  waiting for transfers between devices  15.6 us (26%)
  Pallas kernels  14.3 us (24%)
  local copies, waits for them, and re-layouts  5.16 us (9%)
  between operations  0.71 us (1%)
    ppermute x6, starting transfers between devices, passed_along(): lax.ppermute(shard, axis, [(i, (i + by) % count) for i in range(count)])  12.5 us
    ppermute x3, waiting for transfers between devices, on_device(): lax.ppermute(grouped, 'dp', [(i, (i // 2 ^ c) * 2 + i % 2) for i in range...  8.32 us
    all_to_all x2, starting transfers between devices, exchanged(): return lax.all_to_all(slices, 'dp', split_axis=0, concat_axis=0, tiled=True)  7.51 us
    ppermute x6, waiting for transfers between devices, passed_along(): lax.ppermute(shard, axis, [(i, (i + by) % count) for i in range(count)])  7.22 us
    pallas_call x1, Pallas kernels, span(): pl.pallas_call(span_kernel, grid=(width // tile,), in_specs=[whole_vmem()...  6.17 us
    unnamed x6, local copies, waits for them, and re-layouts  4.27 us
    ppermute x3, starting transfers between devices, on_device(): lax.ppermute(grouped, 'dp', [(i, (i // 2 ^ c) * 2 + i % 2) for i in range...  3.62 us
    pallas_call x2, Pallas kernels, finished(): pl.pallas_call(finish_kernel, grid=(blocks,), in_specs=[whole_vmem()] * 3...  3.11 us
  transfers between devices with their start and end apart: 12, of which 3 were waited for; matrix products, arithmetic and copies ran while one was open for 2% of the time, Pallas kernels for 19%

profile of v1, /device:TPU:0, one launch (start us, length us, event | category | flops | bytes accessed | tf_op | source)
XLA Modules:
  0.0 59.5 jit_solution(4424121178459279519)
XLA Ops:
  0.6 3.1 %collective-permute-start = (bf16[64,4096]{1,0:T(8,128)(2,1)}, bf16[64,4096]{1,0:T(8,128)(2,1)S(1)}, u32[]{:S(2)}, u32[]{:S(2)}) collective-permute-start(bf16[64,4096]{1,0:T(8,128)(2,1)} %bitcast.42), channel_id=1, source_target_pairs={{0,8},{8,16},{16,24},{24,0},{1,9},{9,17},{17,25},{25,1},{2,10},{10... | collective-permute-start | bytes 1572872 | tf_op jit(solution)/shard_map/ppermute | solution.py:24
  3.7 1.0 %copy-done.1 = bf16[1,64,4096]{2,1,0:T(8,128)(2,1)S(1)} copy-done((bf16[1,64,4096]{2,1,0:T(8,128)(2,1)S(1)}, bf16[1,64,4096]{2,1,0:T(8,128)(2,1)}, u32[]{:S(2)}) %copy-start.1) | copy-done | bytes 524312
  4.8 1.0 %copy-done.2 = bf16[1,64,4096]{2,1,0:T(8,128)(2,1)S(1)} copy-done((bf16[1,64,4096]{2,1,0:T(8,128)(2,1)S(1)}, bf16[1,64,4096]{2,1,0:T(8,128)(2,1)}, u32[]{:S(2)}) %copy-start.2) | copy-done | bytes 524312
  5.8 0.2 group_sums.1
  6.0 2.1 %collective-permute-start.2 = (bf16[64,512]{1,0:T(8,128)(2,1)S(1)}, bf16[64,512]{1,0:T(8,128)(2,1)S(1)}, u32[]{:S(2)}, u32[]{:S(2)}) collective-permute-start(bf16[64,512]{1,0:T(8,128)(2,1)S(1)} %get-tuple-element.11), channel_id=1, source_target_pairs={{0,24},{8,0},{16,8},{24,16},{1,25},{9,1},{17,9},{25,17},{2,26},{10... | collective-permute-start | bytes 196616 | tf_op jit(solution)/shard_map/ppermute | solution.py:24
  8.1 0.0 collective-permute-start.3
  8.1 3.8 %collective-permute-start.1 = (bf16[64,4096]{1,0:T(8,128)(2,1)}, bf16[64,4096]{1,0:T(8,128)(2,1)S(1)}, u32[]{:S(2)}, u32[]{:S(2)}) collective-permute-start(bf16[64,4096]{1,0:T(8,128)(2,1)} %bitcast.43), channel_id=1, source_target_pairs={{0,24},{8,0},{16,8},{24,16},{1,25},{9,1},{17,9},{25,17},{2,26},{10... | collective-permute-start | bytes 1572872 | tf_op jit(solution)/shard_map/ppermute | solution.py:24
  11.9 0.8 %slice_bitcast_fusion = (s32[2]{0:T(128)S(1)}, s32[2]{0:T(128)S(1)}) fusion(s32[1,2,2]{2,1,0:T(2,128)} %param.10), kind=kLoop, calls=%fused_computation.3 | loop fusion | bytes 32 | tf_op jit(solution)/shard_map/eq | solution.py:268
  12.7 6.1 %collective-permute-done.down_ref.x_ref = bf16[64,4096]{1,0:T(8,128)(2,1)S(1)} collective-permute-done((bf16[64,4096]{1,0:T(8,128)(2,1)}, bf16[64,4096]{1,0:T(8,128)(2,1)S(1)}, u32[]{:S(2)}, u32[]{:S(2)}) %collective-permute-start) | collective-permute-done | bytes 524320 | tf_op jit(solution)/shard_map/ppermute | solution.py:24
  18.8 1.0 %normalized_slices.2 = bf16[8,64,512]{2,1,0:T(8,128)(2,1)} custom-call(bf16[64,4096]{1,0:T(8,128)(2,1)S(1)} %collective-permute-done.down_ref.x_ref), custom_call_target="tpu_custom_call" | custom-call | flops 1048576 | bytes 1048576 | tf_op jit(solution)/shard_map/normalized_slices/pallas_call | solution.py:72
  19.8 3.9 %all-to-all-start = ((bf16[8,64,512]{2,1,0:T(8,128)(2,1)}), bf16[8,64,512]{2,1,0:T(8,128)(2,1)S(1)}, u32[]{:S(2)}, u32[]{:S(2)}) async-start(bf16[8,64,512]{2,1,0:T(8,128)(2,1)} %normalized_slices.2), calls=%async_computation | async-start | bytes 1048576 | tf_op jit(solution)/shard_map/all_to_all | solution.py:292
  23.8 0.0 collective-permute-done.2
  23.8 0.0 collective-permute-done.3
  23.8 0.1 broadcast_in_dim.10.match_down.match_ref
  23.8 0.1 broadcast_in_dim.11.match_up.match_ref
  23.9 0.1 arranged_sums.1.grouped_ref
  24.0 2.1 %collective-permute-start.6 = (bf16[128,512]{1,0:T(8,128)(2,1)S(1)}, bf16[128,512]{1,0:T(8,128)(2,1)S(1)}, u32[]{:S(2)}, u32[]{:S(2)}) collective-permute-start(bf16[128,512]{1,0:T(8,128)(2,1)S(1)} %arranged_sums.1.grouped_ref), channel_id=1, source_target_pairs={{0,2},{1,3},{2,0},{3,1},{4,6},{5,7},{6,4},{7,5},{8,10},{9,11},{10,... | collective-permute-start | bytes 393224 | tf_op jit(solution)/shard_map/ppermute | solution.py:300
  26.1 1.5 %collective-permute-start.7 = (bf16[128,512]{1,0:T(8,128)(2,1)S(1)}, bf16[128,512]{1,0:T(8,128)(2,1)S(1)}, u32[]{:S(2)}, u32[]{:S(2)}) collective-permute-start(bf16[128,512]{1,0:T(8,128)(2,1)S(1)} %arranged_sums.1.grouped_ref), channel_id=1, source_target_pairs={{0,4},{1,5},{2,6},{3,7},{4,0},{5,1},{6,2},{7,3},{8,12},{9,13},{10,... | collective-permute-start | bytes 393224 | tf_op jit(solution)/shard_map/ppermute | solution.py:300
  27.5 0.1 collective-permute-start.8
  27.6 0.0 collective-permute-start.5
  27.6 8.3 %collective-permute-done.6 = bf16[128,512]{1,0:T(8,128)(2,1)S(1)} collective-permute-done((bf16[128,512]{1,0:T(8,128)(2,1)S(1)}, bf16[128,512]{1,0:T(8,128)(2,1)S(1)}, u32[]{:S(2)}, u32[]{:S(2)}) %collective-permute-start.6) | collective-permute-done | bytes 131104 | tf_op jit(solution)/shard_map/ppermute | solution.py:300
  35.9 3.5 %collective-permute-start.4 = (bf16[64,4096]{1,0:T(8,128)(2,1)}, bf16[64,4096]{1,0:T(8,128)(2,1)}, u32[]{:S(2)}, u32[]{:S(2)}) collective-permute-start(bf16[64,4096]{1,0:T(8,128)(2,1)} %bitcast.32), channel_id=1, source_target_pairs={{0,24},{8,0},{16,8},{24,16},{1,25},{9,1},{17,9},{25,17},{2,26},{10... | collective-permute-start | bytes 1572872 | tf_op jit(solution)/shard_map/ppermute | solution.py:24
  39.4 0.1 pad_maximum_fusion.own_ref
  39.5 0.1 collective-permute-start.9
  39.6 1.0 %normalized_slices.3 = bf16[8,64,512]{2,1,0:T(8,128)(2,1)} custom-call(bf16[64,4096]{1,0:T(8,128)(2,1)S(1)} %collective-permute-done.1.up_ref.x_ref), custom_call_target="tpu_custom_call" | custom-call | flops 1048576 | bytes 1048576 | tf_op jit(solution)/shard_map/normalized_slices/pallas_call | solution.py:72
  40.6 3.6 %all-to-all-start.1 = ((bf16[8,64,512]{2,1,0:T(8,128)(2,1)}), bf16[8,64,512]{2,1,0:T(8,128)(2,1)S(1)}, u32[]{:S(2)}, u32[]{:S(2)}) async-start(bf16[8,64,512]{2,1,0:T(8,128)(2,1)} %normalized_slices.3), calls=%async_computation.1 | async-start | bytes 1048576 | tf_op jit(solution)/shard_map/all_to_all | solution.py:292
  44.2 2.2 %copy-done = bf16[1,4096,512]{2,1,0:T(8,128)(2,1)S(1)} copy-done((bf16[1,4096,512]{2,1,0:T(8,128)(2,1)S(1)}, bf16[1,4096,512]{2,1,0:T(8,128)(2,1)}, u32[]{:S(2)}) %copy-start) | copy-done | bytes 4194328
  46.4 6.2 %span.1 = (bf16[64,4096]{1,0:T(8,128)(2,1)}, bf16[64,4096]{1,0:T(8,128)(2,1)}, f32[64,4096]{1,0:T(8,128)S(1)}, f32[64,4096]{1,0:T(8,128)S(1)}) custom-call(bf16[64,4096]{1,0:T(8,128)(2,1)S(1)} %collective-permute-done.down_ref.x_ref, bf16[64,4096]{1,0:T(8,128)(2,1)S(1)} %collective-permute-done.1.up_ref.x_ref, ...), custom_call_target="tpu_custom_call" | custom-call | flops 1073741824 | bytes 8388608 | tf_op jit(solution)/shard_map/span/pallas_call | solution.py:138
  52.5 1.0 %finished.3 = bf16[2,32,4096]{2,1,0:T(8,128)(2,1)} custom-call(s32[2,2,128]{2,1,0:T(2,128)S(1)} %broadcast_in_dim.11.match_up.match_ref, bf16[2,32,4096]{2,1,0:T(8,128)(2,1)S(1)} %bitcast.29, f32[2,32,4096]{2,1,0:T(8,128)S(1)} %bitcast.28), custom_call_target="tpu_custom_call" | custom-call | flops 524288 | bytes 2097152 | tf_op jit(solution)/shard_map/finished/pallas_call | solution.py:251
  53.6 1.1 %collective-permute-done.4 = bf16[64,4096]{1,0:T(8,128)(2,1)} collective-permute-done((bf16[64,4096]{1,0:T(8,128)(2,1)}, bf16[64,4096]{1,0:T(8,128)(2,1)}, u32[]{:S(2)}, u32[]{:S(2)}) %collective-permute-start.4) | collective-permute-done | bytes 524320 | tf_op jit(solution)/shard_map/ppermute | solution.py:24
  54.7 2.1 %finished.2 = bf16[2,32,4096]{2,1,0:T(8,128)(2,1)} custom-call(s32[2,2,128]{2,1,0:T(2,128)S(1)} %broadcast_in_dim.10.match_down.match_ref, bf16[2,32,4096]{2,1,0:T(8,128)(2,1)} %bitcast.11.raw_ref, f32[2,32,4096]{2,1,0:T(8,128)S(1)} %bitcast.27), custom_call_target="tpu_custom_call" | custom-call | flops 524288 | bytes 2097152 | tf_op jit(solution)/shard_map/finished/pallas_call | solution.py:251
  56.8 2.8 %weight_gradient.1 = f32[512,512]{1,0:T(8,128)} custom-call(s32[1]{0:T(128)} %bitcast.17.me_ref, bf16[8,64,512]{2,1,0:T(8,128)(2,1)S(1)} %all-to-all-done.down_ref, bf16[8,64,512]{2,1,0:T(8,128)(2,1)S(1)} %all-to-all-done.1.up_ref, bf16[4,128,512]{2,1,0:T(8,128)(2,1)S(1)} %pad_maximum_fusion.own_ref, bf16[4,128,512]{2,1,0:T(8,128)(2,1)} %collective-permute-done.9.other_ref), custom_call_target="tpu_custom_call" | custom-call | flops 536870912 | bytes 3145728 | tf_op jit(solution)/shard_map/weight_gradient/pallas_call | solution.py:189
  (12 shorter events, 0.0 us)
Async XLA Ops:
  0.6 18.2 %collective-permute-start = (bf16[64,4096]{1,0:T(8,128)(2,1)}, bf16[64,4096]{1,0:T(8,128)(2,1)S(1)}, u32[]{:S(2)}, u32[]{:S(2)}) collective-permute-start(bf16[64,4096]{1,0:T(8,128)(2,1)} %bitcast.42), channel_id=1, source_target_pairs={{0,8},{8,16},{16,24},{24,0},{1,9},{9,17},{17,25},{25,1},{2,10},{10... | collective-permute-start | bytes 1572872 | tf_op jit(solution)/shard_map/ppermute | solution.py:24
  3.7 1.0 %copy-start.1 = (bf16[1,64,4096]{2,1,0:T(8,128)(2,1)S(1)}, bf16[1,64,4096]{2,1,0:T(8,128)(2,1)}, u32[]{:S(2)}) copy-start(bf16[1,64,4096]{2,1,0:T(8,128)(2,1)} %param.9) | copy-start | bytes 1572868
  4.8 1.0 %copy-start.2 = (bf16[1,64,4096]{2,1,0:T(8,128)(2,1)S(1)}, bf16[1,64,4096]{2,1,0:T(8,128)(2,1)}, u32[]{:S(2)}) copy-start(bf16[1,64,4096]{2,1,0:T(8,128)(2,1)} %param.8) | copy-start | bytes 1572868
  6.0 17.8 %collective-permute-start.2 = (bf16[64,512]{1,0:T(8,128)(2,1)S(1)}, bf16[64,512]{1,0:T(8,128)(2,1)S(1)}, u32[]{:S(2)}, u32[]{:S(2)}) collective-permute-start(bf16[64,512]{1,0:T(8,128)(2,1)S(1)} %get-tuple-element.11), channel_id=1, source_target_pairs={{0,24},{8,0},{16,8},{24,16},{1,25},{9,1},{17,9},{25,17},{2,26},{10... | collective-permute-start | bytes 196616 | tf_op jit(solution)/shard_map/ppermute | solution.py:24
  8.1 15.7 %collective-permute-start.3 = (bf16[64,512]{1,0:T(8,128)(2,1)S(1)}, bf16[64,512]{1,0:T(8,128)(2,1)S(1)}, u32[]{:S(2)}, u32[]{:S(2)}) collective-permute-start(bf16[64,512]{1,0:T(8,128)(2,1)S(1)} %get-tuple-element.12), channel_id=1, source_target_pairs={{0,8},{8,16},{16,24},{24,0},{1,9},{9,17},{17,25},{25,1},{2,10},{10... | collective-permute-start | bytes 196616 | tf_op jit(solution)/shard_map/ppermute | solution.py:24
  8.1 31.5 %collective-permute-start.1 = (bf16[64,4096]{1,0:T(8,128)(2,1)}, bf16[64,4096]{1,0:T(8,128)(2,1)S(1)}, u32[]{:S(2)}, u32[]{:S(2)}) collective-permute-start(bf16[64,4096]{1,0:T(8,128)(2,1)} %bitcast.43), channel_id=1, source_target_pairs={{0,24},{8,0},{16,8},{24,16},{1,25},{9,1},{17,9},{25,17},{2,26},{10... | collective-permute-start | bytes 1572872 | tf_op jit(solution)/shard_map/ppermute | solution.py:24
  19.8 20.8 %all-to-all-start = ((bf16[8,64,512]{2,1,0:T(8,128)(2,1)}), bf16[8,64,512]{2,1,0:T(8,128)(2,1)S(1)}, u32[]{:S(2)}, u32[]{:S(2)}) async-start(bf16[8,64,512]{2,1,0:T(8,128)(2,1)} %normalized_slices.2), calls=%async_computation | async-start | bytes 1048576 | tf_op jit(solution)/shard_map/all_to_all | solution.py:292
  24.0 11.9 %collective-permute-start.6 = (bf16[128,512]{1,0:T(8,128)(2,1)S(1)}, bf16[128,512]{1,0:T(8,128)(2,1)S(1)}, u32[]{:S(2)}, u32[]{:S(2)}) collective-permute-start(bf16[128,512]{1,0:T(8,128)(2,1)S(1)} %arranged_sums.1.grouped_ref), channel_id=1, source_target_pairs={{0,2},{1,3},{2,0},{3,1},{4,6},{5,7},{6,4},{7,5},{8,10},{9,11},{10,... | collective-permute-start | bytes 393224 | tf_op jit(solution)/shard_map/ppermute | solution.py:300
  26.1 13.4 %collective-permute-start.7 = (bf16[128,512]{1,0:T(8,128)(2,1)S(1)}, bf16[128,512]{1,0:T(8,128)(2,1)S(1)}, u32[]{:S(2)}, u32[]{:S(2)}) collective-permute-start(bf16[128,512]{1,0:T(8,128)(2,1)S(1)} %arranged_sums.1.grouped_ref), channel_id=1, source_target_pairs={{0,4},{1,5},{2,6},{3,7},{4,0},{5,1},{6,2},{7,3},{8,12},{9,13},{10,... | collective-permute-start | bytes 393224 | tf_op jit(solution)/shard_map/ppermute | solution.py:300
  27.5 11.9 %collective-permute-start.8 = (bf16[128,512]{1,0:T(8,128)(2,1)S(1)}, bf16[128,512]{1,0:T(8,128)(2,1)S(1)}, u32[]{:S(2)}, u32[]{:S(2)}) collective-permute-start(bf16[128,512]{1,0:T(8,128)(2,1)S(1)} %arranged_sums.1.grouped_ref), channel_id=1, source_target_pairs={{0,6},{1,7},{2,4},{3,5},{4,2},{5,3},{6,0},{7,1},{8,14},{9,15},{10,... | collective-permute-start | bytes 393224 | tf_op jit(solution)/shard_map/ppermute | solution.py:300
  27.6 24.9 %collective-permute-start.5 = (bf16[64,4096]{1,0:T(8,128)(2,1)}, bf16[64,4096]{1,0:T(8,128)(2,1)S(1)}, u32[]{:S(2)}, u32[]{:S(2)}) collective-permute-start(bf16[64,4096]{1,0:T(8,128)(2,1)} %bitcast.30), channel_id=1, source_target_pairs={{0,8},{8,16},{16,24},{24,0},{1,9},{9,17},{17,25},{25,1},{2,10},{10... | collective-permute-start | bytes 1572872 | tf_op jit(solution)/shard_map/ppermute | solution.py:24
  35.9 18.7 %collective-permute-start.4 = (bf16[64,4096]{1,0:T(8,128)(2,1)}, bf16[64,4096]{1,0:T(8,128)(2,1)}, u32[]{:S(2)}, u32[]{:S(2)}) collective-permute-start(bf16[64,4096]{1,0:T(8,128)(2,1)} %bitcast.32), channel_id=1, source_target_pairs={{0,24},{8,0},{16,8},{24,16},{1,25},{9,1},{17,9},{25,17},{2,26},{10... | collective-permute-start | bytes 1572872 | tf_op jit(solution)/shard_map/ppermute | solution.py:24
  39.5 17.2 %collective-permute-start.9 = (bf16[4,128,512]{2,1,0:T(8,128)(2,1)S(1)}, bf16[4,128,512]{2,1,0:T(8,128)(2,1)}, u32[]{:S(2)}, u32[]{:S(2)}) collective-permute-start(bf16[4,128,512]{2,1,0:T(8,128)(2,1)S(1)} %pad_maximum_fusion.own_ref), channel_id=1, source_target_pairs={{0,1},{1,0},{2,3},{3,2},{4,5},{5,4},{6,7},{7,6},{8,9},{9,8},{10,11... | collective-permute-start | bytes 1572872 | tf_op jit(solution)/shard_map/ppermute | solution.py:303
  40.6 16.1 %all-to-all-start.1 = ((bf16[8,64,512]{2,1,0:T(8,128)(2,1)}), bf16[8,64,512]{2,1,0:T(8,128)(2,1)S(1)}, u32[]{:S(2)}, u32[]{:S(2)}) async-start(bf16[8,64,512]{2,1,0:T(8,128)(2,1)} %normalized_slices.3), calls=%async_computation.1 | async-start | bytes 1048576 | tf_op jit(solution)/shard_map/all_to_all | solution.py:292
  44.2 2.2 %copy-start = (bf16[1,4096,512]{2,1,0:T(8,128)(2,1)S(1)}, bf16[1,4096,512]{2,1,0:T(8,128)(2,1)}, u32[]{:S(2)}) copy-start(bf16[1,4096,512]{2,1,0:T(8,128)(2,1)} %param.11) | copy-start | bytes 12582916

commit v2 on v0

v2 whole, which is shorter than its diff:
```python
import functools
import math

import jax
import jax.numpy as jnp
from jax import lax
from jax.experimental import pallas as pl
from jax.experimental.pallas import tpu as pltpu
from jax.sharding import PartitionSpec as P


KVH = 4
HD = 128
GROUPS = 8


EPSILON = 1e-05


MIB = 2**20


def passed_along(shard, axis, by):
    count = lax.axis_size(axis)
    return lax.ppermute(shard, axis, [(i, (i + by) % count) for i in range(count)])


def whole_vmem():
    return pl.BlockSpec(memory_space=pltpu.VMEM)


def called(kernel, operands, outputs, scratch=(), flops=0, vmem=4, **more):
    moved = sum(x.size * x.dtype.itemsize for x in list(operands) + list(outputs))
    return pl.pallas_call(
        kernel,
        in_specs=more.get("in_specs", [whole_vmem()] * len(operands)),
        out_specs=[whole_vmem()] * len(outputs),
        out_shape=list(outputs),
        scratch_shapes=list(scratch),
        compiler_params=pltpu.CompilerParams(vmem_limit_bytes=vmem * MIB),
        cost_estimate=pl.CostEstimate(
            flops=flops, bytes_accessed=moved, transcendentals=0
        ),
    )(*operands)


def group_kernel(down_ref, up_ref, down_out, up_out, first_out, rest_out):
    step = pl.program_id(0)
    for src, dst in ((down_ref, down_out), (up_ref, up_out)):
        for k in range(KVH):
            total = src[:, k * GROUPS * HD : (k * GROUPS + 1) * HD].astype(jnp.float32)
            for j in range(1, GROUPS):
                at = (k * GROUPS + j) * HD
                total = total + src[:, at : at + HD].astype(jnp.float32)
            dst[:, k * HD : (k + 1) * HD] = total.astype(dst.dtype)

    @pl.when(step == 0)
    def _():
        first_out[...] = down_ref[...]

    @pl.when(step > 0)
    def _():
        rest_out[...] = down_ref[...]


def group_sums(down, up):
    rows, width = down.shape
    steps = 4
    step = rows // steps
    wide = pl.BlockSpec((step, width), lambda i: (i, 0))
    narrow = pl.BlockSpec((step, width // GROUPS), lambda i: (i, 0))
    out = jax.ShapeDtypeStruct((rows, width // GROUPS), down.dtype)
    return pl.pallas_call(
        group_kernel,
        grid=(steps,),
        in_specs=[wide, wide],
        out_specs=[
            narrow,
            narrow,
            pl.BlockSpec((step, width), lambda i: (0, 0)),
            pl.BlockSpec((step, width), lambda i: (jnp.maximum(i - 1, 0), 0)),
        ],
        out_shape=[
            out,
            out,
            jax.ShapeDtypeStruct((step, width), down.dtype),
            jax.ShapeDtypeStruct((rows - step, width), down.dtype),
        ],
        name="group_sums",
        compiler_params=pltpu.CompilerParams(vmem_limit_bytes=6 * MIB),
        cost_estimate=pl.CostEstimate(
            flops=2 * rows * width, bytes_accessed=6 * rows * width, transcendentals=0
        ),
    )(down, up)


def inverse_of(x):
    return lax.rsqrt(jnp.mean(x * x, axis=-1, keepdims=True) + EPSILON)


def unit_of(width, members, inner):
    return math.gcd(width // members, inner)


def write_normed(chips, x_ref, piece_refs):
    inverse = inverse_of(x_ref[...].astype(jnp.float32))
    unit = piece_refs[0].shape[-1]
    per_chip = x_ref.shape[1] // chips
    chip = lax.axis_index("dp") // 2
    for c, piece in enumerate(piece_refs):
        base = (chip ^ c) * per_chip
        for b in range(per_chip // unit):
            at = pl.ds(pl.multiple_of(base + b * unit, unit), unit)
            piece[b] = (x_ref[:, at].astype(jnp.float32) * inverse).astype(piece.dtype)


def down_kernel(chips, x_ref, match_down, match_up, down_ref, up_ref, grouped_ref, *pieces):
    write_normed(chips, x_ref, pieces)
    blocks, rows, inner = down_ref.shape
    unit = pieces[0].shape[-1]
    own = x_ref.shape[1] // chips // unit
    for leg, (match, ref) in enumerate(((match_down, down_ref), (match_up, up_ref))):
        for m in range(blocks):
            chosen = ref[0].astype(jnp.float32)
            for j in range(1, blocks):
                mine = match[m, j : j + 1, 0:1] != 0
                chosen = jnp.where(mine, ref[j].astype(jnp.float32), chosen)
            chosen = chosen.astype(grouped_ref.dtype)
            at = (leg * blocks + m) * rows
            grouped_ref[at : at + rows, :] = chosen
            for piece in pieces:
                for b in range(inner // unit):
                    piece[own + leg * (inner // unit) + b, m * rows : (m + 1) * rows, :] = chosen[
                        :, b * unit : (b + 1) * unit
                    ]


def up_kernel(chips, x_ref, *pieces):
    write_normed(chips, x_ref, pieces)


def pieces_down(x, sums_down, sums_up, match_down, match_up, members):
    rows, width = x.shape
    inner = sums_down.shape[1]
    chips = members // 2
    unit = unit_of(width, members, inner)
    count = width // chips // unit + 2 * inner // unit
    blocks = match_down.shape[0]
    cut = (blocks, rows // blocks, inner)
    outputs = [jax.ShapeDtypeStruct((2 * rows, inner), x.dtype)]
    outputs += [jax.ShapeDtypeStruct((count, rows, unit), x.dtype)] * chips
    return called(
        functools.partial(down_kernel, chips),
        (x, match_down, match_up, sums_down.reshape(cut), sums_up.reshape(cut)),
        outputs,
        flops=4 * rows * width,
    )


def pieces_up(x, inner, members):
    rows, width = x.shape
    chips = members // 2
    unit = unit_of(width, members, inner)
    outputs = [jax.ShapeDtypeStruct((width // chips // unit, rows, unit), x.dtype)] * chips
    return called(functools.partial(up_kernel, chips), (x,), outputs, flops=4 * rows * width)


def product_kernel(chips, inner, *refs):
    down, up = refs[:chips], refs[chips : 2 * chips]
    keep_ref, send_ref = refs[2 * chips :]
    unit = down[0].shape[-1]
    half = keep_ref.shape[0] // unit
    own = 2 * half
    core = lax.axis_index("dp") % 2
    over_tokens = (((0,), (0,)), ((), ()))

    def stacked(at, grouped):
        legs = [ref[at[0]] for ref in down]
        legs += [ref[at[1]] for ref in (down if grouped else up)]
        return jnp.concatenate(legs, axis=0)

    for g in range(inner // unit):
        grouped = stacked((own + g, own + inner // unit + g), True)
        for dest, out_ref in ((core, keep_ref), (1 - core, send_ref)):
            for b in range(half):
                at = dest * half + b
                out_ref[b * unit : (b + 1) * unit, g * unit : (g + 1) * unit] = lax.dot_general(
                    stacked((at, at), False),
                    grouped,
                    over_tokens,
                    preferred_element_type=jnp.float32,
                )


def products(down, up, width, inner, members):
    chips = members // 2
    rows = up[0].shape[1]
    out = jax.ShapeDtypeStruct((width // members, inner), jnp.float32)
    return called(
        functools.partial(product_kernel, chips, inner),
        (*down, *up),
        [out, out],
        flops=8 * chips * rows * (width // members) * inner,
        vmem=8,
    )


def combine_kernel(factor, keep_ref, got_ref, out_ref):
    out_ref[...] = (keep_ref[...] + got_ref[...]) * factor


def combined(keep, got, factor):
    rows, inner = keep.shape
    step = rows // 2
    part = pl.BlockSpec((step, inner), lambda i: (i, 0))
    return pl.pallas_call(
        functools.partial(combine_kernel, factor),
        grid=(rows // step,),
        in_specs=[part, part],
        out_specs=part,
        out_shape=jax.ShapeDtypeStruct(keep.shape, keep.dtype),
        name="combine",
        compiler_params=pltpu.CompilerParams(vmem_limit_bytes=4 * MIB),
        cost_estimate=pl.CostEstimate(
            flops=2 * rows * inner, bytes_accessed=12 * rows * inner, transcendentals=0
        ),
    )(keep, got)


def span_kernel(
    down_ref, up_ref, grouped_ref, weight_ref,
    next_down, next_up, through,
    scaled, back, held, arrived,
):
    rows, width = down_ref.shape
    tiles, tile, inner = held.shape
    copies = [
        pltpu.make_async_copy(weight_ref.at[pl.ds(t * tile, tile), :], held.at[t], arrived.at[t])
        for t in range(tiles)
    ]
    for copy in copies:
        copy.start()
    inverses = []
    for leg, ref in enumerate((down_ref, up_ref)):
        x = ref[...].astype(jnp.float32)
        inverse = inverse_of(x)
        inverses.append(inverse)
        scaled[leg * rows : (leg + 1) * rows, :] = x * inverse
    values = jnp.zeros((2 * rows, inner), jnp.float32)
    total = jnp.zeros((2 * rows, HD), jnp.float32)
    grouped = grouped_ref[...]
    for t, copy in enumerate(copies):
        copy.wait()
        weight = held[t]
        at = slice(t * tile, (t + 1) * tile)
        normed = scaled[:, at].astype(down_ref.dtype)
        values = values + jnp.dot(normed, weight, preferred_element_type=jnp.float32)
        part = lax.dot_general(
            grouped, weight, (((1,), (1,)), ((), ())), preferred_element_type=jnp.float32
        )
        back[:, at] = part
        for c in range(tile // HD):
            lanes = slice(c * HD, (c + 1) * HD)
            total = total + part[:, lanes] * scaled[:, t * tile + c * HD : t * tile + (c + 1) * HD]
    means = jnp.sum(total, axis=-1, keepdims=True) * (1.0 / width)
    for leg, (ref, nxt) in enumerate(((down_ref, next_down), (up_ref, next_up))):
        own = slice(leg * rows, (leg + 1) * rows)
        mean = jnp.broadcast_to(means[own], (rows, HD))
        inverse = jnp.broadcast_to(inverses[leg], (rows, HD))
        for k in range(KVH):
            spread = values[own, k * HD : (k + 1) * HD]
            for j in range(GROUPS):
                at = slice((k * GROUPS + j) * HD, (k * GROUPS + j + 1) * HD)
                nxt[:, at] = (ref[:, at].astype(jnp.float32) + spread).astype(nxt.dtype)
                through[leg, :, at] = inverse * (back[own, at] - scaled[own, at] * mean)


def span(down, up, grouped, weight):
    rows, width = down.shape
    inner = weight.shape[1]
    tile = math.gcd(width, 512)
    return called(
        span_kernel,
        (down, up, grouped, weight),
        [jax.ShapeDtypeStruct((rows, width), down.dtype)] * 2
        + [jax.ShapeDtypeStruct((2, rows, width), jnp.float32)],
        scratch=[
            pltpu.VMEM((2 * rows, width), jnp.float32),
            pltpu.VMEM((2 * rows, width), jnp.float32),
            pltpu.VMEM((width // tile, tile, inner), weight.dtype),
            pltpu.SemaphoreType.DMA((width // tile,)),
        ],
        flops=8 * rows * width * inner,
        vmem=12,
        in_specs=[whole_vmem()] * 3 + [pl.BlockSpec(memory_space=pltpu.HBM)],
    )


def finish_kernel(leg, cuts, match_ref, through_ref, *refs):
    pieces, out_ref = refs[:-1], refs[-1]
    blocks, rows, _ = out_ref.shape
    unit = functools.reduce(math.gcd, cuts, rows)

    def units(start):
        at = 0
        for ref, cut in zip(pieces, cuts):
            if start < at + cut:
                return ref[start - at : start - at + unit, :]
            at += cut

    for m in range(blocks):
        for start in range(0, rows, unit):
            chosen = units(start).astype(jnp.float32)
            for j in range(1, blocks):
                mine = match_ref[m, j : j + 1, 0:1] != 0
                chosen = jnp.where(mine, units(j * rows + start).astype(jnp.float32), chosen)
            at = m * rows + start
            total = chosen + through_ref[leg, at : at + unit, :]
            out_ref[m, start : start + unit, :] = total.astype(out_ref.dtype)


def finished(pieces, match, through, leg):
    width = pieces[0].shape[1]
    cuts = [piece.shape[0] for piece in pieces]
    rows = sum(cuts)
    blocks = match.shape[0]
    cut = (blocks, rows // blocks, width)
    (out,) = called(
        functools.partial(finish_kernel, leg, cuts),
        (match, through, *pieces),
        [jax.ShapeDtypeStruct(cut, pieces[0].dtype)],
        flops=2 * rows * width,
    )
    return out.reshape(rows, width)


def matches(roster_row):
    blocks = roster_row.shape[0]
    wanted = jnp.arange(blocks, dtype=jnp.int32)
    equal = (roster_row[None, :] == wanted[:, None]).astype(jnp.int32)
    return jnp.broadcast_to(equal[:, :, None], (blocks, blocks, HD))


def on_device(feed_down, feed_up, cotangent_down, cotangent_up, roster, value_weight):
    members = lax.axis_size("dp")
    chips = members // 2
    weight = value_weight[0]
    rows, width = feed_down.shape[1:]
    inner = weight.shape[1]
    match_down = matches(roster[0, 0])
    match_up = matches(roster[0, 1])

    sums_down, sums_up, first_down, rest_down = group_sums(cotangent_down[0], cotangent_up[0])
    x_down = passed_along(feed_down[0], "section", 1)
    sums_up = passed_along(sums_up, "section", 1)
    sums_down = passed_along(sums_down, "section", -1)
    x_up = passed_along(feed_up[0], "section", -1)
    raw_down = [passed_along(first_down, "section", -1), passed_along(rest_down, "section", -1)]
    raw_up = [passed_along(cotangent_up[0], "section", 1)]

    def exchanged(pieces):
        got = [pieces[0]]
        for c in range(1, chips):
            to = [(i, ((i // 2) ^ c) * 2 + i % 2) for i in range(members)]
            got.append(lax.ppermute(pieces[c], "dp", to))
        return got

    grouped, *sent_down = pieces_down(x_down, sums_down, sums_up, match_down, match_up, members)
    got_down = exchanged(sent_down)
    got_up = exchanged(pieces_up(x_up, inner, members))

    next_down, next_up, through = span(x_down, x_up, grouped, weight)

    keep, send = products(got_down, got_up, width, inner, members)
    got = lax.ppermute(send, "dp", [(i, i ^ 1) for i in range(members)])
    summed = combined(keep, got, float(2 * rows * members) ** (-0.5))

    back_down = finished(raw_down, match_down, through, 0)
    back_up = finished(raw_up, match_up, through, 1)
    return (
        next_down[None],
        next_up[None],
        back_down[None],
        back_up[None],
        summed[None],
    )


def solution(mesh):
    rows = P("section", "dp", None)
    kept = P("section", None, None)
    return jax.shard_map(
        on_device,
        mesh=mesh,
        in_specs=(rows, rows, rows, rows, kept, kept),
        out_specs=(rows, rows, rows, rows, rows),
        check_vma=False,
    )
```

time: 111 us -> 85.8 us (0.77)
  matrix products: 14.2 us -> 0 us
  between operations: 14.2 us -> 0.72 us
  local copies, waits for them, and re-layouts: 15 us -> 3.34 us
  starting transfers between devices: 12.7 us -> 23.1 us
  Pallas kernels: 0 us -> 9.64 us
  other arithmetic: 9.07 us -> 0.01 us
  waiting for transfers between devices: 45.3 us -> 48.9 us
    dot_general x7 -> x0, matrix products: 14.2 us -> none  [the longest x2 5.3 us: one_leg(): lax.dot_general(grouped, weight, (((1,), (1,)), ((), ())), preferred_elem...]
    all_to_all x1 -> x0, waiting for transfers between devices: 13.5 us -> none  [on_device(): lax.all_to_all(normed_all, 'dp', split_axis=1, concat_axis=0, tiled=True)]
    ppermute x4 -> x7, waiting for transfers between devices: 24.6 us -> 37.5 us  [passed_along(): lax.ppermute(shard, axis, [(i, (i + by) % count) for i in range(count)])]
    ppermute x0 -> x7, waiting for transfers between devices: none -> 11.3 us  [the longest x6 11.3 us: exchanged(): got.append(lax.ppermute(pieces[c], 'dp', to))]
    pallas_call x0 -> x8, Pallas kernels: none -> 9.64 us  [the longest x6 8.37 us: called(): pl.pallas_call(kernel, in_specs=more.get('in_specs', [whole_vmem()] * len...]
    ppermute x0 -> x7, starting transfers between devices: none -> 8.5 us  [the longest x6 8.43 us: exchanged(): got.append(lax.ppermute(pieces[c], 'dp', to))]
    all_gather x1 -> x0, waiting for transfers between devices: 7.19 us -> none  [on_device(): lax.all_gather(grouped_all, 'dp', axis=0, tiled=True)]
    another operation x1 -> x0, local copies, waits for them, and re-layouts: 6.38 us -> none
  transfers between devices with their start and end apart: 6 -> 14, of which waited for: 6 -> 4; matrix products, arithmetic and copies ran while one was open for 18% -> 1% of each run, Pallas kernels for 0% -> 9%
where the time goes in v2:
time: 85.8 us; the launch traced here: 85.7 us
  waiting for transfers between devices  48.9 us (57%)
  starting transfers between devices  23.1 us (27%)
  Pallas kernels  9.64 us (11%)
  local copies, waits for them, and re-layouts  3.34 us (4%)
    ppermute x7, waiting for transfers between devices, passed_along(): lax.ppermute(shard, axis, [(i, (i + by) % count) for i in range(count)])  37.5 us
    ppermute x7, starting transfers between devices, passed_along(): lax.ppermute(shard, axis, [(i, (i + by) % count) for i in range(count)])  14.6 us
    ppermute x6, waiting for transfers between devices, exchanged(): got.append(lax.ppermute(pieces[c], 'dp', to))  11.3 us
    ppermute x6, starting transfers between devices, exchanged(): got.append(lax.ppermute(pieces[c], 'dp', to))  8.43 us
    pallas_call x6, Pallas kernels, called(): pl.pallas_call(kernel, in_specs=more.get('in_specs', [whole_vmem()] * len...  8.37 us
    unnamed x6, local copies, waits for them, and re-layouts  2.45 us
  transfers between devices with their start and end apart: 14, of which 4 were waited for; matrix products, arithmetic and copies ran while one was open for 1% of the time, Pallas kernels for 9%

profile of v2, /device:TPU:0, one launch (start us, length us, event | category | flops | bytes accessed | tf_op | source)
XLA Modules:
  0.0 85.7 jit_solution(7415857543227691933)
XLA Ops:
  0.7 1.2 %copy-done.1 = bf16[1,64,4096]{2,1,0:T(8,128)(2,1)S(1)} copy-done((bf16[1,64,4096]{2,1,0:T(8,128)(2,1)S(1)}, bf16[1,64,4096]{2,1,0:T(8,128)(2,1)}, u32[]{:S(2)}) %copy-start.1) | copy-done | bytes 524312
  1.8 1.3 %copy-done.2 = bf16[1,64,4096]{2,1,0:T(8,128)(2,1)S(1)} copy-done((bf16[1,64,4096]{2,1,0:T(8,128)(2,1)S(1)}, bf16[1,64,4096]{2,1,0:T(8,128)(2,1)}, u32[]{:S(2)}) %copy-start.2) | copy-done | bytes 524312
  3.1 0.2 group_sums.1
  3.3 5.1 %collective-permute-start.2 = (bf16[64,512]{1,0:T(8,128)(2,1)S(1)}, bf16[64,512]{1,0:T(8,128)(2,1)S(1)}, u32[]{:S(2)}, u32[]{:S(2)}) collective-permute-start(bf16[64,512]{1,0:T(8,128)(2,1)S(1)} %get-tuple-element.23), channel_id=1, source_target_pairs={{0,24},{8,0},{16,8},{24,16},{1,25},{9,1},{17,9},{25,17},{2,26},{10... | collective-permute-start | bytes 196616 | tf_op jit(solution)/shard_map/ppermute | solution.py:25
  8.5 0.0 collective-permute-start.3
  8.5 0.0 collective-permute-start
  8.5 3.8 %collective-permute-start.1 = (bf16[64,4096]{1,0:T(8,128)(2,1)}, bf16[64,4096]{1,0:T(8,128)(2,1)S(1)}, u32[]{:S(2)}, u32[]{:S(2)}) collective-permute-start(bf16[64,4096]{1,0:T(8,128)(2,1)} %bitcast.25), channel_id=1, source_target_pairs={{0,24},{8,0},{16,8},{24,16},{1,25},{9,1},{17,9},{25,17},{2,26},{10... | collective-permute-start | bytes 1572872 | tf_op jit(solution)/shard_map/ppermute | solution.py:25
  12.3 0.8 slice_bitcast_fusion
  13.1 21.6 %collective-permute-done.1.up_ref.x_ref = bf16[64,4096]{1,0:T(8,128)(2,1)S(1)} collective-permute-done((bf16[64,4096]{1,0:T(8,128)(2,1)}, bf16[64,4096]{1,0:T(8,128)(2,1)S(1)}, u32[]{:S(2)}, u32[]{:S(2)}) %collective-permute-start.1) | collective-permute-done | bytes 524320 | tf_op jit(solution)/shard_map/ppermute | solution.py:25
  34.7 0.2 shard_map.105
  34.9 1.6 %collective-permute-start.10 = (bf16[2,64,512]{2,1,0:T(8,128)(2,1)S(1)}, bf16[2,64,512]{2,1,0:T(8,128)(2,1)S(1)}, u32[]{:S(2)}, u32[]{:S(2)}) collective-permute-start(bf16[2,64,512]{2,1,0:T(8,128)(2,1)S(1)} %get-tuple-element.36), channel_id=1, source_target_pairs={{0,2},{1,3},{2,0},{3,1},{4,6},{5,7},{6,4},{7,5},{8,10},{9,11},{10,... | collective-permute-start | bytes 393224 | tf_op jit(solution)/shard_map/ppermute | solution.py:365
  36.5 0.1 broadcast_in_dim.10.match_down.match_ref
  36.6 0.1 broadcast_in_dim.11.match_up.match_ref
  36.7 0.3 shard_map.101
  36.9 0.6 collective-permute-start.7
  37.5 1.5 %collective-permute-start.8 = (bf16[4,64,512]{2,1,0:T(8,128)(2,1)S(1)}, bf16[4,64,512]{2,1,0:T(8,128)(2,1)S(1)}, u32[]{:S(2)}, u32[]{:S(2)}) collective-permute-start(bf16[4,64,512]{2,1,0:T(8,128)(2,1)S(1)} %get-tuple-element.33), channel_id=1, source_target_pairs={{0,4},{1,5},{2,6},{3,7},{4,0},{5,1},{6,2},{7,3},{8,12},{9,13},{10,... | collective-permute-start | bytes 786440 | tf_op jit(solution)/shard_map/ppermute | solution.py:365
  39.1 1.4 %collective-permute-start.9 = (bf16[4,64,512]{2,1,0:T(8,128)(2,1)S(1)}, bf16[4,64,512]{2,1,0:T(8,128)(2,1)S(1)}, u32[]{:S(2)}, u32[]{:S(2)}) collective-permute-start(bf16[4,64,512]{2,1,0:T(8,128)(2,1)S(1)} %get-tuple-element.34), channel_id=1, source_target_pairs={{0,6},{1,7},{2,4},{3,5},{4,2},{5,3},{6,0},{7,1},{8,14},{9,15},{10,... | collective-permute-start | bytes 786440 | tf_op jit(solution)/shard_map/ppermute | solution.py:365
  40.5 1.5 %collective-permute-start.11 = (bf16[2,64,512]{2,1,0:T(8,128)(2,1)S(1)}, bf16[2,64,512]{2,1,0:T(8,128)(2,1)S(1)}, u32[]{:S(2)}, u32[]{:S(2)}) collective-permute-start(bf16[2,64,512]{2,1,0:T(8,128)(2,1)S(1)} %get-tuple-element.37), channel_id=1, source_target_pairs={{0,4},{1,5},{2,6},{3,7},{4,0},{5,1},{6,2},{7,3},{8,12},{9,13},{10,... | collective-permute-start | bytes 393224 | tf_op jit(solution)/shard_map/ppermute | solution.py:365
  42.0 1.8 %collective-permute-start.12 = (bf16[2,64,512]{2,1,0:T(8,128)(2,1)S(1)}, bf16[2,64,512]{2,1,0:T(8,128)(2,1)S(1)}, u32[]{:S(2)}, u32[]{:S(2)}) collective-permute-start(bf16[2,64,512]{2,1,0:T(8,128)(2,1)S(1)} %get-tuple-element.38), channel_id=1, source_target_pairs={{0,6},{1,7},{2,4},{3,5},{4,2},{5,3},{6,0},{7,1},{8,14},{9,15},{10,... | collective-permute-start | bytes 393224 | tf_op jit(solution)/shard_map/ppermute | solution.py:365
  43.8 11.3 %collective-permute-done.11.refs_6_ = bf16[2,64,512]{2,1,0:T(8,128)(2,1)S(1)} collective-permute-done((bf16[2,64,512]{2,1,0:T(8,128)(2,1)S(1)}, bf16[2,64,512]{2,1,0:T(8,128)(2,1)S(1)}, u32[]{:S(2)}, u32[]{:S(2)}) %collective-permute-start.11) | collective-permute-done | bytes 131104 | tf_op jit(solution)/shard_map/ppermute | solution.py:365
  55.1 0.0 collective-permute-done.12.refs_7_
  55.2 0.8 shard_map.106
  55.9 0.1 collective-permute-start.13
  56.0 3.5 %collective-permute-start.6 = (bf16[64,4096]{1,0:T(8,128)(2,1)}, bf16[64,4096]{1,0:T(8,128)(2,1)S(1)}, u32[]{:S(2)}, u32[]{:S(2)}) collective-permute-start(bf16[64,4096]{1,0:T(8,128)(2,1)} %bitcast.18), channel_id=1, source_target_pairs={{0,8},{8,16},{16,24},{24,0},{1,9},{9,17},{17,25},{25,1},{2,10},{10... | collective-permute-start | bytes 1572872 | tf_op jit(solution)/shard_map/ppermute | solution.py:25
  59.5 0.4 collective-permute-start.5
  59.9 1.7 %collective-permute-start.4 = (bf16[16,4096]{1,0:T(8,128)(2,1)S(1)}, bf16[16,4096]{1,0:T(8,128)(2,1)S(1)}, u32[]{:S(2)}, u32[]{:S(2)}) collective-permute-start(bf16[16,4096]{1,0:T(8,128)(2,1)S(1)} %get-tuple-element.29), channel_id=1, source_target_pairs={{0,24},{8,0},{16,8},{24,16},{1,25},{9,1},{17,9},{25,17},{2,26},{10... | collective-permute-start | bytes 393224 | tf_op jit(solution)/shard_map/ppermute | solution.py:25
  61.6 5.0 %shard_map.102 = (bf16[64,4096]{1,0:T(8,128)(2,1)}, bf16[64,4096]{1,0:T(8,128)(2,1)}, f32[2,64,4096]{2,1,0:T(8,128)S(1)}) custom-call(bf16[64,4096]{1,0:T(8,128)(2,1)S(1)} %collective-permute-done.x_ref.down_ref, bf16[64,4096]{1,0:T(8,128)(2,1)S(1)} %collective-permute-done.1.up_ref.x_ref, bf16[128,512]{1,0:T(8,128)(2,1)S(1)} %get-tuple-element.25.grouped_ref, ...), custom_call_target="tpu_custom_call" | custom-call | flops 1073741824 | bytes 8519680 | tf_op jit(solution)/shard_map/pallas_call | solution.py:34
  66.6 6.3 %collective-permute-done.6.refs_0_ = bf16[64,4096]{1,0:T(8,128)(2,1)S(1)} collective-permute-done((bf16[64,4096]{1,0:T(8,128)(2,1)}, bf16[64,4096]{1,0:T(8,128)(2,1)S(1)}, u32[]{:S(2)}, u32[]{:S(2)}) %collective-permute-start.6) | collective-permute-done | bytes 524320 | tf_op jit(solution)/shard_map/ppermute | solution.py:25
  72.9 1.1 %shard_map.104 = bf16[2,32,4096]{2,1,0:T(8,128)(2,1)} custom-call(s32[2,2,128]{2,1,0:T(2,128)S(1)} %broadcast_in_dim.11.match_up.match_ref, f32[2,64,4096]{2,1,0:T(8,128)S(1)} %get-tuple-element.28.through_ref, bf16[64,4096]{1,0:T(8,128)(2,1)S(1)} %collective-permute-done.6.refs_0_), custom_call_target="tpu_custom_call" | custom-call | flops 524288 | bytes 3147776 | tf_op jit(solution)/shard_map/pallas_call | solution.py:34
  74.0 9.6 %collective-permute-done.4.refs_0_ = bf16[16,4096]{1,0:T(8,128)(2,1)S(1)} collective-permute-done((bf16[16,4096]{1,0:T(8,128)(2,1)S(1)}, bf16[16,4096]{1,0:T(8,128)(2,1)S(1)}, u32[]{:S(2)}, u32[]{:S(2)}) %collective-permute-start.4) | collective-permute-done | bytes 131104 | tf_op jit(solution)/shard_map/ppermute | solution.py:25
  83.6 1.1 %shard_map.103 = bf16[2,32,4096]{2,1,0:T(8,128)(2,1)} custom-call(s32[2,2,128]{2,1,0:T(2,128)S(1)} %broadcast_in_dim.10.match_down.match_ref, f32[2,64,4096]{2,1,0:T(8,128)S(1)} %get-tuple-element.28.through_ref, bf16[16,4096]{1,0:T(8,128)(2,1)S(1)} %collective-permute-done.4.refs_0_, bf16[48,4096]{1,0:T(8,128)(2,1)S(1)} %collective-permute-done.5.refs_1_), custom_call_target="tpu_custom_call" | custom-call | flops 524288 | bytes 3147776 | tf_op jit(solution)/shard_map/pallas_call | solution.py:34
  84.6 1.0 %combine.1 = f32[512,512]{1,0:T(8,128)} custom-call(f32[512,512]{1,0:T(8,128)S(1)} %get-tuple-element.39.keep_ref, f32[512,512]{1,0:T(8,128)S(1)} %collective-permute-done.13.got_ref), custom_call_target="tpu_custom_call" | custom-call | flops 524288 | bytes 3145728 | tf_op jit(solution)/shard_map/combine/pallas_call | solution.py:216
  (15 shorter events, 0.0 us)
Async XLA Ops:
  0.6 61.0 %copy-start = (bf16[1,4096,512]{2,1,0:T(8,128)(2,1)S(1)}, bf16[1,4096,512]{2,1,0:T(8,128)(2,1)}, u32[]{:S(2)}) copy-start(bf16[1,4096,512]{2,1,0:T(8,128)(2,1)} %param.11) | copy-start | bytes 12582916
  0.6 1.2 %copy-start.1 = (bf16[1,64,4096]{2,1,0:T(8,128)(2,1)S(1)}, bf16[1,64,4096]{2,1,0:T(8,128)(2,1)}, u32[]{:S(2)}) copy-start(bf16[1,64,4096]{2,1,0:T(8,128)(2,1)} %param.8) | copy-start | bytes 1572868
  1.8 1.3 %copy-start.2 = (bf16[1,64,4096]{2,1,0:T(8,128)(2,1)S(1)}, bf16[1,64,4096]{2,1,0:T(8,128)(2,1)}, u32[]{:S(2)}) copy-start(bf16[1,64,4096]{2,1,0:T(8,128)(2,1)} %param.9) | copy-start | bytes 1572868
  3.3 33.2 %collective-permute-start.2 = (bf16[64,512]{1,0:T(8,128)(2,1)S(1)}, bf16[64,512]{1,0:T(8,128)(2,1)S(1)}, u32[]{:S(2)}, u32[]{:S(2)}) collective-permute-start(bf16[64,512]{1,0:T(8,128)(2,1)S(1)} %get-tuple-element.23), channel_id=1, source_target_pairs={{0,24},{8,0},{16,8},{24,16},{1,25},{9,1},{17,9},{25,17},{2,26},{10... | collective-permute-start | bytes 196616 | tf_op jit(solution)/shard_map/ppermute | solution.py:25
  8.5 28.0 %collective-permute-start.3 = (bf16[64,512]{1,0:T(8,128)(2,1)S(1)}, bf16[64,512]{1,0:T(8,128)(2,1)S(1)}, u32[]{:S(2)}, u32[]{:S(2)}) collective-permute-start(bf16[64,512]{1,0:T(8,128)(2,1)S(1)} %get-tuple-element.24), channel_id=1, source_target_pairs={{0,8},{8,16},{16,24},{24,0},{1,9},{9,17},{17,25},{25,1},{2,10},{10... | collective-permute-start | bytes 196616 | tf_op jit(solution)/shard_map/ppermute | solution.py:25
  8.5 28.0 %collective-permute-start = (bf16[64,4096]{1,0:T(8,128)(2,1)}, bf16[64,4096]{1,0:T(8,128)(2,1)S(1)}, u32[]{:S(2)}, u32[]{:S(2)}) collective-permute-start(bf16[64,4096]{1,0:T(8,128)(2,1)} %bitcast.26), channel_id=1, source_target_pairs={{0,8},{8,16},{16,24},{24,0},{1,9},{9,17},{17,25},{25,1},{2,10},{10... | collective-permute-start | bytes 1572872 | tf_op jit(solution)/shard_map/ppermute | solution.py:25
  8.5 26.2 %collective-permute-start.1 = (bf16[64,4096]{1,0:T(8,128)(2,1)}, bf16[64,4096]{1,0:T(8,128)(2,1)S(1)}, u32[]{:S(2)}, u32[]{:S(2)}) collective-permute-start(bf16[64,4096]{1,0:T(8,128)(2,1)} %bitcast.25), channel_id=1, source_target_pairs={{0,24},{8,0},{16,8},{24,16},{1,25},{9,1},{17,9},{25,17},{2,26},{10... | collective-permute-start | bytes 1572872 | tf_op jit(solution)/shard_map/ppermute | solution.py:25
  34.9 7.1 %collective-permute-start.10 = (bf16[2,64,512]{2,1,0:T(8,128)(2,1)S(1)}, bf16[2,64,512]{2,1,0:T(8,128)(2,1)S(1)}, u32[]{:S(2)}, u32[]{:S(2)}) collective-permute-start(bf16[2,64,512]{2,1,0:T(8,128)(2,1)S(1)} %get-tuple-element.36), channel_id=1, source_target_pairs={{0,2},{1,3},{2,0},{3,1},{4,6},{5,7},{6,4},{7,5},{8,10},{9,11},{10,... | collective-permute-start | bytes 393224 | tf_op jit(solution)/shard_map/ppermute | solution.py:365
  36.9 18.2 %collective-permute-start.7 = (bf16[4,64,512]{2,1,0:T(8,128)(2,1)S(1)}, bf16[4,64,512]{2,1,0:T(8,128)(2,1)S(1)}, u32[]{:S(2)}, u32[]{:S(2)}) collective-permute-start(bf16[4,64,512]{2,1,0:T(8,128)(2,1)S(1)} %get-tuple-element.32), channel_id=1, source_target_pairs={{0,2},{1,3},{2,0},{3,1},{4,6},{5,7},{6,4},{7,5},{8,10},{9,11},{10,... | collective-permute-start | bytes 786440 | tf_op jit(solution)/shard_map/ppermute | solution.py:365
  37.5 17.6 %collective-permute-start.8 = (bf16[4,64,512]{2,1,0:T(8,128)(2,1)S(1)}, bf16[4,64,512]{2,1,0:T(8,128)(2,1)S(1)}, u32[]{:S(2)}, u32[]{:S(2)}) collective-permute-start(bf16[4,64,512]{2,1,0:T(8,128)(2,1)S(1)} %get-tuple-element.33), channel_id=1, source_target_pairs={{0,4},{1,5},{2,6},{3,7},{4,0},{5,1},{6,2},{7,3},{8,12},{9,13},{10,... | collective-permute-start | bytes 786440 | tf_op jit(solution)/shard_map/ppermute | solution.py:365
  39.1 16.1 %collective-permute-start.9 = (bf16[4,64,512]{2,1,0:T(8,128)(2,1)S(1)}, bf16[4,64,512]{2,1,0:T(8,128)(2,1)S(1)}, u32[]{:S(2)}, u32[]{:S(2)}) collective-permute-start(bf16[4,64,512]{2,1,0:T(8,128)(2,1)S(1)} %get-tuple-element.34), channel_id=1, source_target_pairs={{0,6},{1,7},{2,4},{3,5},{4,2},{5,3},{6,0},{7,1},{8,14},{9,15},{10,... | collective-permute-start | bytes 786440 | tf_op jit(solution)/shard_map/ppermute | solution.py:365
  40.5 14.6 %collective-permute-start.11 = (bf16[2,64,512]{2,1,0:T(8,128)(2,1)S(1)}, bf16[2,64,512]{2,1,0:T(8,128)(2,1)S(1)}, u32[]{:S(2)}, u32[]{:S(2)}) collective-permute-start(bf16[2,64,512]{2,1,0:T(8,128)(2,1)S(1)} %get-tuple-element.37), channel_id=1, source_target_pairs={{0,4},{1,5},{2,6},{3,7},{4,0},{5,1},{6,2},{7,3},{8,12},{9,13},{10,... | collective-permute-start | bytes 393224 | tf_op jit(solution)/shard_map/ppermute | solution.py:365
  42.0 13.1 %collective-permute-start.12 = (bf16[2,64,512]{2,1,0:T(8,128)(2,1)S(1)}, bf16[2,64,512]{2,1,0:T(8,128)(2,1)S(1)}, u32[]{:S(2)}, u32[]{:S(2)}) collective-permute-start(bf16[2,64,512]{2,1,0:T(8,128)(2,1)S(1)} %get-tuple-element.38), channel_id=1, source_target_pairs={{0,6},{1,7},{2,4},{3,5},{4,2},{5,3},{6,0},{7,1},{8,14},{9,15},{10,... | collective-permute-start | bytes 393224 | tf_op jit(solution)/shard_map/ppermute | solution.py:365
  55.9 28.7 %collective-permute-start.13 = (f32[512,512]{1,0:T(8,128)S(1)}, f32[512,512]{1,0:T(8,128)S(1)}, u32[]{:S(2)}, u32[]{:S(2)}) collective-permute-start(f32[512,512]{1,0:T(8,128)S(1)} %get-tuple-element.40), channel_id=1, source_target_pairs={{0,1},{1,0},{2,3},{3,2},{4,5},{5,4},{6,7},{7,6},{8,9},{9,8},{10,11... | collective-permute-start | bytes 3145736 | tf_op jit(solution)/shard_map/ppermute | solution.py:375
  56.0 16.9 %collective-permute-start.6 = (bf16[64,4096]{1,0:T(8,128)(2,1)}, bf16[64,4096]{1,0:T(8,128)(2,1)S(1)}, u32[]{:S(2)}, u32[]{:S(2)}) collective-permute-start(bf16[64,4096]{1,0:T(8,128)(2,1)} %bitcast.18), channel_id=1, source_target_pairs={{0,8},{8,16},{16,24},{24,0},{1,9},{9,17},{17,25},{25,1},{2,10},{10... | collective-permute-start | bytes 1572872 | tf_op jit(solution)/shard_map/ppermute | solution.py:25
  59.5 24.1 %collective-permute-start.5 = (bf16[48,4096]{1,0:T(8,128)(2,1)S(1)}, bf16[48,4096]{1,0:T(8,128)(2,1)S(1)}, u32[]{:S(2)}, u32[]{:S(2)}) collective-permute-start(bf16[48,4096]{1,0:T(8,128)(2,1)S(1)} %get-tuple-element.30), channel_id=1, source_target_pairs={{0,24},{8,0},{16,8},{24,16},{1,25},{9,1},{17,9},{25,17},{2,26},{10... | collective-permute-start | bytes 1179656 | tf_op jit(solution)/shard_map/ppermute | solution.py:25
  59.9 23.7 %collective-permute-start.4 = (bf16[16,4096]{1,0:T(8,128)(2,1)S(1)}, bf16[16,4096]{1,0:T(8,128)(2,1)S(1)}, u32[]{:S(2)}, u32[]{:S(2)}) collective-permute-start(bf16[16,4096]{1,0:T(8,128)(2,1)S(1)} %get-tuple-element.29), channel_id=1, source_target_pairs={{0,24},{8,0},{16,8},{24,16},{1,25},{9,1},{17,9},{25,17},{2,26},{10... | collective-permute-start | bytes 393224 | tf_op jit(solution)/shard_map/ppermute | solution.py:25

commit v3 on v2

--- a/solution.py
+++ b/solution.py
@@ -44,8 +44,8 @@
     )(*operands)
 
 
-def group_kernel(down_ref, up_ref, down_out, up_out, first_out, rest_out):
-    step = pl.program_id(0)
+def group_kernel(down_ref, up_ref, down_out, up_out, *halves):
+    part = pl.program_id(1)
     for src, dst in ((down_ref, down_out), (up_ref, up_out)):
         for k in range(KVH):
             total = src[:, k * GROUPS * HD : (k * GROUPS + 1) * HD].astype(jnp.float32)
@@ -54,42 +54,31 @@
                 total = total + src[:, at : at + HD].astype(jnp.float32)
             dst[:, k * HD : (k + 1) * HD] = total.astype(dst.dtype)
 
-    @pl.when(step == 0)
-    def _():
-        first_out[...] = down_ref[...]
-
-    @pl.when(step > 0)
-    def _():
-        rest_out[...] = down_ref[...]
-
-
-def group_sums(down, up):
+    for own in range(2):
+
+        @pl.when(part == own)
+        def _():
+            halves[own][0] = down_ref[...]
+            halves[2 + own][0] = up_ref[...]
+
+
+def group_sums(down, up, blocks):
     rows, width = down.shape
-    steps = 4
-    step = rows // steps
-    wide = pl.BlockSpec((step, width), lambda i: (i, 0))
-    narrow = pl.BlockSpec((step, width // GROUPS), lambda i: (i, 0))
+    step = rows // blocks // 2
+    wide = pl.BlockSpec((step, width), lambda j, i: (2 * j + i, 0))
+    narrow = pl.BlockSpec((step, width // GROUPS), lambda j, i: (2 * j + i, 0))
+    half = pl.BlockSpec((1, step, width), lambda j, i: (j, 0, 0))
     out = jax.ShapeDtypeStruct((rows, width // GROUPS), down.dtype)
     return pl.pallas_call(
         group_kernel,
-        grid=(steps,),
+        grid=(blocks, 2),
         in_specs=[wide, wide],
-        out_specs=[
-            narrow,
-            narrow,
-            pl.BlockSpec((step, width), lambda i: (0, 0)),
-            pl.BlockSpec((step, width), lambda i: (jnp.maximum(i - 1, 0), 0)),
-        ],
-        out_shape=[
-            out,
-            out,
-            jax.ShapeDtypeStruct((step, width), down.dtype),
-            jax.ShapeDtypeStruct((rows - step, width), down.dtype),
-        ],
+        out_specs=[narrow, narrow] + [half] * 4,
+        out_shape=[out, out] + [jax.ShapeDtypeStruct((blocks, step, width), down.dtype)] * 4,
         name="group_sums",
         compiler_params=pltpu.CompilerParams(vmem_limit_bytes=6 * MIB),
         cost_estimate=pl.CostEstimate(
-            flops=2 * rows * width, bytes_accessed=6 * rows * width, transcendentals=0
+            flops=2 * rows * width, bytes_accessed=8 * rows * width, transcendentals=0
         ),
     )(down, up)
 
@@ -114,7 +103,8 @@
             piece[b] = (x_ref[:, at].astype(jnp.float32) * inverse).astype(piece.dtype)
 
 
-def down_kernel(chips, x_ref, match_down, match_up, down_ref, up_ref, grouped_ref, *pieces):
+def down_kernel(chips, x_ref, match_down, match_up, down_ref, up_ref, *outs):
+    grouped_refs, pieces = outs[:2], outs[2:]
     write_normed(chips, x_ref, pieces)
     blocks, rows, inner = down_ref.shape
     unit = pieces[0].shape[-1]
@@ -125,9 +115,8 @@
             for j in range(1, blocks):
                 mine = match[m, j : j + 1, 0:1] != 0
                 chosen = jnp.where(mine, ref[j].astype(jnp.float32), chosen)
-            chosen = chosen.astype(grouped_ref.dtype)
-            at = (leg * blocks + m) * rows
-            grouped_ref[at : at + rows, :] = chosen
+            chosen = chosen.astype(x_ref.dtype)
+            grouped_refs[leg][m * rows : (m + 1) * rows, :] = chosen
             for piece in pieces:
                 for b in range(inner // unit):
                     piece[own + leg * (inner // unit) + b, m * rows : (m + 1) * rows, :] = chosen[
@@ -147,7 +136,7 @@
     count = width // chips // unit + 2 * inner // unit
     blocks = match_down.shape[0]
     cut = (blocks, rows // blocks, inner)
-    outputs = [jax.ShapeDtypeStruct((2 * rows, inner), x.dtype)]
+    outputs = [jax.ShapeDtypeStruct((rows, inner), x.dtype)] * 2
     outputs += [jax.ShapeDtypeStruct((count, rows, unit), x.dtype)] * chips
     return called(
         functools.partial(down_kernel, chips),
@@ -227,12 +216,8 @@
     )(keep, got)
 
 
-def span_kernel(
-    down_ref, up_ref, grouped_ref, weight_ref,
-    next_down, next_up, through,
-    scaled, back, held, arrived,
-):
-    rows, width = down_ref.shape
+def span_kernel(x_ref, grouped_ref, weight_ref, next_ref, through_ref, scaled, back, held, arrived):
+    rows, width = x_ref.shape
     tiles, tile, inner = held.shape
     copies = [
         pltpu.make_async_copy(weight_ref.at[pl.ds(t * tile, tile), :], held.at[t], arrived.at[t])
@@ -240,20 +225,17 @@
     ]
     for copy in copies:
         copy.start()
-    inverses = []
-    for leg, ref in enumerate((down_ref, up_ref)):
-        x = ref[...].astype(jnp.float32)
-        inverse = inverse_of(x)
-        inverses.append(inverse)
-        scaled[leg * rows : (leg + 1) * rows, :] = x * inverse
-    values = jnp.zeros((2 * rows, inner), jnp.float32)
-    total = jnp.zeros((2 * rows, HD), jnp.float32)
+    x = x_ref[...].astype(jnp.float32)
+    inverse = inverse_of(x)
+    scaled[...] = x * inverse
+    values = jnp.zeros((rows, inner), jnp.float32)
+    total = jnp.zeros((rows, HD), jnp.float32)
     grouped = grouped_ref[...]
     for t, copy in enumerate(copies):
         copy.wait()
         weight = held[t]
         at = slice(t * tile, (t + 1) * tile)
-        normed = scaled[:, at].astype(down_ref.dtype)
+        normed = scaled[:, at].astype(x_ref.dtype)
         values = values + jnp.dot(normed, weight, preferred_element_type=jnp.float32)
         part = lax.dot_general(
             grouped, weight, (((1,), (1,)), ((), ())), preferred_element_type=jnp.float32
@@ -262,76 +244,90 @@
         for c in range(tile // HD):
             lanes = slice(c * HD, (c + 1) * HD)
             total = total + part[:, lanes] * scaled[:, t * tile + c * HD : t * tile + (c + 1) * HD]
-    means = jnp.sum(total, axis=-1, keepdims=True) * (1.0 / width)
-    for leg, (ref, nxt) in enumerate(((down_ref, next_down), (up_ref, next_up))):
-        own = slice(leg * rows, (leg + 1) * rows)
-        mean = jnp.broadcast_to(means[own], (rows, HD))
-        inverse = jnp.broadcast_to(inverses[leg], (rows, HD))
-        for k in range(KVH):
-            spread = values[own, k * HD : (k + 1) * HD]
-            for j in range(GROUPS):
-                at = slice((k * GROUPS + j) * HD, (k * GROUPS + j + 1) * HD)
-                nxt[:, at] = (ref[:, at].astype(jnp.float32) + spread).astype(nxt.dtype)
-                through[leg, :, at] = inverse * (back[own, at] - scaled[own, at] * mean)
-
-
-def span(down, up, grouped, weight):
-    rows, width = down.shape
+    mean = jnp.sum(total, axis=-1, keepdims=True) * (1.0 / width)
+    mean = jnp.broadcast_to(mean, (rows, HD))
+    inverse = jnp.broadcast_to(inverse, (rows, HD))
+    for k in range(KVH):
+        spread = values[:, k * HD : (k + 1) * HD]
+        for j in range(GROUPS):
+            at = slice((k * GROUPS + j) * HD, (k * GROUPS + j + 1) * HD)
+            next_ref[:, at] = (x_ref[:, at].astype(jnp.float32) + spread).astype(next_ref.dtype)
+            through_ref[:, at] = inverse * (back[:, at] - scaled[:, at] * mean)
+
+
+def span(x, grouped, weight):
+    rows, width = x.shape
     inner = weight.shape[1]
     tile = math.gcd(width, 512)
     return called(
         span_kernel,
-        (down, up, grouped, weight),
-        [jax.ShapeDtypeStruct((rows, width), down.dtype)] * 2
-        + [jax.ShapeDtypeStruct((2, rows, width), jnp.float32)],
+        (x, grouped, pltpu.with_memory_space_constraint(weight, pltpu.HBM)),
+        [
+            jax.ShapeDtypeStruct((rows, width), x.dtype),
+            jax.ShapeDtypeStruct((rows, width), jnp.float32),
+        ],
         scratch=[
-            pltpu.VMEM((2 * rows, width), jnp.float32),
-            pltpu.VMEM((2 * rows, width), jnp.float32),
+            pltpu.VMEM((rows, width), jnp.float32),
+            pltpu.VMEM((rows, width), jnp.float32),
             pltpu.VMEM((width // tile, tile, inner), weight.dtype),
             pltpu.SemaphoreType.DMA((width // tile,)),
         ],
-        flops=8 * rows * width * inner,
-        vmem=12,
-        in_specs=[whole_vmem()] * 3 + [pl.BlockSpec(memory_space=pltpu.HBM)],
-    )
-
-
-def finish_kernel(leg, cuts, match_ref, through_ref, *refs):
-    pieces, out_ref = refs[:-1], refs[-1]
-    blocks, rows, _ = out_ref.shape
-    unit = functools.reduce(math.gcd, cuts, rows)
-
-    def units(start):
-        at = 0
-        for ref, cut in zip(pieces, cuts):
-            if start < at + cut:
-                return ref[start - at : start - at + unit, :]
-            at += cut
-
-    for m in range(blocks):
-        for start in range(0, rows, unit):
-            chosen = units(start).astype(jnp.float32)
+        flops=4 * rows * width * inner,
+        vmem=10,
+        in_specs=[whole_vmem()] * 2 + [pl.BlockSpec(memory_space=pltpu.HBM)],
+    )
+
+
+def finish_kernel(parts, match_ref, through_ref, *refs):
+    raws = refs[: len(parts)]
+    out_ref, held, sent = refs[-3:]
+    blocks, half, _ = raws[0].shape
+    copies = []
+    for i, (part, raw) in enumerate(zip(parts, raws)):
+        for m in range(blocks):
+            chosen = raw[0].astype(jnp.float32)
             for j in range(1, blocks):
                 mine = match_ref[m, j : j + 1, 0:1] != 0
-                chosen = jnp.where(mine, units(j * rows + start).astype(jnp.float32), chosen)
-            at = m * rows + start
-            total = chosen + through_ref[leg, at : at + unit, :]
-            out_ref[m, start : start + unit, :] = total.astype(out_ref.dtype)
-
-
-def finished(pieces, match, through, leg):
-    width = pieces[0].shape[1]
-    cuts = [piece.shape[0] for piece in pieces]
-    rows = sum(cuts)
-    blocks = match.shape[0]
-    cut = (blocks, rows // blocks, width)
-    (out,) = called(
-        functools.partial(finish_kernel, leg, cuts),
-        (match, through, *pieces),
-        [jax.ShapeDtypeStruct(cut, pieces[0].dtype)],
-        flops=2 * rows * width,
-    )
-    return out.reshape(rows, width)
+                chosen = jnp.where(mine, raw[j].astype(jnp.float32), chosen)
+            at = (2 * m + part) * half
+            slot = i * blocks + m
+            held[slot] = (chosen + through_ref[at : at + half, :]).astype(held.dtype)
+            copies.append(
+                pltpu.make_async_copy(
+                    held.at[slot], out_ref.at[pl.ds(at, half), :], sent.at[slot]
+                )
+            )
+            copies[-1].start()
+    for copy in copies:
+        copy.wait()
+
+
+def finished(raws, parts, match, through, before=None):
+    rows, width = through.shape
+    blocks, half, _ = raws[0].shape
+    slots = blocks * len(parts)
+    operands = [match, through, *raws] + ([] if before is None else [before])
+    specs = [whole_vmem()] * (2 + len(raws))
+    if before is not None:
+        specs.append(pl.BlockSpec(memory_space=pltpu.HBM))
+    return pl.pallas_call(
+        functools.partial(finish_kernel, parts),
+        in_specs=specs,
+        out_specs=pl.BlockSpec(memory_space=pltpu.HBM),
+        out_shape=jax.ShapeDtypeStruct((rows, width), raws[0].dtype),
+        scratch_shapes=[
+            pltpu.VMEM((slots, half, width), raws[0].dtype),
+            pltpu.SemaphoreType.DMA((slots,)),
+        ],
+        input_output_aliases={} if before is None else {len(operands) - 1: 0},
+        name="finished",
+        compiler_params=pltpu.CompilerParams(vmem_limit_bytes=4 * MIB),
+        cost_estimate=pl.CostEstimate(
+            flops=2 * slots * half * width,
+            bytes_accessed=8 * slots * half * width,
+            transcendentals=0,
+        ),
+    )(*operands)
 
 
 def matches(roster_row):
@@ -350,13 +346,15 @@
     match_down = matches(roster[0, 0])
     match_up = matches(roster[0, 1])
 
-    sums_down, sums_up, first_down, rest_down = group_sums(cotangent_down[0], cotangent_up[0])
+    sums_down, sums_up, *halves = group_sums(
+        cotangent_down[0], cotangent_up[0], roster.shape[2]
+    )
     x_down = passed_along(feed_down[0], "section", 1)
     sums_up = passed_along(sums_up, "section", 1)
     sums_down = passed_along(sums_down, "section", -1)
     x_up = passed_along(feed_up[0], "section", -1)
-    raw_down = [passed_along(first_down, "section", -1), passed_along(rest_down, "section", -1)]
-    raw_up = [passed_along(cotangent_up[0], "section", 1)]
+    raw_down = [passed_along(half, "section", -1) for half in halves[:2]]
+    raw_up = [passed_along(half, "section", 1) for half in halves[2:]]
 
     def exchanged(pieces):
         got = [pieces[0]]
@@ -365,18 +363,20 @@
             got.append(lax.ppermute(pieces[c], "dp", to))
         return got
 
-    grouped, *sent_down = pieces_down(x_down, sums_down, sums_up, match_down, match_up, members)
+    grouped_down, grouped_up, *sent_down = pieces_down(x_down, sums_down, sums_up, match_down, match_up, members)
     got_down = exchanged(sent_down)
     got_up = exchanged(pieces_up(x_up, inner, members))
 
-    next_down, next_up, through = span(x_down, x_up, grouped, weight)
+    next_down, through_down = span(x_down, grouped_down, weight)
+    next_up, through_up = span(x_up, grouped_up, weight)
 
     keep, send = products(got_down, got_up, width, inner, members)
     got = lax.ppermute(send, "dp", [(i, i ^ 1) for i in range(members)])
     summed = combined(keep, got, float(2 * rows * members) ** (-0.5))
 
-    back_down = finished(raw_down, match_down, through, 0)
-    back_up = finished(raw_up, match_up, through, 1)
+    back_up = finished(raw_up, (0, 1), match_up, through_up)
+    part_down = finished(raw_down[:1], (0,), match_down, through_down)
+    back_down = finished(raw_down[1:], (1,), match_down, through_down, before=part_down)
     return (
         next_down[None],
         next_up[None],

time: 85.8 us -> 91.1 us (1.062)
  the two profiles are of different devices: /device:TPU:0 before, /device:TPU:8 now
where the time goes in v3:
time: 91.1 us; the launch traced here: 90.8 us
  waiting for transfers between devices  55.5 us (61%)
  starting transfers between devices  16.7 us (18%)
  Pallas kernels  14.9 us (16%)
  local copies, waits for them, and re-layouts  2.97 us (3%)
    ppermute x8, waiting for transfers between devices, passed_along(): lax.ppermute(shard, axis, [(i, (i + by) % count) for i in range(count)])  41.4 us
    ppermute x6, waiting for transfers between devices, exchanged(): got.append(lax.ppermute(pieces[c], 'dp', to))  14.1 us
    pallas_call x5, Pallas kernels, called(): pl.pallas_call(kernel, in_specs=more.get('in_specs', [whole_vmem()] * len...  11 us
    ppermute x6, starting transfers between devices, exchanged(): got.append(lax.ppermute(pieces[c], 'dp', to))  8.43 us
    ppermute x8, starting transfers between devices, passed_along(): lax.ppermute(shard, axis, [(i, (i + by) % count) for i in range(count)])  8.2 us
    pallas_call x3, Pallas kernels, finished(): pl.pallas_call(functools.partial(finish_kernel, parts), in_specs=specs, o...  2.54 us
    unnamed x4, local copies, waits for them, and re-layouts  2.08 us
  transfers between devices with their start and end apart: 15, of which 4 were waited for; matrix products, arithmetic and copies ran while one was open for 1% of the time, Pallas kernels for 14%

profile of v3, /device:TPU:8, one launch (start us, length us, event | category | flops | bytes accessed | tf_op | source)
XLA Modules:
  0.0 90.8 jit_solution(6118133526148131727)
XLA Ops:
  0.6 1.0 %copy-done = bf16[1,64,4096]{2,1,0:T(8,128)(2,1)S(1)} copy-done((bf16[1,64,4096]{2,1,0:T(8,128)(2,1)S(1)}, bf16[1,64,4096]{2,1,0:T(8,128)(2,1)}, u32[]{:S(2)}) %copy-start) | copy-done | bytes 524312
  1.7 1.0 %copy-done.1 = bf16[1,64,4096]{2,1,0:T(8,128)(2,1)S(1)} copy-done((bf16[1,64,4096]{2,1,0:T(8,128)(2,1)S(1)}, bf16[1,64,4096]{2,1,0:T(8,128)(2,1)}, u32[]{:S(2)}) %copy-start.1) | copy-done | bytes 524312
  2.7 0.3 group_sums.1
  3.1 2.0 %collective-permute-start.2 = (bf16[64,512]{1,0:T(8,128)(2,1)S(1)}, bf16[64,512]{1,0:T(8,128)(2,1)S(1)}, u32[]{:S(2)}, u32[]{:S(2)}) collective-permute-start(bf16[64,512]{1,0:T(8,128)(2,1)S(1)} %get-tuple-element.28), channel_id=1, source_target_pairs={{0,8},{8,16},{16,24},{24,0},{1,9},{9,17},{17,25},{25,1},{2,10},{10... | collective-permute-start | bytes 196616 | tf_op jit(solution)/shard_map/ppermute | solution.py:25
  5.1 1.6 %collective-permute-start = (bf16[64,4096]{1,0:T(8,128)(2,1)}, bf16[64,4096]{1,0:T(8,128)(2,1)S(1)}, u32[]{:S(2)}, u32[]{:S(2)}) collective-permute-start(bf16[64,4096]{1,0:T(8,128)(2,1)} %bitcast.26), channel_id=1, source_target_pairs={{0,8},{8,16},{16,24},{24,0},{1,9},{9,17},{17,25},{25,1},{2,10},{10... | collective-permute-start | bytes 1572872 | tf_op jit(solution)/shard_map/ppermute | solution.py:25
  6.7 0.5 collective-permute-start.3
  7.1 0.8 slice_bitcast_fusion
  7.9 25.6 %collective-permute-done.3.x_ref = bf16[64,4096]{1,0:T(8,128)(2,1)S(1)} collective-permute-done((bf16[64,4096]{1,0:T(8,128)(2,1)}, bf16[64,4096]{1,0:T(8,128)(2,1)S(1)}, u32[]{:S(2)}, u32[]{:S(2)}) %collective-permute-start.3) | collective-permute-done | bytes 524320 | tf_op jit(solution)/shard_map/ppermute | solution.py:25
  33.5 0.2 shard_map.104
  33.7 1.6 %collective-permute-start.11 = (bf16[2,64,512]{2,1,0:T(8,128)(2,1)S(1)}, bf16[2,64,512]{2,1,0:T(8,128)(2,1)S(1)}, u32[]{:S(2)}, u32[]{:S(2)}) collective-permute-start(bf16[2,64,512]{2,1,0:T(8,128)(2,1)S(1)} %get-tuple-element.44), channel_id=1, source_target_pairs={{0,2},{1,3},{2,0},{3,1},{4,6},{5,7},{6,4},{7,5},{8,10},{9,11},{10,... | collective-permute-start | bytes 393224 | tf_op jit(solution)/shard_map/ppermute | solution.py:363
  35.3 0.1 broadcast_in_dim.14.match_down.match_ref
  35.3 0.1 broadcast_in_dim.30.match_up.match_ref
  35.4 0.3 shard_map.101
  35.7 1.6 %collective-permute-start.10 = (bf16[4,64,512]{2,1,0:T(8,128)(2,1)S(1)}, bf16[4,64,512]{2,1,0:T(8,128)(2,1)S(1)}, u32[]{:S(2)}, u32[]{:S(2)}) collective-permute-start(bf16[4,64,512]{2,1,0:T(8,128)(2,1)S(1)} %get-tuple-element.42), channel_id=1, source_target_pairs={{0,6},{1,7},{2,4},{3,5},{4,2},{5,3},{6,0},{7,1},{8,14},{9,15},{10,... | collective-permute-start | bytes 786440 | tf_op jit(solution)/shard_map/ppermute | solution.py:363
  37.2 1.5 %collective-permute-start.8 = (bf16[4,64,512]{2,1,0:T(8,128)(2,1)S(1)}, bf16[4,64,512]{2,1,0:T(8,128)(2,1)S(1)}, u32[]{:S(2)}, u32[]{:S(2)}) collective-permute-start(bf16[4,64,512]{2,1,0:T(8,128)(2,1)S(1)} %get-tuple-element.40), channel_id=1, source_target_pairs={{0,2},{1,3},{2,0},{3,1},{4,6},{5,7},{6,4},{7,5},{8,10},{9,11},{10,... | collective-permute-start | bytes 786440 | tf_op jit(solution)/shard_map/ppermute | solution.py:363
  38.7 0.5 collective-permute-start.9
  39.2 1.5 %collective-permute-start.12 = (bf16[2,64,512]{2,1,0:T(8,128)(2,1)S(1)}, bf16[2,64,512]{2,1,0:T(8,128)(2,1)S(1)}, u32[]{:S(2)}, u32[]{:S(2)}) collective-permute-start(bf16[2,64,512]{2,1,0:T(8,128)(2,1)S(1)} %get-tuple-element.45), channel_id=1, source_target_pairs={{0,4},{1,5},{2,6},{3,7},{4,0},{5,1},{6,2},{7,3},{8,12},{9,13},{10,... | collective-permute-start | bytes 393224 | tf_op jit(solution)/shard_map/ppermute | solution.py:363
  40.8 1.8 %collective-permute-start.13 = (bf16[2,64,512]{2,1,0:T(8,128)(2,1)S(1)}, bf16[2,64,512]{2,1,0:T(8,128)(2,1)S(1)}, u32[]{:S(2)}, u32[]{:S(2)}) collective-permute-start(bf16[2,64,512]{2,1,0:T(8,128)(2,1)S(1)} %get-tuple-element.46), channel_id=1, source_target_pairs={{0,6},{1,7},{2,4},{3,5},{4,2},{5,3},{6,0},{7,1},{8,14},{9,15},{10,... | collective-permute-start | bytes 393224 | tf_op jit(solution)/shard_map/ppermute | solution.py:363
  42.6 14.1 %collective-permute-done.12.refs_6_ = bf16[2,64,512]{2,1,0:T(8,128)(2,1)S(1)} collective-permute-done((bf16[2,64,512]{2,1,0:T(8,128)(2,1)S(1)}, bf16[2,64,512]{2,1,0:T(8,128)(2,1)S(1)}, u32[]{:S(2)}, u32[]{:S(2)}) %collective-permute-start.12) | collective-permute-done | bytes 131104 | tf_op jit(solution)/shard_map/ppermute | solution.py:363
  56.7 0.8 shard_map.105
  57.5 0.1 collective-permute-start.14
  57.6 1.8 %collective-permute-start.4 = (bf16[2,16,4096]{2,1,0:T(8,128)(2,1)S(1)}, bf16[2,16,4096]{2,1,0:T(8,128)(2,1)S(1)}, u32[]{:S(2)}, u32[]{:S(2)}) collective-permute-start(bf16[2,16,4096]{2,1,0:T(8,128)(2,1)S(1)} %get-tuple-element.34), channel_id=1, source_target_pairs={{0,24},{8,0},{16,8},{24,16},{1,25},{9,1},{17,9},{25,17},{2,26},{10... | collective-permute-start | bytes 786440 | tf_op jit(solution)/shard_map/ppermute | solution.py:25
  59.5 0.2 collective-permute-start.6
  59.7 2.0 %collective-permute-start.7 = (bf16[2,16,4096]{2,1,0:T(8,128)(2,1)S(1)}, bf16[2,16,4096]{2,1,0:T(8,128)(2,1)S(1)}, u32[]{:S(2)}, u32[]{:S(2)}) collective-permute-start(bf16[2,16,4096]{2,1,0:T(8,128)(2,1)S(1)} %get-tuple-element.38), channel_id=1, source_target_pairs={{0,8},{8,16},{16,24},{24,0},{1,9},{9,17},{17,25},{25,1},{2,10},{10... | collective-permute-start | bytes 786440 | tf_op jit(solution)/shard_map/ppermute | solution.py:25
  61.7 4.9 %shard_map.102 = (bf16[64,4096]{1,0:T(8,128)(2,1)}, f32[64,4096]{1,0:T(8,128)S(1)}) custom-call(bf16[64,4096]{1,0:T(8,128)(2,1)S(1)} %collective-permute-done.x_ref, bf16[64,512]{1,0:T(8,128)(2,1)S(1)} %get-tuple-element.29.grouped_ref, bf16[4096,512]{1,0:T(8,128)(2,1)} %bitcast.20), custom_call_target="tpu_custom_call" | custom-call | flops 536870912 | bytes 6356992 | tf_op jit(solution)/shard_map/pallas_call | solution.py:34
  66.5 0.2 collective-permute-done.5.refs_0_
  66.8 0.8 finished.3.refs_1_
  67.6 15.5 %collective-permute-done.4.refs_0_ = bf16[2,16,4096]{2,1,0:T(8,128)(2,1)S(1)} collective-permute-done((bf16[2,16,4096]{2,1,0:T(8,128)(2,1)S(1)}, bf16[2,16,4096]{2,1,0:T(8,128)(2,1)S(1)}, u32[]{:S(2)}, u32[]{:S(2)}) %collective-permute-start.4) | collective-permute-done | bytes 262176 | tf_op jit(solution)/shard_map/ppermute | solution.py:25
  83.1 0.8 finished.4
  83.9 4.9 %shard_map.103 = (bf16[64,4096]{1,0:T(8,128)(2,1)}, f32[64,4096]{1,0:T(8,128)S(1)}) custom-call(bf16[64,4096]{1,0:T(8,128)(2,1)S(1)} %collective-permute-done.3.x_ref, bf16[64,512]{1,0:T(8,128)(2,1)S(1)} %get-tuple-element.31.grouped_ref, bf16[4096,512]{1,0:T(8,128)(2,1)} %bitcast.21), custom_call_target="tpu_custom_call" | custom-call | flops 536870912 | bytes 6356992 | tf_op jit(solution)/shard_map/pallas_call | solution.py:34
  88.8 0.9 %finished.5 = bf16[64,4096]{1,0:T(8,128)(2,1)} custom-call(s32[2,2,128]{2,1,0:T(2,128)S(1)} %broadcast_in_dim.30.match_up.match_ref, f32[64,4096]{1,0:T(8,128)S(1)} %get-tuple-element.36.through_ref, bf16[2,16,4096]{2,1,0:T(8,128)(2,1)S(1)} %collective-permute-done.6.refs_0_, bf16[2,16,4096]{2,1,0:T(8,128)(2,1)S(1)} %collective-permute-done.7.refs_1_), custom_call_target="tpu_custom_call" | custom-call | flops 524288 | bytes 2097152 | tf_op jit(solution)/shard_map/finished/pallas_call | solution.py:313
  89.8 1.0 %combine.1 = f32[512,512]{1,0:T(8,128)} custom-call(f32[512,512]{1,0:T(8,128)S(1)} %get-tuple-element.47.keep_ref, f32[512,512]{1,0:T(8,128)S(1)} %collective-permute-done.14.got_ref), custom_call_target="tpu_custom_call" | custom-call | flops 524288 | bytes 3145728 | tf_op jit(solution)/shard_map/combine/pallas_call | solution.py:205
  (17 shorter events, 0.2 us)
Async XLA Ops:
  0.6 1.0 %copy-start = (bf16[1,64,4096]{2,1,0:T(8,128)(2,1)S(1)}, bf16[1,64,4096]{2,1,0:T(8,128)(2,1)}, u32[]{:S(2)}) copy-start(bf16[1,64,4096]{2,1,0:T(8,128)(2,1)} %param.8) | copy-start | bytes 1572868
  1.7 1.0 %copy-start.1 = (bf16[1,64,4096]{2,1,0:T(8,128)(2,1)S(1)}, bf16[1,64,4096]{2,1,0:T(8,128)(2,1)}, u32[]{:S(2)}) copy-start(bf16[1,64,4096]{2,1,0:T(8,128)(2,1)} %param.9) | copy-start | bytes 1572868
  3.0 32.3 %collective-permute-start.1 = (bf16[64,512]{1,0:T(8,128)(2,1)S(1)}, bf16[64,512]{1,0:T(8,128)(2,1)S(1)}, u32[]{:S(2)}, u32[]{:S(2)}) collective-permute-start(bf16[64,512]{1,0:T(8,128)(2,1)S(1)} %get-tuple-element.27), channel_id=1, source_target_pairs={{0,24},{8,0},{16,8},{24,16},{1,25},{9,1},{17,9},{25,17},{2,26},{10... | collective-permute-start | bytes 196616 | tf_op jit(solution)/shard_map/ppermute | solution.py:25
  3.1 32.2 %collective-permute-start.2 = (bf16[64,512]{1,0:T(8,128)(2,1)S(1)}, bf16[64,512]{1,0:T(8,128)(2,1)S(1)}, u32[]{:S(2)}, u32[]{:S(2)}) collective-permute-start(bf16[64,512]{1,0:T(8,128)(2,1)S(1)} %get-tuple-element.28), channel_id=1, source_target_pairs={{0,8},{8,16},{16,24},{24,0},{1,9},{9,17},{17,25},{25,1},{2,10},{10... | collective-permute-start | bytes 196616 | tf_op jit(solution)/shard_map/ppermute | solution.py:25
  5.1 30.2 %collective-permute-start = (bf16[64,4096]{1,0:T(8,128)(2,1)}, bf16[64,4096]{1,0:T(8,128)(2,1)S(1)}, u32[]{:S(2)}, u32[]{:S(2)}) collective-permute-start(bf16[64,4096]{1,0:T(8,128)(2,1)} %bitcast.26), channel_id=1, source_target_pairs={{0,8},{8,16},{16,24},{24,0},{1,9},{9,17},{17,25},{25,1},{2,10},{10... | collective-permute-start | bytes 1572872 | tf_op jit(solution)/shard_map/ppermute | solution.py:25
  6.7 26.8 %collective-permute-start.3 = (bf16[64,4096]{1,0:T(8,128)(2,1)}, bf16[64,4096]{1,0:T(8,128)(2,1)S(1)}, u32[]{:S(2)}, u32[]{:S(2)}) collective-permute-start(bf16[64,4096]{1,0:T(8,128)(2,1)} %bitcast.25), channel_id=1, source_target_pairs={{0,24},{8,0},{16,8},{24,16},{1,25},{9,1},{17,9},{25,17},{2,26},{10... | collective-permute-start | bytes 1572872 | tf_op jit(solution)/shard_map/ppermute | solution.py:25
  33.7 7.1 %collective-permute-start.11 = (bf16[2,64,512]{2,1,0:T(8,128)(2,1)S(1)}, bf16[2,64,512]{2,1,0:T(8,128)(2,1)S(1)}, u32[]{:S(2)}, u32[]{:S(2)}) collective-permute-start(bf16[2,64,512]{2,1,0:T(8,128)(2,1)S(1)} %get-tuple-element.44), channel_id=1, source_target_pairs={{0,2},{1,3},{2,0},{3,1},{4,6},{5,7},{6,4},{7,5},{8,10},{9,11},{10,... | collective-permute-start | bytes 393224 | tf_op jit(solution)/shard_map/ppermute | solution.py:363
  35.7 21.0 %collective-permute-start.10 = (bf16[4,64,512]{2,1,0:T(8,128)(2,1)S(1)}, bf16[4,64,512]{2,1,0:T(8,128)(2,1)S(1)}, u32[]{:S(2)}, u32[]{:S(2)}) collective-permute-start(bf16[4,64,512]{2,1,0:T(8,128)(2,1)S(1)} %get-tuple-element.42), channel_id=1, source_target_pairs={{0,6},{1,7},{2,4},{3,5},{4,2},{5,3},{6,0},{7,1},{8,14},{9,15},{10,... | collective-permute-start | bytes 786440 | tf_op jit(solution)/shard_map/ppermute | solution.py:363
  37.2 19.5 %collective-permute-start.8 = (bf16[4,64,512]{2,1,0:T(8,128)(2,1)S(1)}, bf16[4,64,512]{2,1,0:T(8,128)(2,1)S(1)}, u32[]{:S(2)}, u32[]{:S(2)}) collective-permute-start(bf16[4,64,512]{2,1,0:T(8,128)(2,1)S(1)} %get-tuple-element.40), channel_id=1, source_target_pairs={{0,2},{1,3},{2,0},{3,1},{4,6},{5,7},{6,4},{7,5},{8,10},{9,11},{10,... | collective-permute-start | bytes 786440 | tf_op jit(solution)/shard_map/ppermute | solution.py:363
  38.7 18.0 %collective-permute-start.9 = (bf16[4,64,512]{2,1,0:T(8,128)(2,1)S(1)}, bf16[4,64,512]{2,1,0:T(8,128)(2,1)S(1)}, u32[]{:S(2)}, u32[]{:S(2)}) collective-permute-start(bf16[4,64,512]{2,1,0:T(8,128)(2,1)S(1)} %get-tuple-element.41), channel_id=1, source_target_pairs={{0,4},{1,5},{2,6},{3,7},{4,0},{5,1},{6,2},{7,3},{8,12},{9,13},{10,... | collective-permute-start | bytes 786440 | tf_op jit(solution)/shard_map/ppermute | solution.py:363
  39.2 17.5 %collective-permute-start.12 = (bf16[2,64,512]{2,1,0:T(8,128)(2,1)S(1)}, bf16[2,64,512]{2,1,0:T(8,128)(2,1)S(1)}, u32[]{:S(2)}, u32[]{:S(2)}) collective-permute-start(bf16[2,64,512]{2,1,0:T(8,128)(2,1)S(1)} %get-tuple-element.45), channel_id=1, source_target_pairs={{0,4},{1,5},{2,6},{3,7},{4,0},{5,1},{6,2},{7,3},{8,12},{9,13},{10,... | collective-permute-start | bytes 393224 | tf_op jit(solution)/shard_map/ppermute | solution.py:363
  40.8 15.9 %collective-permute-start.13 = (bf16[2,64,512]{2,1,0:T(8,128)(2,1)S(1)}, bf16[2,64,512]{2,1,0:T(8,128)(2,1)S(1)}, u32[]{:S(2)}, u32[]{:S(2)}) collective-permute-start(bf16[2,64,512]{2,1,0:T(8,128)(2,1)S(1)} %get-tuple-element.46), channel_id=1, source_target_pairs={{0,6},{1,7},{2,4},{3,5},{4,2},{5,3},{6,0},{7,1},{8,14},{9,15},{10,... | collective-permute-start | bytes 393224 | tf_op jit(solution)/shard_map/ppermute | solution.py:363
  57.5 32.3 %collective-permute-start.14 = (f32[512,512]{1,0:T(8,128)S(1)}, f32[512,512]{1,0:T(8,128)S(1)}, u32[]{:S(2)}, u32[]{:S(2)}) collective-permute-start(f32[512,512]{1,0:T(8,128)S(1)} %get-tuple-element.48), channel_id=1, source_target_pairs={{0,1},{1,0},{2,3},{3,2},{4,5},{5,4},{6,7},{7,6},{8,9},{9,8},{10,11... | collective-permute-start | bytes 3145736 | tf_op jit(solution)/shard_map/ppermute | solution.py:374
  57.6 9.2 %collective-permute-start.5 = (bf16[2,16,4096]{2,1,0:T(8,128)(2,1)S(1)}, bf16[2,16,4096]{2,1,0:T(8,128)(2,1)S(1)}, u32[]{:S(2)}, u32[]{:S(2)}) collective-permute-start(bf16[2,16,4096]{2,1,0:T(8,128)(2,1)S(1)} %get-tuple-element.35), channel_id=1, source_target_pairs={{0,24},{8,0},{16,8},{24,16},{1,25},{9,1},{17,9},{25,17},{2,26},{10... | collective-permute-start | bytes 786440 | tf_op jit(solution)/shard_map/ppermute | solution.py:25
  57.6 25.5 %collective-permute-start.4 = (bf16[2,16,4096]{2,1,0:T(8,128)(2,1)S(1)}, bf16[2,16,4096]{2,1,0:T(8,128)(2,1)S(1)}, u32[]{:S(2)}, u32[]{:S(2)}) collective-permute-start(bf16[2,16,4096]{2,1,0:T(8,128)(2,1)S(1)} %get-tuple-element.34), channel_id=1, source_target_pairs={{0,24},{8,0},{16,8},{24,16},{1,25},{9,1},{17,9},{25,17},{2,26},{10... | collective-permute-start | bytes 786440 | tf_op jit(solution)/shard_map/ppermute | solution.py:25
  59.5 29.4 %collective-permute-start.6 = (bf16[2,16,4096]{2,1,0:T(8,128)(2,1)S(1)}, bf16[2,16,4096]{2,1,0:T(8,128)(2,1)S(1)}, u32[]{:S(2)}, u32[]{:S(2)}) collective-permute-start(bf16[2,16,4096]{2,1,0:T(8,128)(2,1)S(1)} %get-tuple-element.37), channel_id=1, source_target_pairs={{0,8},{8,16},{16,24},{24,0},{1,9},{9,17},{17,25},{25,1},{2,10},{10... | collective-permute-start | bytes 786440 | tf_op jit(solution)/shard_map/ppermute | solution.py:25
  59.7 29.1 %collective-permute-start.7 = (bf16[2,16,4096]{2,1,0:T(8,128)(2,1)S(1)}, bf16[2,16,4096]{2,1,0:T(8,128)(2,1)S(1)}, u32[]{:S(2)}, u32[]{:S(2)}) collective-permute-start(bf16[2,16,4096]{2,1,0:T(8,128)(2,1)S(1)} %get-tuple-element.38), channel_id=1, source_target_pairs={{0,8},{8,16},{16,24},{24,0},{1,9},{9,17},{17,25},{25,1},{2,10},{10... | collective-permute-start | bytes 786440 | tf_op jit(solution)/shard_map/ppermute | solution.py:25

commit v4 on v3

--- a/solution.py
+++ b/solution.py
@@ -58,8 +58,7 @@
 
         @pl.when(part == own)
         def _():
-            halves[own][0] = down_ref[...]
-            halves[2 + own][0] = up_ref[...]
+            halves[own][0] = up_ref[...]
 
 
 def group_sums(down, up, blocks):
@@ -73,12 +72,12 @@
         group_kernel,
         grid=(blocks, 2),
         in_specs=[wide, wide],
-        out_specs=[narrow, narrow] + [half] * 4,
-        out_shape=[out, out] + [jax.ShapeDtypeStruct((blocks, step, width), down.dtype)] * 4,
+        out_specs=[narrow, narrow] + [half] * 2,
+        out_shape=[out, out] + [jax.ShapeDtypeStruct((blocks, step, width), down.dtype)] * 2,
         name="group_sums",
         compiler_params=pltpu.CompilerParams(vmem_limit_bytes=6 * MIB),
         cost_estimate=pl.CostEstimate(
-            flops=2 * rows * width, bytes_accessed=8 * rows * width, transcendentals=0
+            flops=2 * rows * width, bytes_accessed=6 * rows * width, transcendentals=0
         ),
     )(down, up)
 
@@ -194,20 +193,32 @@
     )
 
 
-def combine_kernel(factor, keep_ref, got_ref, out_ref):
-    out_ref[...] = (keep_ref[...] + got_ref[...]) * factor
+def combine_kernel(factor, keep_ref, got_ref, out_ref, held, sent):
+    slots, step, _ = held.shape
+    copies = []
+    for i in range(slots):
+        at = i * step
+        held[i] = (keep_ref[at : at + step, :] + got_ref[at : at + step, :]) * factor
+        copies.append(
+            pltpu.make_async_copy(held.at[i], out_ref.at[pl.ds(at, step), :], sent.at[i])
+        )
+        copies[-1].start()
+    for copy in copies:
+        copy.wait()
 
 
 def combined(keep, got, factor):
     rows, inner = keep.shape
-    step = rows // 2
-    part = pl.BlockSpec((step, inner), lambda i: (i, 0))
+    slots = 4
     return pl.pallas_call(
         functools.partial(combine_kernel, factor),
-        grid=(rows // step,),
-        in_specs=[part, part],
-        out_specs=part,
+        in_specs=[whole_vmem()] * 2,
+        out_specs=pl.BlockSpec(memory_space=pltpu.HBM),
         out_shape=jax.ShapeDtypeStruct(keep.shape, keep.dtype),
+        scratch_shapes=[
+            pltpu.VMEM((slots, rows // slots, inner), keep.dtype),
+            pltpu.SemaphoreType.DMA((slots,)),
+        ],
         name="combine",
         compiler_params=pltpu.CompilerParams(vmem_limit_bytes=4 * MIB),
         cost_estimate=pl.CostEstimate(
@@ -216,21 +227,44 @@
     )(keep, got)
 
 
-def span_kernel(x_ref, grouped_ref, weight_ref, next_ref, through_ref, scaled, back, held, arrived):
-    rows, width = x_ref.shape
-    tiles, tile, inner = held.shape
+def weight_copies(weight_ref, held, arrived):
+    tiles, tile, _ = held.shape
     copies = [
         pltpu.make_async_copy(weight_ref.at[pl.ds(t * tile, tile), :], held.at[t], arrived.at[t])
         for t in range(tiles)
     ]
     for copy in copies:
         copy.start()
+    return copies
+
+
+def write_span(x_ref, scaled, back, values, total, inverse, next_ref, through_ref):
+    rows, width = x_ref.shape
+    mean = jnp.sum(total, axis=-1, keepdims=True) * (1.0 / width)
+    mean = jnp.broadcast_to(mean, (rows, HD))
+    inverse = jnp.broadcast_to(inverse, (rows, HD))
+    for k in range(KVH):
+        spread = values[:, k * HD : (k + 1) * HD]
+        for j in range(GROUPS):
+            at = slice((k * GROUPS + j) * HD, (k * GROUPS + j + 1) * HD)
+            next_ref[:, at] = (x_ref[:, at].astype(jnp.float32) + spread).astype(next_ref.dtype)
+            through_ref[:, at] = inverse * (back[:, at] - scaled[:, at] * mean)
+
+
+def early_kernel(
+    x_ref, down_ref, up_ref, weight_ref,
+    next_ref, through_ref, back_ref,
+    scaled, back, held, arrived,
+):
+    rows, _ = x_ref.shape
+    tile, inner = held.shape[1:]
+    copies = weight_copies(weight_ref, held, arrived)
     x = x_ref[...].astype(jnp.float32)
     inverse = inverse_of(x)
     scaled[...] = x * inverse
     values = jnp.zeros((rows, inner), jnp.float32)
     total = jnp.zeros((rows, HD), jnp.float32)
-    grouped = grouped_ref[...]
+    grouped = jnp.concatenate([down_ref[...], up_ref[...]], axis=0)
     for t, copy in enumerate(copies):
         copy.wait()
         weight = held[t]
@@ -240,55 +274,68 @@
         part = lax.dot_general(
             grouped, weight, (((1,), (1,)), ((), ())), preferred_element_type=jnp.float32
         )
-        back[:, at] = part
+        back[:, at] = part[:rows]
+        back_ref[:, at] = part[rows:]
         for c in range(tile // HD):
             lanes = slice(c * HD, (c + 1) * HD)
-            total = total + part[:, lanes] * scaled[:, t * tile + c * HD : t * tile + (c + 1) * HD]
-    mean = jnp.sum(total, axis=-1, keepdims=True) * (1.0 / width)
-    mean = jnp.broadcast_to(mean, (rows, HD))
-    inverse = jnp.broadcast_to(inverse, (rows, HD))
-    for k in range(KVH):
-        spread = values[:, k * HD : (k + 1) * HD]
-        for j in range(GROUPS):
-            at = slice((k * GROUPS + j) * HD, (k * GROUPS + j + 1) * HD)
-            next_ref[:, at] = (x_ref[:, at].astype(jnp.float32) + spread).astype(next_ref.dtype)
-            through_ref[:, at] = inverse * (back[:, at] - scaled[:, at] * mean)
-
-
-def span(x, grouped, weight):
-    rows, width = x.shape
+            both = slice(t * tile + c * HD, t * tile + (c + 1) * HD)
+            total = total + part[:rows, lanes] * scaled[:, both]
+    write_span(x_ref, scaled, back, values, total, inverse, next_ref, through_ref)
+
+
+def late_kernel(x_ref, back_ref, weight_ref, next_ref, through_ref, scaled, held, arrived):
+    rows, _ = x_ref.shape
+    tile, inner = held.shape[1:]
+    copies = weight_copies(weight_ref, held, arrived)
+    x = x_ref[...].astype(jnp.float32)
+    inverse = inverse_of(x)
+    scaled[...] = x * inverse
+    values = jnp.zeros((rows, inner), jnp.float32)
+    total = jnp.zeros((rows, HD), jnp.float32)
+    for t, copy in enumerate(copies):
+        copy.wait()
+        at = slice(t * tile, (t + 1) * tile)
+        normed = scaled[:, at].astype(x_ref.dtype)
+        values = values + jnp.dot(normed, held[t], preferred_element_type=jnp.float32)
+        for c in range(tile // HD):
+            both = slice(t * tile + c * HD, t * tile + (c + 1) * HD)
+            total = total + back_ref[:, both] * scaled[:, both]
+    write_span(x_ref, scaled, back_ref, values, total, inverse, next_ref, through_ref)
+
+
+def span(kernel, operands, weight, outputs, held, passes):
+    rows, width = operands[0].shape
     inner = weight.shape[1]
     tile = math.gcd(width, 512)
+    wide = jax.ShapeDtypeStruct((rows, width), jnp.float32)
     return called(
-        span_kernel,
-        (x, grouped, pltpu.with_memory_space_constraint(weight, pltpu.HBM)),
-        [
-            jax.ShapeDtypeStruct((rows, width), x.dtype),
-            jax.ShapeDtypeStruct((rows, width), jnp.float32),
-        ],
-        scratch=[
-            pltpu.VMEM((rows, width), jnp.float32),
-            pltpu.VMEM((rows, width), jnp.float32),
+        kernel,
+        (*operands, pltpu.with_memory_space_constraint(weight, pltpu.HBM)),
+        [jax.ShapeDtypeStruct((rows, width), operands[0].dtype)] + [wide] * outputs,
+        scratch=[pltpu.VMEM((rows, width), jnp.float32)] * held
+        + [
             pltpu.VMEM((width // tile, tile, inner), weight.dtype),
             pltpu.SemaphoreType.DMA((width // tile,)),
         ],
-        flops=4 * rows * width * inner,
+        flops=2 * passes * rows * width * inner,
         vmem=10,
-        in_specs=[whole_vmem()] * 2 + [pl.BlockSpec(memory_space=pltpu.HBM)],
+        in_specs=[whole_vmem()] * len(operands) + [pl.BlockSpec(memory_space=pltpu.HBM)],
     )
 
 
 def finish_kernel(parts, match_ref, through_ref, *refs):
-    raws = refs[: len(parts)]
+    raw = refs[0]
     out_ref, held, sent = refs[-3:]
-    blocks, half, _ = raws[0].shape
+    blocks = raw.shape[0]
+    half = raw.shape[1] // len(parts)
     copies = []
-    for i, (part, raw) in enumerate(zip(parts, raws)):
+    for i, part in enumerate(parts):
+        inside = slice(i * half, (i + 1) * half)
         for m in range(blocks):
-            chosen = raw[0].astype(jnp.float32)
+            chosen = raw[0, inside, :].astype(jnp.float32)
             for j in range(1, blocks):
                 mine = match_ref[m, j : j + 1, 0:1] != 0
-                chosen = jnp.where(mine, raw[j].astype(jnp.float32), chosen)
+                chosen = jnp.where(mine, raw[j, inside, :].astype(jnp.float32), chosen)
             at = (2 * m + part) * half
             slot = i * blocks + m
             held[slot] = (chosen + through_ref[at : at + half, :]).astype(held.dtype)
@@ -302,21 +349,22 @@
         copy.wait()
 
 
-def finished(raws, parts, match, through, before=None):
+def finished(raw, parts, match, through, before=None):
     rows, width = through.shape
-    blocks, half, _ = raws[0].shape
+    blocks = raw.shape[0]
+    half = raw.shape[1] // len(parts)
     slots = blocks * len(parts)
-    operands = [match, through, *raws] + ([] if before is None else [before])
-    specs = [whole_vmem()] * (2 + len(raws))
+    operands = [match, through, raw] + ([] if before is None else [before])
+    specs = [whole_vmem()] * 3
     if before is not None:
         specs.append(pl.BlockSpec(memory_space=pltpu.HBM))
     return pl.pallas_call(
         functools.partial(finish_kernel, parts),
         in_specs=specs,
         out_specs=pl.BlockSpec(memory_space=pltpu.HBM),
-        out_shape=jax.ShapeDtypeStruct((rows, width), raws[0].dtype),
+        out_shape=jax.ShapeDtypeStruct((rows, width), raw.dtype),
         scratch_shapes=[
-            pltpu.VMEM((slots, half, width), raws[0].dtype),
+            pltpu.VMEM((slots, half, width), raw.dtype),
             pltpu.SemaphoreType.DMA((slots,)),
         ],
         input_output_aliases={} if before is None else {len(operands) - 1: 0},
@@ -353,8 +401,8 @@
     sums_up = passed_along(sums_up, "section", 1)
     sums_down = passed_along(sums_down, "section", -1)
     x_up = passed_along(feed_up[0], "section", -1)
-    raw_down = [passed_along(half, "section", -1) for half in halves[:2]]
-    raw_up = [passed_along(half, "section", 1) for half in halves[2:]]
+    raw_up = [passed_along(half, "section", 1) for half in halves]
+    raw_down = passed_along(cotangent_down[0], "section", -1)
 
     def exchanged(pieces):
         got = [pieces[0]]
@@ -367,16 +415,20 @@
     got_down = exchanged(sent_down)
     got_up = exchanged(pieces_up(x_up, inner, members))
 
-    next_down, through_down = span(x_down, grouped_down, weight)
-    next_up, through_up = span(x_up, grouped_up, weight)
+    next_down, through_down, back_norm = span(
+        early_kernel, (x_down, grouped_down, grouped_up), weight, 2, 2, 3
+    )
+    next_up, through_up = span(late_kernel, (x_up, back_norm), weight, 1, 1, 1)
 
     keep, send = products(got_down, got_up, width, inner, members)
     got = lax.ppermute(send, "dp", [(i, i ^ 1) for i in range(members)])
     summed = combined(keep, got, float(2 * rows * members) ** (-0.5))
 
-    back_up = finished(raw_up, (0, 1), match_up, through_up)
-    part_down = finished(raw_down[:1], (0,), match_down, through_down)
-    back_down = finished(raw_down[1:], (1,), match_down, through_down, before=part_down)
+    blocks = roster.shape[2]
+    raw_down = raw_down.reshape(blocks, rows // blocks, width)
+    back_down = finished(raw_down, (0, 1), match_down, through_down)
+    part_up = finished(raw_up[0], (0,), match_up, through_up)
+    back_up = finished(raw_up[1], (1,), match_up, through_up, before=part_up)
     return (
         next_down[None],
         next_up[None],

time: 91.1 us -> 81 us (0.89)
  the two profiles are of different devices: /device:TPU:8 before, /device:TPU:0 now
where the time goes in v4:
time: 81 us; the launch traced here: 80.8 us
  waiting for transfers between devices  44.9 us (55%)
  starting transfers between devices  18.6 us (23%)
  Pallas kernels  13.5 us (17%)
  local copies, waits for them, and re-layouts  2.98 us (4%)
    ppermute x7, waiting for transfers between devices, passed_along(): lax.ppermute(shard, axis, [(i, (i + by) % count) for i in range(count)])  32 us
    ppermute x6, waiting for transfers between devices, exchanged(): got.append(lax.ppermute(pieces[c], 'dp', to))  13 us
    ppermute x7, starting transfers between devices, passed_along(): lax.ppermute(shard, axis, [(i, (i + by) % count) for i in range(count)])  10.4 us
    pallas_call x5, Pallas kernels, called(): pl.pallas_call(kernel, in_specs=more.get('in_specs', [whole_vmem()] * len...  9.7 us
    ppermute x6, starting transfers between devices, exchanged(): got.append(lax.ppermute(pieces[c], 'dp', to))  8.06 us
    pallas_call x3, Pallas kernels, finished(): pl.pallas_call(functools.partial(finish_kernel, parts), in_specs=specs, o...  2.54 us
    unnamed x6, local copies, waits for them, and re-layouts  2.09 us
  transfers between devices with their start and end apart: 14, of which 5 were waited for; matrix products, arithmetic and copies ran while one was open for 1% of the time, Pallas kernels for 15%

profile of v4, /device:TPU:0, one launch (start us, length us, event | category | flops | bytes accessed | tf_op | source)
XLA Modules:
  0.0 80.8 jit_solution(18035013439012688707)
XLA Ops:
  0.6 3.1 %collective-permute-start = (bf16[64,4096]{1,0:T(8,128)(2,1)}, bf16[64,4096]{1,0:T(8,128)(2,1)S(1)}, u32[]{:S(2)}, u32[]{:S(2)}) collective-permute-start(bf16[64,4096]{1,0:T(8,128)(2,1)} %bitcast.29), channel_id=1, source_target_pairs={{0,8},{8,16},{16,24},{24,0},{1,9},{9,17},{17,25},{25,1},{2,10},{10... | collective-permute-start | bytes 1572872 | tf_op jit(solution)/shard_map/ppermute | solution.py:25
  3.7 2.1 %collective-permute-start.3 = (bf16[64,4096]{1,0:T(8,128)(2,1)}, bf16[64,4096]{1,0:T(8,128)(2,1)S(1)}, u32[]{:S(2)}, u32[]{:S(2)}) collective-permute-start(bf16[64,4096]{1,0:T(8,128)(2,1)} %bitcast.28), channel_id=1, source_target_pairs={{0,24},{8,0},{16,8},{24,16},{1,25},{9,1},{17,9},{25,17},{2,26},{10... | collective-permute-start | bytes 1572872 | tf_op jit(solution)/shard_map/ppermute | solution.py:25
  5.8 1.0 %copy-done = bf16[1,64,4096]{2,1,0:T(8,128)(2,1)S(1)} copy-done((bf16[1,64,4096]{2,1,0:T(8,128)(2,1)S(1)}, bf16[1,64,4096]{2,1,0:T(8,128)(2,1)}, u32[]{:S(2)}) %copy-start) | copy-done | bytes 524312
  6.9 1.0 %copy-done.1 = bf16[1,64,4096]{2,1,0:T(8,128)(2,1)S(1)} copy-done((bf16[1,64,4096]{2,1,0:T(8,128)(2,1)S(1)}, bf16[1,64,4096]{2,1,0:T(8,128)(2,1)}, u32[]{:S(2)}) %copy-start.1) | copy-done | bytes 524312
  7.9 0.2 group_sums.1
  8.2 2.0 %collective-permute-start.1 = (bf16[64,512]{1,0:T(8,128)(2,1)S(1)}, bf16[64,512]{1,0:T(8,128)(2,1)S(1)}, u32[]{:S(2)}, u32[]{:S(2)}) collective-permute-start(bf16[64,512]{1,0:T(8,128)(2,1)S(1)} %get-tuple-element.26), channel_id=1, source_target_pairs={{0,24},{8,0},{16,8},{24,16},{1,25},{9,1},{17,9},{25,17},{2,26},{10... | collective-permute-start | bytes 196616 | tf_op jit(solution)/shard_map/ppermute | solution.py:25
  10.2 0.8 slice_bitcast_fusion
  11.0 18.2 %collective-permute-done.3.x_ref = bf16[64,4096]{1,0:T(8,128)(2,1)S(1)} collective-permute-done((bf16[64,4096]{1,0:T(8,128)(2,1)}, bf16[64,4096]{1,0:T(8,128)(2,1)S(1)}, u32[]{:S(2)}, u32[]{:S(2)}) %collective-permute-start.3) | collective-permute-done | bytes 524320 | tf_op jit(solution)/shard_map/ppermute | solution.py:25
  29.2 0.2 shard_map.104
  29.5 1.6 %collective-permute-start.10 = (bf16[2,64,512]{2,1,0:T(8,128)(2,1)S(1)}, bf16[2,64,512]{2,1,0:T(8,128)(2,1)S(1)}, u32[]{:S(2)}, u32[]{:S(2)}) collective-permute-start(bf16[2,64,512]{2,1,0:T(8,128)(2,1)S(1)} %get-tuple-element.42), channel_id=1, source_target_pairs={{0,2},{1,3},{2,0},{3,1},{4,6},{5,7},{6,4},{7,5},{8,10},{9,11},{10,... | collective-permute-start | bytes 393224 | tf_op jit(solution)/shard_map/ppermute | solution.py:411
  31.0 1.0 %collective-permute-done.2 = bf16[64,512]{1,0:T(8,128)(2,1)S(1)} collective-permute-done((bf16[64,512]{1,0:T(8,128)(2,1)S(1)}, bf16[64,512]{1,0:T(8,128)(2,1)S(1)}, u32[]{:S(2)}, u32[]{:S(2)}) %collective-permute-start.2) | collective-permute-done | bytes 65568 | tf_op jit(solution)/shard_map/ppermute | solution.py:25
  32.0 0.1 broadcast_in_dim.30.match_up.match_ref
  32.1 0.3 shard_map.101
  32.4 1.6 %collective-permute-start.7 = (bf16[4,64,512]{2,1,0:T(8,128)(2,1)S(1)}, bf16[4,64,512]{2,1,0:T(8,128)(2,1)S(1)}, u32[]{:S(2)}, u32[]{:S(2)}) collective-permute-start(bf16[4,64,512]{2,1,0:T(8,128)(2,1)S(1)} %get-tuple-element.38), channel_id=1, source_target_pairs={{0,2},{1,3},{2,0},{3,1},{4,6},{5,7},{6,4},{7,5},{8,10},{9,11},{10,... | collective-permute-start | bytes 786440 | tf_op jit(solution)/shard_map/ppermute | solution.py:411
  34.0 1.5 %collective-permute-start.8 = (bf16[4,64,512]{2,1,0:T(8,128)(2,1)S(1)}, bf16[4,64,512]{2,1,0:T(8,128)(2,1)S(1)}, u32[]{:S(2)}, u32[]{:S(2)}) collective-permute-start(bf16[4,64,512]{2,1,0:T(8,128)(2,1)S(1)} %get-tuple-element.39), channel_id=1, source_target_pairs={{0,4},{1,5},{2,6},{3,7},{4,0},{5,1},{6,2},{7,3},{8,12},{9,13},{10,... | collective-permute-start | bytes 786440 | tf_op jit(solution)/shard_map/ppermute | solution.py:411
  35.5 0.5 collective-permute-start.9
  36.0 1.5 %collective-permute-start.11 = (bf16[2,64,512]{2,1,0:T(8,128)(2,1)S(1)}, bf16[2,64,512]{2,1,0:T(8,128)(2,1)S(1)}, u32[]{:S(2)}, u32[]{:S(2)}) collective-permute-start(bf16[2,64,512]{2,1,0:T(8,128)(2,1)S(1)} %get-tuple-element.43), channel_id=1, source_target_pairs={{0,4},{1,5},{2,6},{3,7},{4,0},{5,1},{6,2},{7,3},{8,12},{9,13},{10,... | collective-permute-start | bytes 393224 | tf_op jit(solution)/shard_map/ppermute | solution.py:411
  37.5 1.4 %collective-permute-start.12 = (bf16[2,64,512]{2,1,0:T(8,128)(2,1)S(1)}, bf16[2,64,512]{2,1,0:T(8,128)(2,1)S(1)}, u32[]{:S(2)}, u32[]{:S(2)}) collective-permute-start(bf16[2,64,512]{2,1,0:T(8,128)(2,1)S(1)} %get-tuple-element.44), channel_id=1, source_target_pairs={{0,6},{1,7},{2,4},{3,5},{4,2},{5,3},{6,0},{7,1},{8,14},{9,15},{10,... | collective-permute-start | bytes 393224 | tf_op jit(solution)/shard_map/ppermute | solution.py:411
  38.9 13.0 %collective-permute-done.11.refs_6_ = bf16[2,64,512]{2,1,0:T(8,128)(2,1)S(1)} collective-permute-done((bf16[2,64,512]{2,1,0:T(8,128)(2,1)S(1)}, bf16[2,64,512]{2,1,0:T(8,128)(2,1)S(1)}, u32[]{:S(2)}, u32[]{:S(2)}) %collective-permute-start.11) | collective-permute-done | bytes 131104 | tf_op jit(solution)/shard_map/ppermute | solution.py:411
  51.9 0.8 shard_map.105
  52.7 0.1 collective-permute-start.13
  52.8 1.3 %collective-permute-start.4 = (bf16[64,4096]{1,0:T(8,128)(2,1)S(1)}, bf16[64,4096]{1,0:T(8,128)(2,1)S(1)}, u32[]{:S(2)}, u32[]{:S(2)}) collective-permute-start(bf16[64,4096]{1,0:T(8,128)(2,1)S(1)} %bitcast.20), channel_id=1, source_target_pairs={{0,24},{8,0},{16,8},{24,16},{1,25},{9,1},{17,9},{25,17},{2,26},{10... | collective-permute-start | bytes 1572872 | tf_op jit(solution)/shard_map/ppermute | solution.py:25
  54.0 0.8 collective-permute-start.6
  54.8 1.1 %collective-permute-start.5 = (bf16[2,16,4096]{2,1,0:T(8,128)(2,1)S(1)}, bf16[2,16,4096]{2,1,0:T(8,128)(2,1)S(1)}, u32[]{:S(2)}, u32[]{:S(2)}) collective-permute-start(bf16[2,16,4096]{2,1,0:T(8,128)(2,1)S(1)} %get-tuple-element.35), channel_id=1, source_target_pairs={{0,8},{8,16},{16,24},{24,0},{1,9},{9,17},{17,25},{25,1},{2,10},{10... | collective-permute-start | bytes 786440 | tf_op jit(solution)/shard_map/ppermute | solution.py:25
  55.9 5.0 %shard_map.102 = (bf16[64,4096]{1,0:T(8,128)(2,1)}, f32[64,4096]{1,0:T(8,128)S(1)}, f32[64,4096]{1,0:T(8,128)S(1)}) custom-call(bf16[64,4096]{1,0:T(8,128)(2,1)S(1)} %collective-permute-done.x_ref, bf16[64,512]{1,0:T(8,128)(2,1)S(1)} %get-tuple-element.28.down_ref, bf16[64,512]{1,0:T(8,128)(2,1)S(1)} %get-tuple-element.29.up_ref, bf16[4096,512]{1,0:T(8,128)(2,1)} %bitcast.23), custom_call_target="tpu_custom_call" | custom-call | flops 805306368 | bytes 7471104 | tf_op jit(solution)/shard_map/pallas_call | solution.py:34
  61.0 3.4 %shard_map.103 = (bf16[64,4096]{1,0:T(8,128)(2,1)}, f32[64,4096]{1,0:T(8,128)S(1)}) custom-call(bf16[64,4096]{1,0:T(8,128)(2,1)S(1)} %collective-permute-done.3.x_ref, f32[64,4096]{1,0:T(8,128)S(1)} %get-tuple-element.31.back_ref, bf16[4096,512]{1,0:T(8,128)(2,1)} %bitcast.24), custom_call_target="tpu_custom_call" | custom-call | flops 268435456 | bytes 7340032 | tf_op jit(solution)/shard_map/pallas_call | solution.py:34
  64.4 8.5 %collective-permute-done.6.refs_0_ = bf16[2,16,4096]{2,1,0:T(8,128)(2,1)S(1)} collective-permute-done((bf16[2,16,4096]{2,1,0:T(8,128)(2,1)S(1)}, bf16[2,16,4096]{2,1,0:T(8,128)(2,1)S(1)}, u32[]{:S(2)}, u32[]{:S(2)}) %collective-permute-start.6) | collective-permute-done | bytes 262176 | tf_op jit(solution)/shard_map/ppermute | solution.py:25
  72.9 0.8 finished.4.refs_1_
  73.7 4.3 %collective-permute-done.5.refs_0_ = bf16[2,16,4096]{2,1,0:T(8,128)(2,1)S(1)} collective-permute-done((bf16[2,16,4096]{2,1,0:T(8,128)(2,1)S(1)}, bf16[2,16,4096]{2,1,0:T(8,128)(2,1)S(1)}, u32[]{:S(2)}, u32[]{:S(2)}) %collective-permute-start.5) | collective-permute-done | bytes 262176 | tf_op jit(solution)/shard_map/ppermute | solution.py:25
  78.0 0.8 finished.5
  78.8 0.9 %finished.3 = bf16[64,4096]{1,0:T(8,128)(2,1)} custom-call(s32[2,2,128]{2,1,0:T(2,128)S(1)} %broadcast_in_dim.14.match_down.match_ref, f32[64,4096]{1,0:T(8,128)S(1)} %get-tuple-element.33.through_ref, bf16[2,32,4096]{2,1,0:T(8,128)(2,1)S(1)} %bitcast.17), custom_call_target="tpu_custom_call" | custom-call | flops 524288 | bytes 2097152 | tf_op jit(solution)/shard_map/finished/pallas_call | solution.py:361
  79.7 1.0 %combine.1 = f32[512,512]{1,0:T(8,128)} custom-call(f32[512,512]{1,0:T(8,128)S(1)} %get-tuple-element.45.keep_ref, f32[512,512]{1,0:T(8,128)S(1)} %collective-permute-done.13.got_ref), custom_call_target="tpu_custom_call" | custom-call | flops 524288 | bytes 3145728 | tf_op jit(solution)/shard_map/combine/pallas_call | solution.py:213
  (17 shorter events, 0.2 us)
Async XLA Ops:
  0.6 31.4 %collective-permute-start = (bf16[64,4096]{1,0:T(8,128)(2,1)}, bf16[64,4096]{1,0:T(8,128)(2,1)S(1)}, u32[]{:S(2)}, u32[]{:S(2)}) collective-permute-start(bf16[64,4096]{1,0:T(8,128)(2,1)} %bitcast.29), channel_id=1, source_target_pairs={{0,8},{8,16},{16,24},{24,0},{1,9},{9,17},{17,25},{25,1},{2,10},{10... | collective-permute-start | bytes 1572872 | tf_op jit(solution)/shard_map/ppermute | solution.py:25
  3.7 25.5 %collective-permute-start.3 = (bf16[64,4096]{1,0:T(8,128)(2,1)}, bf16[64,4096]{1,0:T(8,128)(2,1)S(1)}, u32[]{:S(2)}, u32[]{:S(2)}) collective-permute-start(bf16[64,4096]{1,0:T(8,128)(2,1)} %bitcast.28), channel_id=1, source_target_pairs={{0,24},{8,0},{16,8},{24,16},{1,25},{9,1},{17,9},{25,17},{2,26},{10... | collective-permute-start | bytes 1572872 | tf_op jit(solution)/shard_map/ppermute | solution.py:25
  5.8 1.0 %copy-start = (bf16[1,64,4096]{2,1,0:T(8,128)(2,1)S(1)}, bf16[1,64,4096]{2,1,0:T(8,128)(2,1)}, u32[]{:S(2)}) copy-start(bf16[1,64,4096]{2,1,0:T(8,128)(2,1)} %param.9) | copy-start | bytes 1572868
  6.9 1.0 %copy-start.1 = (bf16[1,64,4096]{2,1,0:T(8,128)(2,1)S(1)}, bf16[1,64,4096]{2,1,0:T(8,128)(2,1)}, u32[]{:S(2)}) copy-start(bf16[1,64,4096]{2,1,0:T(8,128)(2,1)} %param.8) | copy-start | bytes 1572868
  7.9 44.8 %copy-start.2 = (bf16[1,64,4096]{2,1,0:T(8,128)(2,1)S(1)}, bf16[1,64,4096]{2,1,0:T(8,128)(2,1)}, u32[]{:S(2)}) copy-start(bf16[1,64,4096]{2,1,0:T(8,128)(2,1)} %param.8) | copy-start | bytes 1572868
  8.2 22.9 %collective-permute-start.1 = (bf16[64,512]{1,0:T(8,128)(2,1)S(1)}, bf16[64,512]{1,0:T(8,128)(2,1)S(1)}, u32[]{:S(2)}, u32[]{:S(2)}) collective-permute-start(bf16[64,512]{1,0:T(8,128)(2,1)S(1)} %get-tuple-element.26), channel_id=1, source_target_pairs={{0,24},{8,0},{16,8},{24,16},{1,25},{9,1},{17,9},{25,17},{2,26},{10... | collective-permute-start | bytes 196616 | tf_op jit(solution)/shard_map/ppermute | solution.py:25
  10.2 21.8 %collective-permute-start.2 = (bf16[64,512]{1,0:T(8,128)(2,1)S(1)}, bf16[64,512]{1,0:T(8,128)(2,1)S(1)}, u32[]{:S(2)}, u32[]{:S(2)}) collective-permute-start(bf16[64,512]{1,0:T(8,128)(2,1)S(1)} %get-tuple-element.27), channel_id=1, source_target_pairs={{0,8},{8,16},{16,24},{24,0},{1,9},{9,17},{17,25},{25,1},{2,10},{10... | collective-permute-start | bytes 196616 | tf_op jit(solution)/shard_map/ppermute | solution.py:25
  29.5 8.0 %collective-permute-start.10 = (bf16[2,64,512]{2,1,0:T(8,128)(2,1)S(1)}, bf16[2,64,512]{2,1,0:T(8,128)(2,1)S(1)}, u32[]{:S(2)}, u32[]{:S(2)}) collective-permute-start(bf16[2,64,512]{2,1,0:T(8,128)(2,1)S(1)} %get-tuple-element.42), channel_id=1, source_target_pairs={{0,2},{1,3},{2,0},{3,1},{4,6},{5,7},{6,4},{7,5},{8,10},{9,11},{10,... | collective-permute-start | bytes 393224 | tf_op jit(solution)/shard_map/ppermute | solution.py:411
  32.4 19.5 %collective-permute-start.7 = (bf16[4,64,512]{2,1,0:T(8,128)(2,1)S(1)}, bf16[4,64,512]{2,1,0:T(8,128)(2,1)S(1)}, u32[]{:S(2)}, u32[]{:S(2)}) collective-permute-start(bf16[4,64,512]{2,1,0:T(8,128)(2,1)S(1)} %get-tuple-element.38), channel_id=1, source_target_pairs={{0,2},{1,3},{2,0},{3,1},{4,6},{5,7},{6,4},{7,5},{8,10},{9,11},{10,... | collective-permute-start | bytes 786440 | tf_op jit(solution)/shard_map/ppermute | solution.py:411
  34.0 17.9 %collective-permute-start.8 = (bf16[4,64,512]{2,1,0:T(8,128)(2,1)S(1)}, bf16[4,64,512]{2,1,0:T(8,128)(2,1)S(1)}, u32[]{:S(2)}, u32[]{:S(2)}) collective-permute-start(bf16[4,64,512]{2,1,0:T(8,128)(2,1)S(1)} %get-tuple-element.39), channel_id=1, source_target_pairs={{0,4},{1,5},{2,6},{3,7},{4,0},{5,1},{6,2},{7,3},{8,12},{9,13},{10,... | collective-permute-start | bytes 786440 | tf_op jit(solution)/shard_map/ppermute | solution.py:411
  35.5 16.4 %collective-permute-start.9 = (bf16[4,64,512]{2,1,0:T(8,128)(2,1)S(1)}, bf16[4,64,512]{2,1,0:T(8,128)(2,1)S(1)}, u32[]{:S(2)}, u32[]{:S(2)}) collective-permute-start(bf16[4,64,512]{2,1,0:T(8,128)(2,1)S(1)} %get-tuple-element.40), channel_id=1, source_target_pairs={{0,6},{1,7},{2,4},{3,5},{4,2},{5,3},{6,0},{7,1},{8,14},{9,15},{10,... | collective-permute-start | bytes 786440 | tf_op jit(solution)/shard_map/ppermute | solution.py:411
  36.0 15.9 %collective-permute-start.11 = (bf16[2,64,512]{2,1,0:T(8,128)(2,1)S(1)}, bf16[2,64,512]{2,1,0:T(8,128)(2,1)S(1)}, u32[]{:S(2)}, u32[]{:S(2)}) collective-permute-start(bf16[2,64,512]{2,1,0:T(8,128)(2,1)S(1)} %get-tuple-element.43), channel_id=1, source_target_pairs={{0,4},{1,5},{2,6},{3,7},{4,0},{5,1},{6,2},{7,3},{8,12},{9,13},{10,... | collective-permute-start | bytes 393224 | tf_op jit(solution)/shard_map/ppermute | solution.py:411
  37.5 14.4 %collective-permute-start.12 = (bf16[2,64,512]{2,1,0:T(8,128)(2,1)S(1)}, bf16[2,64,512]{2,1,0:T(8,128)(2,1)S(1)}, u32[]{:S(2)}, u32[]{:S(2)}) collective-permute-start(bf16[2,64,512]{2,1,0:T(8,128)(2,1)S(1)} %get-tuple-element.44), channel_id=1, source_target_pairs={{0,6},{1,7},{2,4},{3,5},{4,2},{5,3},{6,0},{7,1},{8,14},{9,15},{10,... | collective-permute-start | bytes 393224 | tf_op jit(solution)/shard_map/ppermute | solution.py:411
  52.7 27.1 %collective-permute-start.13 = (f32[512,512]{1,0:T(8,128)S(1)}, f32[512,512]{1,0:T(8,128)S(1)}, u32[]{:S(2)}, u32[]{:S(2)}) collective-permute-start(f32[512,512]{1,0:T(8,128)S(1)} %get-tuple-element.46), channel_id=1, source_target_pairs={{0,1},{1,0},{2,3},{3,2},{4,5},{5,4},{6,7},{7,6},{8,9},{9,8},{10,11... | collective-permute-start | bytes 3145736 | tf_op jit(solution)/shard_map/ppermute | solution.py:424
  52.8 26.0 %collective-permute-start.4 = (bf16[64,4096]{1,0:T(8,128)(2,1)S(1)}, bf16[64,4096]{1,0:T(8,128)(2,1)S(1)}, u32[]{:S(2)}, u32[]{:S(2)}) collective-permute-start(bf16[64,4096]{1,0:T(8,128)(2,1)S(1)} %bitcast.20), channel_id=1, source_target_pairs={{0,24},{8,0},{16,8},{24,16},{1,25},{9,1},{17,9},{25,17},{2,26},{10... | collective-permute-start | bytes 1572872 | tf_op jit(solution)/shard_map/ppermute | solution.py:25
  54.0 18.8 %collective-permute-start.6 = (bf16[2,16,4096]{2,1,0:T(8,128)(2,1)S(1)}, bf16[2,16,4096]{2,1,0:T(8,128)(2,1)S(1)}, u32[]{:S(2)}, u32[]{:S(2)}) collective-permute-start(bf16[2,16,4096]{2,1,0:T(8,128)(2,1)S(1)} %get-tuple-element.36), channel_id=1, source_target_pairs={{0,8},{8,16},{16,24},{24,0},{1,9},{9,17},{17,25},{25,1},{2,10},{10... | collective-permute-start | bytes 786440 | tf_op jit(solution)/shard_map/ppermute | solution.py:25
  54.8 23.1 %collective-permute-start.5 = (bf16[2,16,4096]{2,1,0:T(8,128)(2,1)S(1)}, bf16[2,16,4096]{2,1,0:T(8,128)(2,1)S(1)}, u32[]{:S(2)}, u32[]{:S(2)}) collective-permute-start(bf16[2,16,4096]{2,1,0:T(8,128)(2,1)S(1)} %get-tuple-element.35), channel_id=1, source_target_pairs={{0,8},{8,16},{16,24},{24,0},{1,9},{9,17},{17,25},{25,1},{2,10},{10... | collective-permute-start | bytes 786440 | tf_op jit(solution)/shard_map/ppermute | solution.py:25

commit v5 on v4

--- a/solution.py
+++ b/solution.py
@@ -44,9 +44,9 @@
     )(*operands)
 
 
-def group_kernel(down_ref, up_ref, down_out, up_out, *halves):
+def group_kernel(early_ref, late_ref, early_out, late_out, *halves):
     part = pl.program_id(1)
-    for src, dst in ((down_ref, down_out), (up_ref, up_out)):
+    for src, dst in ((early_ref, early_out), (late_ref, late_out)):
         for k in range(KVH):
             total = src[:, k * GROUPS * HD : (k * GROUPS + 1) * HD].astype(jnp.float32)
             for j in range(1, GROUPS):
@@ -58,28 +58,28 @@
 
         @pl.when(part == own)
         def _():
-            halves[own][0] = up_ref[...]
-
-
-def group_sums(down, up, blocks):
-    rows, width = down.shape
+            halves[own][0] = late_ref[...]
+
+
+def group_sums(early, late, blocks):
+    rows, width = early.shape
     step = rows // blocks // 2
     wide = pl.BlockSpec((step, width), lambda j, i: (2 * j + i, 0))
     narrow = pl.BlockSpec((step, width // GROUPS), lambda j, i: (2 * j + i, 0))
     half = pl.BlockSpec((1, step, width), lambda j, i: (j, 0, 0))
-    out = jax.ShapeDtypeStruct((rows, width // GROUPS), down.dtype)
+    out = jax.ShapeDtypeStruct((rows, width // GROUPS), early.dtype)
     return pl.pallas_call(
         group_kernel,
         grid=(blocks, 2),
         in_specs=[wide, wide],
         out_specs=[narrow, narrow] + [half] * 2,
-        out_shape=[out, out] + [jax.ShapeDtypeStruct((blocks, step, width), down.dtype)] * 2,
+        out_shape=[out, out] + [jax.ShapeDtypeStruct((blocks, step, width), early.dtype)] * 2,
         name="group_sums",
         compiler_params=pltpu.CompilerParams(vmem_limit_bytes=6 * MIB),
         cost_estimate=pl.CostEstimate(
             flops=2 * rows * width, bytes_accessed=6 * rows * width, transcendentals=0
         ),
-    )(down, up)
+    )(early, late)
 
 
 def inverse_of(x):
@@ -102,13 +102,13 @@
             piece[b] = (x_ref[:, at].astype(jnp.float32) * inverse).astype(piece.dtype)
 
 
-def down_kernel(chips, x_ref, match_down, match_up, down_ref, up_ref, *outs):
+def early_pieces_kernel(chips, x_ref, match_early, match_late, early_ref, late_ref, *outs):
     grouped_refs, pieces = outs[:2], outs[2:]
     write_normed(chips, x_ref, pieces)
-    blocks, rows, inner = down_ref.shape
+    blocks, rows, inner = early_ref.shape
     unit = pieces[0].shape[-1]
     own = x_ref.shape[1] // chips // unit
-    for leg, (match, ref) in enumerate(((match_down, down_ref), (match_up, up_ref))):
+    for leg, (match, ref) in enumerate(((match_early, early_ref), (match_late, late_ref))):
         for m in range(blocks):
             chosen = ref[0].astype(jnp.float32)
             for j in range(1, blocks):
@@ -123,48 +123,50 @@
                     ]
 
 
-def up_kernel(chips, x_ref, *pieces):
+def late_pieces_kernel(chips, x_ref, *pieces):
     write_normed(chips, x_ref, pieces)
 
 
-def pieces_down(x, sums_down, sums_up, match_down, match_up, members):
+def pieces_early(x, sums_early, sums_late, match_early, match_late, members):
     rows, width = x.shape
-    inner = sums_down.shape[1]
+    inner = sums_early.shape[1]
     chips = members // 2
     unit = unit_of(width, members, inner)
     count = width // chips // unit + 2 * inner // unit
-    blocks = match_down.shape[0]
+    blocks = match_early.shape[0]
     cut = (blocks, rows // blocks, inner)
     outputs = [jax.ShapeDtypeStruct((rows, inner), x.dtype)] * 2
     outputs += [jax.ShapeDtypeStruct((count, rows, unit), x.dtype)] * chips
     return called(
-        functools.partial(down_kernel, chips),
-        (x, match_down, match_up, sums_down.reshape(cut), sums_up.reshape(cut)),
+        functools.partial(early_pieces_kernel, chips),
+        (x, match_early, match_late, sums_early.reshape(cut), sums_late.reshape(cut)),
         outputs,
         flops=4 * rows * width,
     )
 
 
-def pieces_up(x, inner, members):
+def pieces_late(x, inner, members):
     rows, width = x.shape
     chips = members // 2
     unit = unit_of(width, members, inner)
     outputs = [jax.ShapeDtypeStruct((width // chips // unit, rows, unit), x.dtype)] * chips
-    return called(functools.partial(up_kernel, chips), (x,), outputs, flops=4 * rows * width)
+    return called(
+        functools.partial(late_pieces_kernel, chips), (x,), outputs, flops=4 * rows * width
+    )
 
 
 def product_kernel(chips, inner, *refs):
-    down, up = refs[:chips], refs[chips : 2 * chips]
+    early, late = refs[:chips], refs[chips : 2 * chips]
     keep_ref, send_ref = refs[2 * chips :]
-    unit = down[0].shape[-1]
+    unit = early[0].shape[-1]
     half = keep_ref.shape[0] // unit
     own = 2 * half
     core = lax.axis_index("dp") % 2
     over_tokens = (((0,), (0,)), ((), ()))
 
     def stacked(at, grouped):
-        legs = [ref[at[0]] for ref in down]
-        legs += [ref[at[1]] for ref in (down if grouped else up)]
+        legs = [ref[at[0]] for ref in early]
+        legs += [ref[at[1]] for ref in (early if grouped else late)]
         return jnp.concatenate(legs, axis=0)
 
     for g in range(inner // unit):
@@ -180,13 +182,13 @@
                 )
 
 
-def products(down, up, width, inner, members):
+def products(early, late, width, inner, members):
     chips = members // 2
-    rows = up[0].shape[1]
+    rows = late[0].shape[1]
     out = jax.ShapeDtypeStruct((width // members, inner), jnp.float32)
     return called(
         functools.partial(product_kernel, chips, inner),
-        (*down, *up),
+        (*early, *late),
         [out, out],
         flops=8 * chips * rows * (width // members) * inner,
         vmem=8,
@@ -251,8 +253,8 @@
             through_ref[:, at] = inverse * (back[:, at] - scaled[:, at] * mean)
 
 
-def early_kernel(
-    x_ref, down_ref, up_ref, weight_ref,
+def first_span_kernel(
+    x_ref, early_ref, late_ref, weight_ref,
     next_ref, through_ref, back_ref,
     scaled, back, held, arrived,
 ):
@@ -264,7 +266,7 @@
     scaled[...] = x * inverse
     values = jnp.zeros((rows, inner), jnp.float32)
     total = jnp.zeros((rows, HD), jnp.float32)
-    grouped = jnp.concatenate([down_ref[...], up_ref[...]], axis=0)
+    grouped = jnp.concatenate([early_ref[...], late_ref[...]], axis=0)
     for t, copy in enumerate(copies):
         copy.wait()
         weight = held[t]
@@ -283,7 +285,7 @@
     write_span(x_ref, scaled, back, values, total, inverse, next_ref, through_ref)
 
 
-def late_kernel(x_ref, back_ref, weight_ref, next_ref, through_ref, scaled, held, arrived):
+def second_span_kernel(x_ref, back_ref, weight_ref, next_ref, through_ref, scaled, held, arrived):
     rows, _ = x_ref.shape
     tile, inner = held.shape[1:]
     copies = weight_copies(weight_ref, held, arrived)
@@ -385,24 +387,25 @@
     return jnp.broadcast_to(equal[:, :, None], (blocks, blocks, HD))
 
 
-def on_device(feed_down, feed_up, cotangent_down, cotangent_up, roster, value_weight):
+def relayed(
+    feed_early, feed_late, cotangent_early, cotangent_late, roster_early, roster_late, weight, by
+):
     members = lax.axis_size("dp")
     chips = members // 2
-    weight = value_weight[0]
-    rows, width = feed_down.shape[1:]
+    rows, width = feed_early.shape
     inner = weight.shape[1]
-    match_down = matches(roster[0, 0])
-    match_up = matches(roster[0, 1])
-
-    sums_down, sums_up, *halves = group_sums(
-        cotangent_down[0], cotangent_up[0], roster.shape[2]
-    )
-    x_down = passed_along(feed_down[0], "section", 1)
-    sums_up = passed_along(sums_up, "section", 1)
-    sums_down = passed_along(sums_down, "section", -1)
-    x_up = passed_along(feed_up[0], "section", -1)
-    raw_up = [passed_along(half, "section", 1) for half in halves]
-    raw_down = passed_along(cotangent_down[0], "section", -1)
+    match_early = matches(roster_early)
+    match_late = matches(roster_late)
+
+    sums_early, sums_late, *halves = group_sums(
+        cotangent_early, cotangent_late, roster_early.shape[0]
+    )
+    x_early = passed_along(feed_early, "section", by)
+    sums_late = passed_along(sums_late, "section", by)
+    sums_early = passed_along(sums_early, "section", -by)
+    x_late = passed_along(feed_late, "section", -by)
+    raw_late = [passed_along(half, "section", by) for half in halves]
+    raw_early = passed_along(cotangent_early, "section", -by)
 
     def exchanged(pieces):
         got = [pieces[0]]
@@ -411,24 +414,38 @@
             got.append(lax.ppermute(pieces[c], "dp", to))
         return got
 
-    grouped_down, grouped_up, *sent_down = pieces_down(x_down, sums_down, sums_up, match_down, match_up, members)
-    got_down = exchanged(sent_down)
-    got_up = exchanged(pieces_up(x_up, inner, members))
-
-    next_down, through_down, back_norm = span(
-        early_kernel, (x_down, grouped_down, grouped_up), weight, 2, 2, 3
-    )
-    next_up, through_up = span(late_kernel, (x_up, back_norm), weight, 1, 1, 1)
-
-    keep, send = products(got_down, got_up, width, inner, members)
+    grouped_early, grouped_late, *sent_early = pieces_early(x_early, sums_early, sums_late, match_early, match_late, members)
+    got_early = exchanged(sent_early)
+    got_late = exchanged(pieces_late(x_late, inner, members))
+
+    next_early, through_early, back_norm = span(
+        first_span_kernel, (x_early, grouped_early, grouped_late), weight, 2, 2, 3
+    )
+    next_late, through_late = span(second_span_kernel, (x_late, back_norm), weight, 1, 1, 1)
+
+    keep, send = products(got_early, got_late, width, inner, members)
     got = lax.ppermute(send, "dp", [(i, i ^ 1) for i in range(members)])
     summed = combined(keep, got, float(2 * rows * members) ** (-0.5))
 
-    blocks = roster.shape[2]
-    raw_down = raw_down.reshape(blocks, rows // blocks, width)
-    back_down = finished(raw_down, (0, 1), match_down, through_down)
-    part_up = finished(raw_up[0], (0,), match_up, through_up)
-    back_up = finished(raw_up[1], (1,), match_up, through_up, before=part_up)
+    blocks = roster_early.shape[0]
+    raw_early = raw_early.reshape(blocks, rows // blocks, width)
+    back_early = finished(raw_early, (0, 1), match_early, through_early)
+    part_late = finished(raw_late[0], (0,), match_late, through_late)
+    back_late = finished(raw_late[1], (1,), match_late, through_late, before=part_late)
+    return next_early, next_late, back_early, back_late, summed
+
+
+def on_device(feed_down, feed_up, cotangent_down, cotangent_up, roster, value_weight):
+    next_up, next_down, back_up, back_down, summed = relayed(
+        feed_up[0],
+        feed_down[0],
+        cotangent_up[0],
+        cotangent_down[0],
+        roster[0, 1],
+        roster[0, 0],
+        value_weight[0],
+        -1,
+    )
     return (
         next_down[None],
         next_up[None],

time: 81 us -> 82.6 us (1.020)
  starting transfers between devices: 18.6 us -> 21.6 us
  waiting for transfers between devices: 44.9 us -> 43.5 us
    ppermute x7, starting transfers between devices: 10.4 us -> 13.2 us  [passed_along(): lax.ppermute(shard, axis, [(i, (i + by) % count) for i in range(count)])]
    ppermute x7, waiting for transfers between devices: 32 us -> 30.5 us  [passed_along(): lax.ppermute(shard, axis, [(i, (i + by) % count) for i in range(count)])]
  transfers between devices with their start and end apart: 14 -> 14, of which waited for: 5 -> 5; matrix products, arithmetic and copies ran while one was open for 1% -> 1% of each run, Pallas kernels for 15% -> 14%
where the time goes in v5:
time: 82.6 us; the launch traced here: 82.3 us
  waiting for transfers between devices  43.5 us (53%)
  starting transfers between devices  21.6 us (26%)
  Pallas kernels  13.5 us (16%)
  local copies, waits for them, and re-layouts  2.98 us (4%)
    ppermute x7, waiting for transfers between devices, passed_along(): lax.ppermute(shard, axis, [(i, (i + by) % count) for i in range(count)])  30.5 us
    ppermute x7, starting transfers between devices, passed_along(): lax.ppermute(shard, axis, [(i, (i + by) % count) for i in range(count)])  13.2 us
    ppermute x6, waiting for transfers between devices, exchanged(): got.append(lax.ppermute(pieces[c], 'dp', to))  13 us
    pallas_call x5, Pallas kernels, called(): pl.pallas_call(kernel, in_specs=more.get('in_specs', [whole_vmem()] * len...  9.71 us
    ppermute x6, starting transfers between devices, exchanged(): got.append(lax.ppermute(pieces[c], 'dp', to))  8.28 us
    pallas_call x3, Pallas kernels, finished(): pl.pallas_call(functools.partial(finish_kernel, parts), in_specs=specs, o...  2.54 us
    unnamed x6, local copies, waits for them, and re-layouts  2.09 us
  transfers between devices with their start and end apart: 14, of which 5 were waited for; matrix products, arithmetic and copies ran while one was open for 1% of the time, Pallas kernels for 14%

profile of v5, /device:TPU:0, one launch (start us, length us, event | category | flops | bytes accessed | tf_op | source)
XLA Modules:
  0.0 82.3 jit_solution(2508788586688377282)
XLA Ops:
  0.6 3.1 %collective-permute-start = (bf16[64,4096]{1,0:T(8,128)(2,1)}, bf16[64,4096]{1,0:T(8,128)(2,1)S(1)}, u32[]{:S(2)}, u32[]{:S(2)}) collective-permute-start(bf16[64,4096]{1,0:T(8,128)(2,1)} %bitcast.28), channel_id=1, source_target_pairs={{0,8},{8,16},{16,24},{24,0},{1,9},{9,17},{17,25},{25,1},{2,10},{10... | collective-permute-start | bytes 1572872 | tf_op jit(solution)/shard_map/ppermute | solution.py:25
  3.7 2.1 %collective-permute-start.1 = (bf16[64,4096]{1,0:T(8,128)(2,1)}, bf16[64,4096]{1,0:T(8,128)(2,1)S(1)}, u32[]{:S(2)}, u32[]{:S(2)}) collective-permute-start(bf16[64,4096]{1,0:T(8,128)(2,1)} %bitcast.29), channel_id=1, source_target_pairs={{0,24},{8,0},{16,8},{24,16},{1,25},{9,1},{17,9},{25,17},{2,26},{10... | collective-permute-start | bytes 1572872 | tf_op jit(solution)/shard_map/ppermute | solution.py:25
  5.8 1.0 %copy-done = bf16[1,64,4096]{2,1,0:T(8,128)(2,1)S(1)} copy-done((bf16[1,64,4096]{2,1,0:T(8,128)(2,1)S(1)}, bf16[1,64,4096]{2,1,0:T(8,128)(2,1)}, u32[]{:S(2)}) %copy-start) | copy-done | bytes 524312
  6.9 1.0 %copy-done.1 = bf16[1,64,4096]{2,1,0:T(8,128)(2,1)S(1)} copy-done((bf16[1,64,4096]{2,1,0:T(8,128)(2,1)S(1)}, bf16[1,64,4096]{2,1,0:T(8,128)(2,1)}, u32[]{:S(2)}) %copy-start.1) | copy-done | bytes 524312
  7.9 0.2 group_sums.1
  8.2 3.8 %collective-permute-start.3 = (bf16[64,512]{1,0:T(8,128)(2,1)S(1)}, bf16[64,512]{1,0:T(8,128)(2,1)S(1)}, u32[]{:S(2)}, u32[]{:S(2)}) collective-permute-start(bf16[64,512]{1,0:T(8,128)(2,1)S(1)} %get-tuple-element.27), channel_id=1, source_target_pairs={{0,24},{8,0},{16,8},{24,16},{1,25},{9,1},{17,9},{25,17},{2,26},{10... | collective-permute-start | bytes 196616 | tf_op jit(solution)/shard_map/ppermute | solution.py:25
  12.0 0.8 slice_bitcast_fusion
  12.8 6.0 %collective-permute-done.x_ref = bf16[64,4096]{1,0:T(8,128)(2,1)S(1)} collective-permute-done((bf16[64,4096]{1,0:T(8,128)(2,1)}, bf16[64,4096]{1,0:T(8,128)(2,1)S(1)}, u32[]{:S(2)}, u32[]{:S(2)}) %collective-permute-start) | collective-permute-done | bytes 524320 | tf_op jit(solution)/shard_map/ppermute | solution.py:25
  18.8 0.2 shard_map.104
  19.0 1.8 %collective-permute-start.10 = (bf16[2,64,512]{2,1,0:T(8,128)(2,1)S(1)}, bf16[2,64,512]{2,1,0:T(8,128)(2,1)S(1)}, u32[]{:S(2)}, u32[]{:S(2)}) collective-permute-start(bf16[2,64,512]{2,1,0:T(8,128)(2,1)S(1)} %get-tuple-element.42), channel_id=1, source_target_pairs={{0,2},{1,3},{2,0},{3,1},{4,6},{5,7},{6,4},{7,5},{8,10},{9,11},{10,... | collective-permute-start | bytes 393224 | tf_op jit(solution)/shard_map/ppermute | solution.py:414
  20.8 10.6 %collective-permute-done.2 = bf16[64,512]{1,0:T(8,128)(2,1)S(1)} collective-permute-done((bf16[64,512]{1,0:T(8,128)(2,1)S(1)}, bf16[64,512]{1,0:T(8,128)(2,1)S(1)}, u32[]{:S(2)}, u32[]{:S(2)}) %collective-permute-start.2) | collective-permute-done | bytes 65568 | tf_op jit(solution)/shard_map/ppermute | solution.py:25
  31.4 0.1 broadcast_in_dim.30.match_late.match_ref
  31.5 0.3 shard_map.101
  31.8 1.6 %collective-permute-start.7 = (bf16[4,64,512]{2,1,0:T(8,128)(2,1)S(1)}, bf16[4,64,512]{2,1,0:T(8,128)(2,1)S(1)}, u32[]{:S(2)}, u32[]{:S(2)}) collective-permute-start(bf16[4,64,512]{2,1,0:T(8,128)(2,1)S(1)} %get-tuple-element.38), channel_id=1, source_target_pairs={{0,2},{1,3},{2,0},{3,1},{4,6},{5,7},{6,4},{7,5},{8,10},{9,11},{10,... | collective-permute-start | bytes 786440 | tf_op jit(solution)/shard_map/ppermute | solution.py:414
  33.4 1.5 %collective-permute-start.8 = (bf16[4,64,512]{2,1,0:T(8,128)(2,1)S(1)}, bf16[4,64,512]{2,1,0:T(8,128)(2,1)S(1)}, u32[]{:S(2)}, u32[]{:S(2)}) collective-permute-start(bf16[4,64,512]{2,1,0:T(8,128)(2,1)S(1)} %get-tuple-element.39), channel_id=1, source_target_pairs={{0,4},{1,5},{2,6},{3,7},{4,0},{5,1},{6,2},{7,3},{8,12},{9,13},{10,... | collective-permute-start | bytes 786440 | tf_op jit(solution)/shard_map/ppermute | solution.py:414
  34.9 0.5 collective-permute-start.9
  35.4 1.5 %collective-permute-start.11 = (bf16[2,64,512]{2,1,0:T(8,128)(2,1)S(1)}, bf16[2,64,512]{2,1,0:T(8,128)(2,1)S(1)}, u32[]{:S(2)}, u32[]{:S(2)}) collective-permute-start(bf16[2,64,512]{2,1,0:T(8,128)(2,1)S(1)} %get-tuple-element.43), channel_id=1, source_target_pairs={{0,4},{1,5},{2,6},{3,7},{4,0},{5,1},{6,2},{7,3},{8,12},{9,13},{10,... | collective-permute-start | bytes 393224 | tf_op jit(solution)/shard_map/ppermute | solution.py:414
  36.9 1.4 %collective-permute-start.12 = (bf16[2,64,512]{2,1,0:T(8,128)(2,1)S(1)}, bf16[2,64,512]{2,1,0:T(8,128)(2,1)S(1)}, u32[]{:S(2)}, u32[]{:S(2)}) collective-permute-start(bf16[2,64,512]{2,1,0:T(8,128)(2,1)S(1)} %get-tuple-element.44), channel_id=1, source_target_pairs={{0,6},{1,7},{2,4},{3,5},{4,2},{5,3},{6,0},{7,1},{8,14},{9,15},{10,... | collective-permute-start | bytes 393224 | tf_op jit(solution)/shard_map/ppermute | solution.py:414
  38.3 12.9 %collective-permute-done.11.refs_6_ = bf16[2,64,512]{2,1,0:T(8,128)(2,1)S(1)} collective-permute-done((bf16[2,64,512]{2,1,0:T(8,128)(2,1)S(1)}, bf16[2,64,512]{2,1,0:T(8,128)(2,1)S(1)}, u32[]{:S(2)}, u32[]{:S(2)}) %collective-permute-start.11) | collective-permute-done | bytes 131104 | tf_op jit(solution)/shard_map/ppermute | solution.py:414
  51.3 0.8 shard_map.105
  52.1 0.1 collective-permute-start.13
  52.2 2.4 %collective-permute-start.6 = (bf16[64,4096]{1,0:T(8,128)(2,1)S(1)}, bf16[64,4096]{1,0:T(8,128)(2,1)S(1)}, u32[]{:S(2)}, u32[]{:S(2)}) collective-permute-start(bf16[64,4096]{1,0:T(8,128)(2,1)S(1)} %bitcast.20), channel_id=1, source_target_pairs={{0,8},{8,16},{16,24},{24,0},{1,9},{9,17},{17,25},{25,1},{2,10},{10... | collective-permute-start | bytes 1572872 | tf_op jit(solution)/shard_map/ppermute | solution.py:25
  54.6 1.4 %collective-permute-start.5 = (bf16[2,16,4096]{2,1,0:T(8,128)(2,1)S(1)}, bf16[2,16,4096]{2,1,0:T(8,128)(2,1)S(1)}, u32[]{:S(2)}, u32[]{:S(2)}) collective-permute-start(bf16[2,16,4096]{2,1,0:T(8,128)(2,1)S(1)} %get-tuple-element.35), channel_id=1, source_target_pairs={{0,24},{8,0},{16,8},{24,16},{1,25},{9,1},{17,9},{25,17},{2,26},{10... | collective-permute-start | bytes 786440 | tf_op jit(solution)/shard_map/ppermute | solution.py:25
  56.0 0.3 collective-permute-start.4
  56.3 5.0 %shard_map.102 = (bf16[64,4096]{1,0:T(8,128)(2,1)}, f32[64,4096]{1,0:T(8,128)S(1)}, f32[64,4096]{1,0:T(8,128)S(1)}) custom-call(bf16[64,4096]{1,0:T(8,128)(2,1)S(1)} %collective-permute-done.1.x_ref, bf16[64,512]{1,0:T(8,128)(2,1)S(1)} %get-tuple-element.28.early_ref, bf16[64,512]{1,0:T(8,128)(2,1)S(1)} %get-tuple-element.29.late_ref, bf16[4096,512]{1,0:T(8,128)(2,1)} %bitcast.23), custom_call_target="tpu_custom_call" | custom-call | flops 805306368 | bytes 7471104 | tf_op jit(solution)/shard_map/pallas_call | solution.py:34
  61.4 3.4 %shard_map.103 = (bf16[64,4096]{1,0:T(8,128)(2,1)}, f32[64,4096]{1,0:T(8,128)S(1)}) custom-call(bf16[64,4096]{1,0:T(8,128)(2,1)S(1)} %collective-permute-done.x_ref, f32[64,4096]{1,0:T(8,128)S(1)} %get-tuple-element.30.back_ref, bf16[4096,512]{1,0:T(8,128)(2,1)} %bitcast.24), custom_call_target="tpu_custom_call" | custom-call | flops 268435456 | bytes 7340032 | tf_op jit(solution)/shard_map/pallas_call | solution.py:34
  64.8 9.3 %collective-permute-done.5.refs_0_ = bf16[2,16,4096]{2,1,0:T(8,128)(2,1)S(1)} collective-permute-done((bf16[2,16,4096]{2,1,0:T(8,128)(2,1)S(1)}, bf16[2,16,4096]{2,1,0:T(8,128)(2,1)S(1)}, u32[]{:S(2)}, u32[]{:S(2)}) %collective-permute-start.5) | collective-permute-done | bytes 262176 | tf_op jit(solution)/shard_map/ppermute | solution.py:25
  74.0 0.8 finished.3.refs_1_
  74.8 4.7 %collective-permute-done.4.refs_0_ = bf16[2,16,4096]{2,1,0:T(8,128)(2,1)S(1)} collective-permute-done((bf16[2,16,4096]{2,1,0:T(8,128)(2,1)S(1)}, bf16[2,16,4096]{2,1,0:T(8,128)(2,1)S(1)}, u32[]{:S(2)}, u32[]{:S(2)}) %collective-permute-start.4) | collective-permute-done | bytes 262176 | tf_op jit(solution)/shard_map/ppermute | solution.py:25
  79.5 0.8 finished.4
  80.4 0.9 %finished.5 = bf16[64,4096]{1,0:T(8,128)(2,1)} custom-call(s32[2,2,128]{2,1,0:T(2,128)S(1)} %broadcast_in_dim.14.match_early.match_ref, f32[64,4096]{1,0:T(8,128)S(1)} %get-tuple-element.36.through_ref, bf16[2,32,4096]{2,1,0:T(8,128)(2,1)S(1)} %bitcast.17), custom_call_target="tpu_custom_call" | custom-call | flops 524288 | bytes 2097152 | tf_op jit(solution)/shard_map/finished/pallas_call | solution.py:363
  81.3 1.0 %combine.1 = f32[512,512]{1,0:T(8,128)} custom-call(f32[512,512]{1,0:T(8,128)S(1)} %get-tuple-element.45.keep_ref, f32[512,512]{1,0:T(8,128)S(1)} %collective-permute-done.13.got_ref), custom_call_target="tpu_custom_call" | custom-call | flops 524288 | bytes 3145728 | tf_op jit(solution)/shard_map/combine/pallas_call | solution.py:215
  (17 shorter events, 0.2 us)
Async XLA Ops:
  0.6 18.2 %collective-permute-start = (bf16[64,4096]{1,0:T(8,128)(2,1)}, bf16[64,4096]{1,0:T(8,128)(2,1)S(1)}, u32[]{:S(2)}, u32[]{:S(2)}) collective-permute-start(bf16[64,4096]{1,0:T(8,128)(2,1)} %bitcast.28), channel_id=1, source_target_pairs={{0,8},{8,16},{16,24},{24,0},{1,9},{9,17},{17,25},{25,1},{2,10},{10... | collective-permute-start | bytes 1572872 | tf_op jit(solution)/shard_map/ppermute | solution.py:25
  3.7 27.6 %collective-permute-start.1 = (bf16[64,4096]{1,0:T(8,128)(2,1)}, bf16[64,4096]{1,0:T(8,128)(2,1)S(1)}, u32[]{:S(2)}, u32[]{:S(2)}) collective-permute-start(bf16[64,4096]{1,0:T(8,128)(2,1)} %bitcast.29), channel_id=1, source_target_pairs={{0,24},{8,0},{16,8},{24,16},{1,25},{9,1},{17,9},{25,17},{2,26},{10... | collective-permute-start | bytes 1572872 | tf_op jit(solution)/shard_map/ppermute | solution.py:25
  5.8 1.0 %copy-start = (bf16[1,64,4096]{2,1,0:T(8,128)(2,1)S(1)}, bf16[1,64,4096]{2,1,0:T(8,128)(2,1)}, u32[]{:S(2)}) copy-start(bf16[1,64,4096]{2,1,0:T(8,128)(2,1)} %param.8) | copy-start | bytes 1572868
  6.9 1.0 %copy-start.1 = (bf16[1,64,4096]{2,1,0:T(8,128)(2,1)S(1)}, bf16[1,64,4096]{2,1,0:T(8,128)(2,1)}, u32[]{:S(2)}) copy-start(bf16[1,64,4096]{2,1,0:T(8,128)(2,1)} %param.9) | copy-start | bytes 1572868
  7.9 44.2 %copy-start.2 = (bf16[1,64,4096]{2,1,0:T(8,128)(2,1)S(1)}, bf16[1,64,4096]{2,1,0:T(8,128)(2,1)}, u32[]{:S(2)}) copy-start(bf16[1,64,4096]{2,1,0:T(8,128)(2,1)} %param.9) | copy-start | bytes 1572868
  8.2 23.2 %collective-permute-start.2 = (bf16[64,512]{1,0:T(8,128)(2,1)S(1)}, bf16[64,512]{1,0:T(8,128)(2,1)S(1)}, u32[]{:S(2)}, u32[]{:S(2)}) collective-permute-start(bf16[64,512]{1,0:T(8,128)(2,1)S(1)} %get-tuple-element.26), channel_id=1, source_target_pairs={{0,8},{8,16},{16,24},{24,0},{1,9},{9,17},{17,25},{25,1},{2,10},{10... | collective-permute-start | bytes 196616 | tf_op jit(solution)/shard_map/ppermute | solution.py:25
  8.2 23.2 %collective-permute-start.3 = (bf16[64,512]{1,0:T(8,128)(2,1)S(1)}, bf16[64,512]{1,0:T(8,128)(2,1)S(1)}, u32[]{:S(2)}, u32[]{:S(2)}) collective-permute-start(bf16[64,512]{1,0:T(8,128)(2,1)S(1)} %get-tuple-element.27), channel_id=1, source_target_pairs={{0,24},{8,0},{16,8},{24,16},{1,25},{9,1},{17,9},{25,17},{2,26},{10... | collective-permute-start | bytes 196616 | tf_op jit(solution)/shard_map/ppermute | solution.py:25
  19.0 17.9 %collective-permute-start.10 = (bf16[2,64,512]{2,1,0:T(8,128)(2,1)S(1)}, bf16[2,64,512]{2,1,0:T(8,128)(2,1)S(1)}, u32[]{:S(2)}, u32[]{:S(2)}) collective-permute-start(bf16[2,64,512]{2,1,0:T(8,128)(2,1)S(1)} %get-tuple-element.42), channel_id=1, source_target_pairs={{0,2},{1,3},{2,0},{3,1},{4,6},{5,7},{6,4},{7,5},{8,10},{9,11},{10,... | collective-permute-start | bytes 393224 | tf_op jit(solution)/shard_map/ppermute | solution.py:414
  31.8 19.5 %collective-permute-start.7 = (bf16[4,64,512]{2,1,0:T(8,128)(2,1)S(1)}, bf16[4,64,512]{2,1,0:T(8,128)(2,1)S(1)}, u32[]{:S(2)}, u32[]{:S(2)}) collective-permute-start(bf16[4,64,512]{2,1,0:T(8,128)(2,1)S(1)} %get-tuple-element.38), channel_id=1, source_target_pairs={{0,2},{1,3},{2,0},{3,1},{4,6},{5,7},{6,4},{7,5},{8,10},{9,11},{10,... | collective-permute-start | bytes 786440 | tf_op jit(solution)/shard_map/ppermute | solution.py:414
  33.4 17.9 %collective-permute-start.8 = (bf16[4,64,512]{2,1,0:T(8,128)(2,1)S(1)}, bf16[4,64,512]{2,1,0:T(8,128)(2,1)S(1)}, u32[]{:S(2)}, u32[]{:S(2)}) collective-permute-start(bf16[4,64,512]{2,1,0:T(8,128)(2,1)S(1)} %get-tuple-element.39), channel_id=1, source_target_pairs={{0,4},{1,5},{2,6},{3,7},{4,0},{5,1},{6,2},{7,3},{8,12},{9,13},{10,... | collective-permute-start | bytes 786440 | tf_op jit(solution)/shard_map/ppermute | solution.py:414
  34.9 16.4 %collective-permute-start.9 = (bf16[4,64,512]{2,1,0:T(8,128)(2,1)S(1)}, bf16[4,64,512]{2,1,0:T(8,128)(2,1)S(1)}, u32[]{:S(2)}, u32[]{:S(2)}) collective-permute-start(bf16[4,64,512]{2,1,0:T(8,128)(2,1)S(1)} %get-tuple-element.40), channel_id=1, source_target_pairs={{0,6},{1,7},{2,4},{3,5},{4,2},{5,3},{6,0},{7,1},{8,14},{9,15},{10,... | collective-permute-start | bytes 786440 | tf_op jit(solution)/shard_map/ppermute | solution.py:414
  35.4 15.9 %collective-permute-start.11 = (bf16[2,64,512]{2,1,0:T(8,128)(2,1)S(1)}, bf16[2,64,512]{2,1,0:T(8,128)(2,1)S(1)}, u32[]{:S(2)}, u32[]{:S(2)}) collective-permute-start(bf16[2,64,512]{2,1,0:T(8,128)(2,1)S(1)} %get-tuple-element.43), channel_id=1, source_target_pairs={{0,4},{1,5},{2,6},{3,7},{4,0},{5,1},{6,2},{7,3},{8,12},{9,13},{10,... | collective-permute-start | bytes 393224 | tf_op jit(solution)/shard_map/ppermute | solution.py:414
  36.9 14.4 %collective-permute-start.12 = (bf16[2,64,512]{2,1,0:T(8,128)(2,1)S(1)}, bf16[2,64,512]{2,1,0:T(8,128)(2,1)S(1)}, u32[]{:S(2)}, u32[]{:S(2)}) collective-permute-start(bf16[2,64,512]{2,1,0:T(8,128)(2,1)S(1)} %get-tuple-element.44), channel_id=1, source_target_pairs={{0,6},{1,7},{2,4},{3,5},{4,2},{5,3},{6,0},{7,1},{8,14},{9,15},{10,... | collective-permute-start | bytes 393224 | tf_op jit(solution)/shard_map/ppermute | solution.py:414
  52.1 29.2 %collective-permute-start.13 = (f32[512,512]{1,0:T(8,128)S(1)}, f32[512,512]{1,0:T(8,128)S(1)}, u32[]{:S(2)}, u32[]{:S(2)}) collective-permute-start(f32[512,512]{1,0:T(8,128)S(1)} %get-tuple-element.46), channel_id=1, source_target_pairs={{0,1},{1,0},{2,3},{3,2},{4,5},{5,4},{6,7},{7,6},{8,9},{9,8},{10,11... | collective-permute-start | bytes 3145736 | tf_op jit(solution)/shard_map/ppermute | solution.py:427
  52.2 28.2 %collective-permute-start.6 = (bf16[64,4096]{1,0:T(8,128)(2,1)S(1)}, bf16[64,4096]{1,0:T(8,128)(2,1)S(1)}, u32[]{:S(2)}, u32[]{:S(2)}) collective-permute-start(bf16[64,4096]{1,0:T(8,128)(2,1)S(1)} %bitcast.20), channel_id=1, source_target_pairs={{0,8},{8,16},{16,24},{24,0},{1,9},{9,17},{17,25},{25,1},{2,10},{10... | collective-permute-start | bytes 1572872 | tf_op jit(solution)/shard_map/ppermute | solution.py:25
  54.6 19.4 %collective-permute-start.5 = (bf16[2,16,4096]{2,1,0:T(8,128)(2,1)S(1)}, bf16[2,16,4096]{2,1,0:T(8,128)(2,1)S(1)}, u32[]{:S(2)}, u32[]{:S(2)}) collective-permute-start(bf16[2,16,4096]{2,1,0:T(8,128)(2,1)S(1)} %get-tuple-element.35), channel_id=1, source_target_pairs={{0,24},{8,0},{16,8},{24,16},{1,25},{9,1},{17,9},{25,17},{2,26},{10... | collective-permute-start | bytes 786440 | tf_op jit(solution)/shard_map/ppermute | solution.py:25
  56.0 23.5 %collective-permute-start.4 = (bf16[2,16,4096]{2,1,0:T(8,128)(2,1)S(1)}, bf16[2,16,4096]{2,1,0:T(8,128)(2,1)S(1)}, u32[]{:S(2)}, u32[]{:S(2)}) collective-permute-start(bf16[2,16,4096]{2,1,0:T(8,128)(2,1)S(1)} %get-tuple-element.34), channel_id=1, source_target_pairs={{0,24},{8,0},{16,8},{24,16},{1,25},{9,1},{17,9},{25,17},{2,26},{10... | collective-permute-start | bytes 786440 | tf_op jit(solution)/shard_map/ppermute | solution.py:25

commit v6 on v3

v6 whole, which is shorter than its diff:
```python
import functools
import math

import jax
import jax.numpy as jnp
from jax import lax
from jax.experimental import pallas as pl
from jax.experimental.pallas import tpu as pltpu
from jax.sharding import PartitionSpec as P


KVH = 4
HD = 128
GROUPS = 8


EPSILON = 1e-05


MIB = 2**20


def passed_along(shard, axis, by):
    count = lax.axis_size(axis)
    return lax.ppermute(shard, axis, [(i, (i + by) % count) for i in range(count)])


def whole_vmem():
    return pl.BlockSpec(memory_space=pltpu.VMEM)


def called(kernel, operands, outputs, scratch=(), flops=0, vmem=4, **more):
    moved = sum(x.size * x.dtype.itemsize for x in list(operands) + list(outputs))
    return pl.pallas_call(
        kernel,
        in_specs=more.get("in_specs", [whole_vmem()] * len(operands)),
        out_specs=[whole_vmem()] * len(outputs),
        out_shape=list(outputs),
        scratch_shapes=list(scratch),
        compiler_params=pltpu.CompilerParams(vmem_limit_bytes=vmem * MIB),
        cost_estimate=pl.CostEstimate(
            flops=flops, bytes_accessed=moved, transcendentals=0
        ),
    )(*operands)


def group_sum(load):
    sums = []
    for k in range(KVH):
        total = load(k * GROUPS * HD).astype(jnp.float32)
        for j in range(1, GROUPS):
            total = total + load((k * GROUPS + j) * HD).astype(jnp.float32)
        sums.append(total)
    return sums


def group_kernel(
    early_ref, late_ref, early_out, late_out, first_out, rest_out, second_out
):
    block = pl.program_id(0)
    part = pl.program_id(1)
    opening = (part == 0) & (block == 0)
    for k, total in enumerate(group_sum(lambda at: early_ref[:, at : at + HD])):
        early_out[:, k * HD : (k + 1) * HD] = total.astype(early_out.dtype)

    @pl.when(opening)
    def _():
        first_out[0] = late_ref[...]

    @pl.when(jnp.logical_not(opening))
    def _():
        for k, total in enumerate(group_sum(lambda at: late_ref[:, at : at + HD])):
            late_out[0, :, k * HD : (k + 1) * HD] = total.astype(late_out.dtype)

    @pl.when((part == 0) & (block > 0))
    def _():
        rest_out[0] = late_ref[...]

    @pl.when(part == 1)
    def _():
        second_out[0] = late_ref[...]


def group_sums(early, late, blocks):
    rows, width = early.shape
    inner = width // GROUPS
    step = rows // blocks // 2
    wide = pl.BlockSpec((step, width), lambda j, i: (2 * j + i, 0))
    narrow = pl.BlockSpec((step, inner), lambda j, i: (2 * j + i, 0))
    later = pl.BlockSpec((1, step, inner), lambda j, i: (jnp.maximum(2 * j + i - 1, 0), 0, 0))
    shape = (1, step, width)
    first = pl.BlockSpec(shape, lambda j, i: (0, 0, 0))
    rest = pl.BlockSpec(shape, lambda j, i: (jnp.maximum(j - 1, 0), 0, 0))
    second = pl.BlockSpec(shape, lambda j, i: (j, 0, 0))
    return pl.pallas_call(
        group_kernel,
        grid=(blocks, 2),
        in_specs=[wide, wide],
        out_specs=[narrow, later, first, rest, second],
        out_shape=[
            jax.ShapeDtypeStruct((rows, inner), early.dtype),
            jax.ShapeDtypeStruct((2 * blocks - 1, step, inner), late.dtype),
        ]
        + [
            jax.ShapeDtypeStruct((count, step, width), late.dtype)
            for count in (1, blocks - 1, blocks)
        ],
        name="group_sums",
        compiler_params=pltpu.CompilerParams(vmem_limit_bytes=6 * MIB),
        cost_estimate=pl.CostEstimate(
            flops=2 * rows * width, bytes_accessed=6 * rows * width, transcendentals=0
        ),
    )(early, late)


def inverse_of(x):
    return lax.rsqrt(jnp.mean(x * x, axis=-1, keepdims=True) + EPSILON)


def unit_of(width, members, inner):
    return math.gcd(width // members, inner)


def write_normed(chips, x_ref, piece_refs):
    inverse = inverse_of(x_ref[...].astype(jnp.float32))
    unit = piece_refs[0].shape[-1]
    per_chip = x_ref.shape[1] // chips
    chip = lax.axis_index("dp") // 2
    for c, piece in enumerate(piece_refs):
        base = (chip ^ c) * per_chip
        for b in range(per_chip // unit):
            at = pl.ds(pl.multiple_of(base + b * unit, unit), unit)
            piece[b] = (x_ref[:, at].astype(jnp.float32) * inverse).astype(piece.dtype)


def arranged(match_ref, m, block_of, blocks):
    chosen = block_of(0).astype(jnp.float32)
    for j in range(1, blocks):
        mine = match_ref[m, j : j + 1, 0:1] != 0
        chosen = jnp.where(mine, block_of(j).astype(jnp.float32), chosen)
    return chosen


def write_grouped(at, value, own, grouped_ref, piece_refs):
    rows, inner = value.shape
    unit = piece_refs[0].shape[-1]
    grouped_ref[at : at + rows, :] = value
    for piece in piece_refs:
        for b in range(inner // unit):
            piece[own + b, at : at + rows, :] = value[:, b * unit : (b + 1) * unit]


def early_pieces_kernel(chips, x_ref, match_ref, sums_ref, grouped_ref, *pieces):
    write_normed(chips, x_ref, pieces)
    blocks, rows, _ = sums_ref.shape
    own = x_ref.shape[1] // chips // pieces[0].shape[-1]
    for m in range(blocks):
        value = arranged(match_ref, m, lambda j: sums_ref[j], blocks).astype(x_ref.dtype)
        write_grouped(m * rows, value, own, grouped_ref, pieces)


def late_pieces_kernel(chips, x_ref, match_ref, first_ref, sums_ref, grouped_ref, *pieces):
    write_normed(chips, x_ref, pieces)
    half = first_ref.shape[1]
    blocks = match_ref.shape[0]
    own = x_ref.shape[1] // chips // pieces[0].shape[-1]
    first = group_sum(lambda at: first_ref[0, :, at : at + HD])
    first = jnp.concatenate(first, axis=-1).astype(x_ref.dtype)

    def sums_of(at):
        return first if at == 0 else sums_ref[at - 1]

    for part in range(2):
        for m in range(blocks):
            value = arranged(match_ref, m, lambda j: sums_of(2 * j + part), blocks)
            at = (2 * m + part) * half
            write_grouped(at, value.astype(x_ref.dtype), own, grouped_ref, pieces)


def pieces_of(kernel, x, operands, inner, members):
    rows, width = x.shape
    chips = members // 2
    unit = unit_of(width, members, inner)
    count = width // chips // unit + inner // unit
    outputs = [jax.ShapeDtypeStruct((rows, inner), x.dtype)]
    outputs += [jax.ShapeDtypeStruct((count, rows, unit), x.dtype)] * chips
    return called(functools.partial(kernel, chips), (x, *operands), outputs, flops=4 * rows * width)


def product_kernel(chips, inner, *refs):
    early, late = refs[:chips], refs[chips : 2 * chips]
    keep_ref, send_ref = refs[2 * chips :]
    unit = early[0].shape[-1]
    half = keep_ref.shape[0] // unit
    own = 2 * half
    core = lax.axis_index("dp") % 2
    over_tokens = (((0,), (0,)), ((), ()))

    def stacked(at):
        return jnp.concatenate([ref[at] for ref in (*early, *late)], axis=0)

    for g in range(inner // unit):
        grouped = stacked(own + g)
        for dest, out_ref in ((core, keep_ref), (1 - core, send_ref)):
            for b in range(half):
                out_ref[b * unit : (b + 1) * unit, g * unit : (g + 1) * unit] = lax.dot_general(
                    stacked(dest * half + b),
                    grouped,
                    over_tokens,
                    preferred_element_type=jnp.float32,
                )


def products(early, late, width, inner, members):
    chips = members // 2
    rows = late[0].shape[1]
    out = jax.ShapeDtypeStruct((width // members, inner), jnp.float32)
    return called(
        functools.partial(product_kernel, chips, inner),
        (*early, *late),
        [out, out],
        flops=8 * chips * rows * (width // members) * inner,
        vmem=8,
    )


def combine_kernel(factor, keep_ref, got_ref, out_ref, held, sent):
    slots, step, _ = held.shape
    copies = []
    for i in range(slots):
        at = i * step
        held[i] = (keep_ref[at : at + step, :] + got_ref[at : at + step, :]) * factor
        copies.append(
            pltpu.make_async_copy(held.at[i], out_ref.at[pl.ds(at, step), :], sent.at[i])
        )
        copies[-1].start()
    for copy in copies:
        copy.wait()


def combined(keep, got, factor):
    rows, inner = keep.shape
    slots = 4
    return pl.pallas_call(
        functools.partial(combine_kernel, factor),
        in_specs=[whole_vmem()] * 2,
        out_specs=pl.BlockSpec(memory_space=pltpu.HBM),
        out_shape=jax.ShapeDtypeStruct(keep.shape, keep.dtype),
        scratch_shapes=[
            pltpu.VMEM((slots, rows // slots, inner), keep.dtype),
            pltpu.SemaphoreType.DMA((slots,)),
        ],
        name="combine",
        compiler_params=pltpu.CompilerParams(vmem_limit_bytes=4 * MIB),
        cost_estimate=pl.CostEstimate(
            flops=2 * rows * inner, bytes_accessed=12 * rows * inner, transcendentals=0
        ),
    )(keep, got)


def span_kernel(x_ref, grouped_ref, weight_ref, next_ref, through_ref, scaled, back, held, arrived):
    rows, width = x_ref.shape
    tiles, tile, inner = held.shape
    copies = [
        pltpu.make_async_copy(weight_ref.at[pl.ds(t * tile, tile), :], held.at[t], arrived.at[t])
        for t in range(tiles)
    ]
    for copy in copies:
        copy.start()
    x = x_ref[...].astype(jnp.float32)
    inverse = inverse_of(x)
    scaled[...] = x * inverse
    values = jnp.zeros((rows, inner), jnp.float32)
    total = jnp.zeros((rows, HD), jnp.float32)
    grouped = grouped_ref[...]
    for t, copy in enumerate(copies):
        copy.wait()
        weight = held[t]
        at = slice(t * tile, (t + 1) * tile)
        normed = scaled[:, at].astype(x_ref.dtype)
        values = values + jnp.dot(normed, weight, preferred_element_type=jnp.float32)
        part = lax.dot_general(
            grouped, weight, (((1,), (1,)), ((), ())), preferred_element_type=jnp.float32
        )
        back[:, at] = part
        for c in range(tile // HD):
            lanes = slice(c * HD, (c + 1) * HD)
            total = total + part[:, lanes] * scaled[:, t * tile + c * HD : t * tile + (c + 1) * HD]
    mean = jnp.sum(total, axis=-1, keepdims=True) * (1.0 / width)
    mean = jnp.broadcast_to(mean, (rows, HD))
    inverse = jnp.broadcast_to(inverse, (rows, HD))
    for k in range(KVH):
        spread = values[:, k * HD : (k + 1) * HD]
        for j in range(GROUPS):
            at = slice((k * GROUPS + j) * HD, (k * GROUPS + j + 1) * HD)
            next_ref[:, at] = (x_ref[:, at].astype(jnp.float32) + spread).astype(next_ref.dtype)
            through_ref[:, at] = inverse * (back[:, at] - scaled[:, at] * mean)


def span(x, grouped, weight):
    rows, width = x.shape
    inner = weight.shape[1]
    tile = math.gcd(width, 512)
    return called(
        span_kernel,
        (x, grouped, pltpu.with_memory_space_constraint(weight, pltpu.HBM)),
        [
            jax.ShapeDtypeStruct((rows, width), x.dtype),
            jax.ShapeDtypeStruct((rows, width), jnp.float32),
        ],
        scratch=[
            pltpu.VMEM((rows, width), jnp.float32),
            pltpu.VMEM((rows, width), jnp.float32),
            pltpu.VMEM((width // tile, tile, inner), weight.dtype),
            pltpu.SemaphoreType.DMA((width // tile,)),
        ],
        flops=4 * rows * width * inner,
        vmem=10,
        in_specs=[whole_vmem()] * 2 + [pl.BlockSpec(memory_space=pltpu.HBM)],
    )


def finish_kernel(parts, places, match_ref, through_ref, *refs):
    out_ref, held, sent = refs[-3:]
    blocks = match_ref.shape[0]
    half = held.shape[1]
    copies = []
    for i, part in enumerate(parts):

        def received(j):
            operand, at = places[i * blocks + j]
            return refs[operand][at].astype(jnp.float32)

        for m in range(blocks):
            chosen = received(0)
            for j in range(1, blocks):
                mine = match_ref[m, j : j + 1, 0:1] != 0
                chosen = jnp.where(mine, received(j), chosen)
            at = (2 * m + part) * half
            slot = i * blocks + m
            held[slot] = (chosen + through_ref[at : at + half, :]).astype(held.dtype)
            copies.append(
                pltpu.make_async_copy(
                    held.at[slot], out_ref.at[pl.ds(at, half), :], sent.at[slot]
                )
            )
            copies[-1].start()
    for copy in copies:
        copy.wait()


def finished(raws, parts, places, match, through, before=None):
    rows, width = through.shape
    blocks = match.shape[0]
    slots = blocks * len(parts)
    half = rows // blocks // 2
    operands = [match, through, *raws] + ([] if before is None else [before])
    specs = [whole_vmem()] * (2 + len(raws))
    if before is not None:
        specs.append(pl.BlockSpec(memory_space=pltpu.HBM))
    return pl.pallas_call(
        functools.partial(finish_kernel, parts, places),
        in_specs=specs,
        out_specs=pl.BlockSpec(memory_space=pltpu.HBM),
        out_shape=jax.ShapeDtypeStruct((rows, width), raws[0].dtype),
        scratch_shapes=[
            pltpu.VMEM((slots, half, width), raws[0].dtype),
            pltpu.SemaphoreType.DMA((slots,)),
        ],
        input_output_aliases={} if before is None else {len(operands) - 1: 0},
        name="finished",
        compiler_params=pltpu.CompilerParams(vmem_limit_bytes=4 * MIB),
        cost_estimate=pl.CostEstimate(
            flops=2 * slots * half * width,
            bytes_accessed=8 * slots * half * width,
            transcendentals=0,
        ),
    )(*operands)


def matches(roster_row):
    blocks = roster_row.shape[0]
    wanted = jnp.arange(blocks, dtype=jnp.int32)
    equal = (roster_row[None, :] == wanted[:, None]).astype(jnp.int32)
    return jnp.broadcast_to(equal[:, :, None], (blocks, blocks, HD))


def relayed(
    feed_early, feed_late, cotangent_early, cotangent_late, roster_early, roster_late, weight, by
):
    members = lax.axis_size("dp")
    chips = members // 2
    rows, width = feed_early.shape
    inner = weight.shape[1]
    match_early = matches(roster_early)
    match_late = matches(roster_late)

    sums_early, sums_late, *pieces = group_sums(
        cotangent_early, cotangent_late, roster_early.shape[0]
    )
    x_early = passed_along(feed_early, "section", by)
    sums_late = passed_along(sums_late, "section", by)
    sums_early = passed_along(sums_early, "section", -by)
    x_late = passed_along(feed_late, "section", -by)
    raw_late = [passed_along(piece, "section", by) for piece in pieces]
    raw_early = passed_along(cotangent_early, "section", -by)

    def exchanged(pieces):
        got = [pieces[0]]
        for c in range(1, chips):
            to = [(i, ((i // 2) ^ c) * 2 + i % 2) for i in range(members)]
            got.append(lax.ppermute(pieces[c], "dp", to))
        return got

    blocks = roster_early.shape[0]
    sums_early = sums_early.reshape(blocks, rows // blocks, inner)
    grouped_early, *sent_early = pieces_of(
        early_pieces_kernel, x_early, (match_early, sums_early), inner, members
    )
    got_early = exchanged(sent_early)
    grouped_late, *sent_late = pieces_of(
        late_pieces_kernel, x_late, (match_late, raw_late[0], sums_late), inner, members
    )
    got_late = exchanged(sent_late)

    next_early, through_early = span(x_early, grouped_early, weight)
    next_late, through_late = span(x_late, grouped_late, weight)

    keep, send = products(got_early, got_late, width, inner, members)
    got = lax.ppermute(send, "dp", [(i, i ^ 1) for i in range(members)])
    summed = combined(keep, got, float(2 * rows * members) ** (-0.5))

    raw_early = [raw_early.reshape(2 * blocks, rows // blocks // 2, width)]
    whole = [(0, 2 * j + part) for part in range(2) for j in range(blocks)]
    firsts = [(min(j, 1), max(j - 1, 0)) for j in range(blocks)]
    seconds = [(0, j) for j in range(blocks)]
    back_early = finished(raw_early, (0, 1), whole, match_early, through_early)
    part_late = finished(raw_late[:2], (0,), firsts, match_late, through_late)
    back_late = finished(raw_late[2:], (1,), seconds, match_late, through_late, part_late)
    return next_early, next_late, back_early, back_late, summed


def on_device(feed_down, feed_up, cotangent_down, cotangent_up, roster, value_weight):
    next_up, next_down, back_up, back_down, summed = relayed(
        feed_up[0],
        feed_down[0],
        cotangent_up[0],
        cotangent_down[0],
        roster[0, 1],
        roster[0, 0],
        value_weight[0],
        -1,
    )
    return (
        next_down[None],
        next_up[None],
        back_down[None],
        back_up[None],
        summed[None],
    )


def solution(mesh):
    rows = P("section", "dp", None)
    kept = P("section", None, None)
    return jax.shard_map(
        on_device,
        mesh=mesh,
        in_specs=(rows, rows, rows, rows, kept, kept),
        out_specs=(rows, rows, rows, rows, rows),
        check_vma=False,
    )
```

time: 91.1 us -> 79.4 us (0.87)
  the two profiles are of different devices: /device:TPU:8 before, /device:TPU:0 now
where the time goes in v6:
time: 79.4 us; the launch traced here: 79.2 us
  waiting for transfers between devices  38.5 us (48%)
  starting transfers between devices  22.1 us (28%)
  Pallas kernels  14.8 us (19%)
  local copies, waits for them, and re-layouts  2.98 us (4%)
    ppermute x8, waiting for transfers between devices, passed_along(): lax.ppermute(shard, axis, [(i, (i + by) % count) for i in range(count)])  30 us
    ppermute x8, starting transfers between devices, passed_along(): lax.ppermute(shard, axis, [(i, (i + by) % count) for i in range(count)])  14.9 us
    pallas_call x5, Pallas kernels, called(): pl.pallas_call(kernel, in_specs=more.get('in_specs', [whole_vmem()] * len...  11 us
    ppermute x6, waiting for transfers between devices, exchanged(): got.append(lax.ppermute(pieces[c], 'dp', to))  8.55 us
    ppermute x6, starting transfers between devices, exchanged(): got.append(lax.ppermute(pieces[c], 'dp', to))  7.11 us
    pallas_call x3, Pallas kernels, finished(): pl.pallas_call(functools.partial(finish_kernel, parts, places), in_specs=...  2.55 us
    unnamed x6, local copies, waits for them, and re-layouts  2.09 us
  transfers between devices with their start and end apart: 15, of which 5 were waited for; matrix products, arithmetic and copies ran while one was open for 1% of the time, Pallas kernels for 16%

profile of v6, /device:TPU:0, one launch (start us, length us, event | category | flops | bytes accessed | tf_op | source)
XLA Modules:
  0.0 79.2 jit_solution(1161998108104137401)
XLA Ops:
  0.6 3.1 %collective-permute-start = (bf16[64,4096]{1,0:T(8,128)(2,1)}, bf16[64,4096]{1,0:T(8,128)(2,1)S(1)}, u32[]{:S(2)}, u32[]{:S(2)}) collective-permute-start(bf16[64,4096]{1,0:T(8,128)(2,1)} %bitcast.26), channel_id=1, source_target_pairs={{0,8},{8,16},{16,24},{24,0},{1,9},{9,17},{17,25},{25,1},{2,10},{10... | collective-permute-start | bytes 1572872 | tf_op jit(solution)/shard_map/ppermute | solution.py:25
  3.7 1.0 %copy-done = bf16[1,64,4096]{2,1,0:T(8,128)(2,1)S(1)} copy-done((bf16[1,64,4096]{2,1,0:T(8,128)(2,1)S(1)}, bf16[1,64,4096]{2,1,0:T(8,128)(2,1)}, u32[]{:S(2)}) %copy-start) | copy-done | bytes 524312
  4.8 1.0 %copy-done.1 = bf16[1,64,4096]{2,1,0:T(8,128)(2,1)S(1)} copy-done((bf16[1,64,4096]{2,1,0:T(8,128)(2,1)S(1)}, bf16[1,64,4096]{2,1,0:T(8,128)(2,1)}, u32[]{:S(2)}) %copy-start.1) | copy-done | bytes 524312
  5.8 0.3 group_sums.1
  6.1 2.1 %collective-permute-start.1 = (bf16[1,16,4096]{2,1,0:T(8,128)(2,1)S(1)}, bf16[1,16,4096]{2,1,0:T(8,128)(2,1)S(1)}, u32[]{:S(2)}, u32[]{:S(2)}) collective-permute-start(bf16[1,16,4096]{2,1,0:T(8,128)(2,1)S(1)} %get-tuple-element.26), channel_id=1, source_target_pairs={{0,24},{8,0},{16,8},{24,16},{1,25},{9,1},{17,9},{25,17},{2,26},{10... | collective-permute-start | bytes 393224 | tf_op jit(solution)/shard_map/ppermute | solution.py:25
  8.2 2.0 %collective-permute-start.2 = (bf16[3,16,512]{2,1,0:T(8,128)(2,1)S(1)}, bf16[3,16,512]{2,1,0:T(8,128)(2,1)S(1)}, u32[]{:S(2)}, u32[]{:S(2)}) collective-permute-start(bf16[3,16,512]{2,1,0:T(8,128)(2,1)S(1)} %get-tuple-element.27), channel_id=1, source_target_pairs={{0,24},{8,0},{16,8},{24,16},{1,25},{9,1},{17,9},{25,17},{2,26},{10... | collective-permute-start | bytes 147464 | tf_op jit(solution)/shard_map/ppermute | solution.py:25
  10.2 3.8 %collective-permute-start.3 = (bf16[64,4096]{1,0:T(8,128)(2,1)}, bf16[64,4096]{1,0:T(8,128)(2,1)S(1)}, u32[]{:S(2)}, u32[]{:S(2)}) collective-permute-start(bf16[64,4096]{1,0:T(8,128)(2,1)} %bitcast.27), channel_id=1, source_target_pairs={{0,24},{8,0},{16,8},{24,16},{1,25},{9,1},{17,9},{25,17},{2,26},{10... | collective-permute-start | bytes 1572872 | tf_op jit(solution)/shard_map/ppermute | solution.py:25
  14.0 0.8 slice_bitcast_fusion
  14.8 7.8 %collective-permute-done.2.sums_ref = bf16[3,16,512]{2,1,0:T(8,128)(2,1)S(1)} collective-permute-done((bf16[3,16,512]{2,1,0:T(8,128)(2,1)S(1)}, bf16[3,16,512]{2,1,0:T(8,128)(2,1)S(1)}, u32[]{:S(2)}, u32[]{:S(2)}) %collective-permute-start.2) | collective-permute-done | bytes 49184 | tf_op jit(solution)/shard_map/ppermute | solution.py:25
  22.6 0.3 shard_map.101
  22.9 1.6 %collective-permute-start.11 = (bf16[3,64,512]{2,1,0:T(8,128)(2,1)S(1)}, bf16[3,64,512]{2,1,0:T(8,128)(2,1)S(1)}, u32[]{:S(2)}, u32[]{:S(2)}) collective-permute-start(bf16[3,64,512]{2,1,0:T(8,128)(2,1)S(1)} %get-tuple-element.42), channel_id=1, source_target_pairs={{0,2},{1,3},{2,0},{3,1},{4,6},{5,7},{6,4},{7,5},{8,10},{9,11},{10,... | collective-permute-start | bytes 589832 | tf_op jit(solution)/shard_map/ppermute | solution.py:412
  24.5 1.5 %collective-permute-start.12 = (bf16[3,64,512]{2,1,0:T(8,128)(2,1)S(1)}, bf16[3,64,512]{2,1,0:T(8,128)(2,1)S(1)}, u32[]{:S(2)}, u32[]{:S(2)}) collective-permute-start(bf16[3,64,512]{2,1,0:T(8,128)(2,1)S(1)} %get-tuple-element.43), channel_id=1, source_target_pairs={{0,4},{1,5},{2,6},{3,7},{4,0},{5,1},{6,2},{7,3},{8,12},{9,13},{10,... | collective-permute-start | bytes 589832 | tf_op jit(solution)/shard_map/ppermute | solution.py:412
  26.0 0.5 collective-permute-start.13
  26.5 7.9 %collective-permute-done.3.x_ref = bf16[64,4096]{1,0:T(8,128)(2,1)S(1)} collective-permute-done((bf16[64,4096]{1,0:T(8,128)(2,1)}, bf16[64,4096]{1,0:T(8,128)(2,1)S(1)}, u32[]{:S(2)}, u32[]{:S(2)}) %collective-permute-start.3) | collective-permute-done | bytes 524320 | tf_op jit(solution)/shard_map/ppermute | solution.py:25
  34.4 0.1 broadcast_in_dim.31.match_ref
  34.5 0.2 shard_map.103
  34.7 2.5 %collective-permute-start.10 = (bf16[3,64,512]{2,1,0:T(8,128)(2,1)S(1)}, bf16[3,64,512]{2,1,0:T(8,128)(2,1)S(1)}, u32[]{:S(2)}, u32[]{:S(2)}) collective-permute-start(bf16[3,64,512]{2,1,0:T(8,128)(2,1)S(1)} %get-tuple-element.40), channel_id=1, source_target_pairs={{0,6},{1,7},{2,4},{3,5},{4,2},{5,3},{6,0},{7,1},{8,14},{9,15},{10,... | collective-permute-start | bytes 589832 | tf_op jit(solution)/shard_map/ppermute | solution.py:412
  37.2 0.5 collective-permute-start.8
  37.8 0.5 collective-permute-start.9
  38.3 5.2 %collective-permute-done.10.refs_3_ = bf16[3,64,512]{2,1,0:T(8,128)(2,1)S(1)} collective-permute-done((bf16[3,64,512]{2,1,0:T(8,128)(2,1)S(1)}, bf16[3,64,512]{2,1,0:T(8,128)(2,1)S(1)}, u32[]{:S(2)}, u32[]{:S(2)}) %collective-permute-start.10) | collective-permute-done | bytes 196640 | tf_op jit(solution)/shard_map/ppermute | solution.py:412
  43.5 3.3 %collective-permute-done.8.refs_1_ = bf16[3,64,512]{2,1,0:T(8,128)(2,1)S(1)} collective-permute-done((bf16[3,64,512]{2,1,0:T(8,128)(2,1)S(1)}, bf16[3,64,512]{2,1,0:T(8,128)(2,1)S(1)}, u32[]{:S(2)}, u32[]{:S(2)}) %collective-permute-start.8) | collective-permute-done | bytes 196640 | tf_op jit(solution)/shard_map/ppermute | solution.py:412
  46.8 0.8 shard_map.105
  47.6 0.1 collective-permute-start.14
  47.7 0.6 collective-permute-start.7
  48.3 3.3 %collective-permute-start.5 = (bf16[2,16,4096]{2,1,0:T(8,128)(2,1)S(1)}, bf16[2,16,4096]{2,1,0:T(8,128)(2,1)S(1)}, u32[]{:S(2)}, u32[]{:S(2)}) collective-permute-start(bf16[2,16,4096]{2,1,0:T(8,128)(2,1)S(1)} %get-tuple-element.34), channel_id=1, source_target_pairs={{0,24},{8,0},{16,8},{24,16},{1,25},{9,1},{17,9},{25,17},{2,26},{10... | collective-permute-start | bytes 786440 | tf_op jit(solution)/shard_map/ppermute | solution.py:25
  51.6 4.9 %shard_map.102 = (bf16[64,4096]{1,0:T(8,128)(2,1)}, f32[64,4096]{1,0:T(8,128)S(1)}) custom-call(bf16[64,4096]{1,0:T(8,128)(2,1)S(1)} %collective-permute-done.x_ref, bf16[64,512]{1,0:T(8,128)(2,1)S(1)} %get-tuple-element.28.grouped_ref, bf16[4096,512]{1,0:T(8,128)(2,1)} %bitcast.21), custom_call_target="tpu_custom_call" | custom-call | flops 536870912 | bytes 6356992 | tf_op jit(solution)/shard_map/pallas_call | solution.py:34
  56.4 14.2 %collective-permute-done.6.refs_1_ = bf16[1,16,4096]{2,1,0:T(8,128)(2,1)S(1)} collective-permute-done((bf16[1,16,4096]{2,1,0:T(8,128)(2,1)S(1)}, bf16[1,16,4096]{2,1,0:T(8,128)(2,1)S(1)}, u32[]{:S(2)}, u32[]{:S(2)}) %collective-permute-start.6) | collective-permute-done | bytes 131104 | tf_op jit(solution)/shard_map/ppermute | solution.py:25
  70.7 0.8 %finished.3.refs_1_ = bf16[64,4096]{1,0:T(8,128)(2,1)} custom-call(s32[2,2,128]{2,1,0:T(2,128)S(1)} %broadcast_in_dim.14.match_ref, f32[64,4096]{1,0:T(8,128)S(1)} %get-tuple-element.33.through_ref, bf16[1,16,4096]{2,1,0:T(8,128)(2,1)S(1)} %collective-permute-done.1.first_ref.refs_0_, bf16[1,16,4096]{2,1,0:T(8,128)(2,1)S(1)} %collective-permute-done.6.refs_1_), custom_call_target="tpu_custom_call" | custom-call | flops 262144 | bytes 1048576 | tf_op jit(solution)/shard_map/finished/pallas_call | solution.py:361
  71.5 0.8 %finished.4 = bf16[64,4096]{1,0:T(8,128)(2,1)} custom-call(s32[2,2,128]{2,1,0:T(2,128)S(1)} %broadcast_in_dim.14.match_ref, f32[64,4096]{1,0:T(8,128)S(1)} %get-tuple-element.33.through_ref, bf16[2,16,4096]{2,1,0:T(8,128)(2,1)S(1)} %collective-permute-done.5.refs_0_, bf16[64,4096]{1,0:T(8,128)(2,1)} %finished.3.refs_1_), custom_call_target="tpu_custom_call", output_to_operand_aliasing={{}: (3, {})} | custom-call | flops 262144 | bytes 1048576 | tf_op jit(solution)/shard_map/finished/pallas_call | solution.py:361
  72.3 4.9 %shard_map.104 = (bf16[64,4096]{1,0:T(8,128)(2,1)}, f32[64,4096]{1,0:T(8,128)S(1)}) custom-call(bf16[64,4096]{1,0:T(8,128)(2,1)S(1)} %collective-permute-done.3.x_ref, bf16[64,512]{1,0:T(8,128)(2,1)S(1)} %get-tuple-element.31.grouped_ref, bf16[4096,512]{1,0:T(8,128)(2,1)} %bitcast.22), custom_call_target="tpu_custom_call" | custom-call | flops 536870912 | bytes 6356992 | tf_op jit(solution)/shard_map/pallas_call | solution.py:34
  77.2 0.9 %finished.5 = bf16[64,4096]{1,0:T(8,128)(2,1)} custom-call(s32[2,2,128]{2,1,0:T(2,128)S(1)} %broadcast_in_dim.31.match_ref, f32[64,4096]{1,0:T(8,128)S(1)} %get-tuple-element.36.through_ref, bf16[4,16,4096]{2,1,0:T(8,128)(2,1)S(1)} %bitcast.16), custom_call_target="tpu_custom_call" | custom-call | flops 524288 | bytes 2097152 | tf_op jit(solution)/shard_map/finished/pallas_call | solution.py:361
  78.2 1.0 %combine.1 = f32[512,512]{1,0:T(8,128)} custom-call(f32[512,512]{1,0:T(8,128)S(1)} %get-tuple-element.45.keep_ref, f32[512,512]{1,0:T(8,128)S(1)} %collective-permute-done.14.got_ref), custom_call_target="tpu_custom_call" | custom-call | flops 524288 | bytes 3145728 | tf_op jit(solution)/shard_map/combine/pallas_call | solution.py:244
  (19 shorter events, 0.2 us)
Async XLA Ops:
  0.6 21.9 %collective-permute-start = (bf16[64,4096]{1,0:T(8,128)(2,1)}, bf16[64,4096]{1,0:T(8,128)(2,1)S(1)}, u32[]{:S(2)}, u32[]{:S(2)}) collective-permute-start(bf16[64,4096]{1,0:T(8,128)(2,1)} %bitcast.26), channel_id=1, source_target_pairs={{0,8},{8,16},{16,24},{24,0},{1,9},{9,17},{17,25},{25,1},{2,10},{10... | collective-permute-start | bytes 1572872 | tf_op jit(solution)/shard_map/ppermute | solution.py:25
  3.7 1.0 %copy-start = (bf16[1,64,4096]{2,1,0:T(8,128)(2,1)S(1)}, bf16[1,64,4096]{2,1,0:T(8,128)(2,1)}, u32[]{:S(2)}) copy-start(bf16[1,64,4096]{2,1,0:T(8,128)(2,1)} %param.8) | copy-start | bytes 1572868
  4.8 1.0 %copy-start.1 = (bf16[1,64,4096]{2,1,0:T(8,128)(2,1)S(1)}, bf16[1,64,4096]{2,1,0:T(8,128)(2,1)}, u32[]{:S(2)}) copy-start(bf16[1,64,4096]{2,1,0:T(8,128)(2,1)} %param.9) | copy-start | bytes 1572868
  5.8 41.8 %copy-start.2 = (bf16[1,64,4096]{2,1,0:T(8,128)(2,1)S(1)}, bf16[1,64,4096]{2,1,0:T(8,128)(2,1)}, u32[]{:S(2)}) copy-start(bf16[1,64,4096]{2,1,0:T(8,128)(2,1)} %param.9) | copy-start | bytes 1572868
  6.1 16.5 %collective-permute-start.1 = (bf16[1,16,4096]{2,1,0:T(8,128)(2,1)S(1)}, bf16[1,16,4096]{2,1,0:T(8,128)(2,1)S(1)}, u32[]{:S(2)}, u32[]{:S(2)}) collective-permute-start(bf16[1,16,4096]{2,1,0:T(8,128)(2,1)S(1)} %get-tuple-element.26), channel_id=1, source_target_pairs={{0,24},{8,0},{16,8},{24,16},{1,25},{9,1},{17,9},{25,17},{2,26},{10... | collective-permute-start | bytes 393224 | tf_op jit(solution)/shard_map/ppermute | solution.py:25
  8.2 14.4 %collective-permute-start.2 = (bf16[3,16,512]{2,1,0:T(8,128)(2,1)S(1)}, bf16[3,16,512]{2,1,0:T(8,128)(2,1)S(1)}, u32[]{:S(2)}, u32[]{:S(2)}) collective-permute-start(bf16[3,16,512]{2,1,0:T(8,128)(2,1)S(1)} %get-tuple-element.27), channel_id=1, source_target_pairs={{0,24},{8,0},{16,8},{24,16},{1,25},{9,1},{17,9},{25,17},{2,26},{10... | collective-permute-start | bytes 147464 | tf_op jit(solution)/shard_map/ppermute | solution.py:25
  10.2 16.3 %collective-permute-start.4 = (bf16[64,512]{1,0:T(8,128)(2,1)S(1)}, bf16[64,512]{1,0:T(8,128)(2,1)S(1)}, u32[]{:S(2)}, u32[]{:S(2)}) collective-permute-start(bf16[64,512]{1,0:T(8,128)(2,1)S(1)} %get-tuple-element.30), channel_id=1, source_target_pairs={{0,8},{8,16},{16,24},{24,0},{1,9},{9,17},{17,25},{25,1},{2,10},{10... | collective-permute-start | bytes 196616 | tf_op jit(solution)/shard_map/ppermute | solution.py:25
  10.2 24.2 %collective-permute-start.3 = (bf16[64,4096]{1,0:T(8,128)(2,1)}, bf16[64,4096]{1,0:T(8,128)(2,1)S(1)}, u32[]{:S(2)}, u32[]{:S(2)}) collective-permute-start(bf16[64,4096]{1,0:T(8,128)(2,1)} %bitcast.27), channel_id=1, source_target_pairs={{0,24},{8,0},{16,8},{24,16},{1,25},{9,1},{17,9},{25,17},{2,26},{10... | collective-permute-start | bytes 1572872 | tf_op jit(solution)/shard_map/ppermute | solution.py:25
  22.9 14.9 %collective-permute-start.11 = (bf16[3,64,512]{2,1,0:T(8,128)(2,1)S(1)}, bf16[3,64,512]{2,1,0:T(8,128)(2,1)S(1)}, u32[]{:S(2)}, u32[]{:S(2)}) collective-permute-start(bf16[3,64,512]{2,1,0:T(8,128)(2,1)S(1)} %get-tuple-element.42), channel_id=1, source_target_pairs={{0,2},{1,3},{2,0},{3,1},{4,6},{5,7},{6,4},{7,5},{8,10},{9,11},{10,... | collective-permute-start | bytes 589832 | tf_op jit(solution)/shard_map/ppermute | solution.py:412
  24.5 13.8 %collective-permute-start.12 = (bf16[3,64,512]{2,1,0:T(8,128)(2,1)S(1)}, bf16[3,64,512]{2,1,0:T(8,128)(2,1)S(1)}, u32[]{:S(2)}, u32[]{:S(2)}) collective-permute-start(bf16[3,64,512]{2,1,0:T(8,128)(2,1)S(1)} %get-tuple-element.43), channel_id=1, source_target_pairs={{0,4},{1,5},{2,6},{3,7},{4,0},{5,1},{6,2},{7,3},{8,12},{9,13},{10,... | collective-permute-start | bytes 589832 | tf_op jit(solution)/shard_map/ppermute | solution.py:412
  26.0 12.3 %collective-permute-start.13 = (bf16[3,64,512]{2,1,0:T(8,128)(2,1)S(1)}, bf16[3,64,512]{2,1,0:T(8,128)(2,1)S(1)}, u32[]{:S(2)}, u32[]{:S(2)}) collective-permute-start(bf16[3,64,512]{2,1,0:T(8,128)(2,1)S(1)} %get-tuple-element.44), channel_id=1, source_target_pairs={{0,6},{1,7},{2,4},{3,5},{4,2},{5,3},{6,0},{7,1},{8,14},{9,15},{10,... | collective-permute-start | bytes 589832 | tf_op jit(solution)/shard_map/ppermute | solution.py:412
  34.7 8.8 %collective-permute-start.10 = (bf16[3,64,512]{2,1,0:T(8,128)(2,1)S(1)}, bf16[3,64,512]{2,1,0:T(8,128)(2,1)S(1)}, u32[]{:S(2)}, u32[]{:S(2)}) collective-permute-start(bf16[3,64,512]{2,1,0:T(8,128)(2,1)S(1)} %get-tuple-element.40), channel_id=1, source_target_pairs={{0,6},{1,7},{2,4},{3,5},{4,2},{5,3},{6,0},{7,1},{8,14},{9,15},{10,... | collective-permute-start | bytes 589832 | tf_op jit(solution)/shard_map/ppermute | solution.py:412
  37.2 9.6 %collective-permute-start.8 = (bf16[3,64,512]{2,1,0:T(8,128)(2,1)S(1)}, bf16[3,64,512]{2,1,0:T(8,128)(2,1)S(1)}, u32[]{:S(2)}, u32[]{:S(2)}) collective-permute-start(bf16[3,64,512]{2,1,0:T(8,128)(2,1)S(1)} %get-tuple-element.38), channel_id=1, source_target_pairs={{0,2},{1,3},{2,0},{3,1},{4,6},{5,7},{6,4},{7,5},{8,10},{9,11},{10,... | collective-permute-start | bytes 589832 | tf_op jit(solution)/shard_map/ppermute | solution.py:412
  37.8 9.1 %collective-permute-start.9 = (bf16[3,64,512]{2,1,0:T(8,128)(2,1)S(1)}, bf16[3,64,512]{2,1,0:T(8,128)(2,1)S(1)}, u32[]{:S(2)}, u32[]{:S(2)}) collective-permute-start(bf16[3,64,512]{2,1,0:T(8,128)(2,1)S(1)} %get-tuple-element.39), channel_id=1, source_target_pairs={{0,4},{1,5},{2,6},{3,7},{4,0},{5,1},{6,2},{7,3},{8,12},{9,13},{10,... | collective-permute-start | bytes 589832 | tf_op jit(solution)/shard_map/ppermute | solution.py:412
  47.6 30.6 %collective-permute-start.14 = (f32[512,512]{1,0:T(8,128)S(1)}, f32[512,512]{1,0:T(8,128)S(1)}, u32[]{:S(2)}, u32[]{:S(2)}) collective-permute-start(f32[512,512]{1,0:T(8,128)S(1)} %get-tuple-element.46), channel_id=1, source_target_pairs={{0,1},{1,0},{2,3},{3,2},{4,5},{5,4},{6,7},{7,6},{8,9},{9,8},{10,11... | collective-permute-start | bytes 3145736 | tf_op jit(solution)/shard_map/ppermute | solution.py:430
  47.7 29.6 %collective-permute-start.7 = (bf16[64,4096]{1,0:T(8,128)(2,1)S(1)}, bf16[64,4096]{1,0:T(8,128)(2,1)S(1)}, u32[]{:S(2)}, u32[]{:S(2)}) collective-permute-start(bf16[64,4096]{1,0:T(8,128)(2,1)S(1)} %bitcast.19), channel_id=1, source_target_pairs={{0,8},{8,16},{16,24},{24,0},{1,9},{9,17},{17,25},{25,1},{2,10},{10... | collective-permute-start | bytes 1572872 | tf_op jit(solution)/shard_map/ppermute | solution.py:25
  48.3 23.2 %collective-permute-start.5 = (bf16[2,16,4096]{2,1,0:T(8,128)(2,1)S(1)}, bf16[2,16,4096]{2,1,0:T(8,128)(2,1)S(1)}, u32[]{:S(2)}, u32[]{:S(2)}) collective-permute-start(bf16[2,16,4096]{2,1,0:T(8,128)(2,1)S(1)} %get-tuple-element.34), channel_id=1, source_target_pairs={{0,24},{8,0},{16,8},{24,16},{1,25},{9,1},{17,9},{25,17},{2,26},{10... | collective-permute-start | bytes 786440 | tf_op jit(solution)/shard_map/ppermute | solution.py:25
  51.5 19.1 %collective-permute-start.6 = (bf16[1,16,4096]{2,1,0:T(8,128)(2,1)S(1)}, bf16[1,16,4096]{2,1,0:T(8,128)(2,1)S(1)}, u32[]{:S(2)}, u32[]{:S(2)}) collective-permute-start(bf16[1,16,4096]{2,1,0:T(8,128)(2,1)S(1)} %get-tuple-element.35), channel_id=1, source_target_pairs={{0,24},{8,0},{16,8},{24,16},{1,25},{9,1},{17,9},{25,17},{2,26},{10... | collective-permute-start | bytes 393224 | tf_op jit(solution)/shard_map/ppermute | solution.py:25

commit v7 on v6

--- a/solution.py
+++ b/solution.py
@@ -59,18 +59,12 @@
 ):
     block = pl.program_id(0)
     part = pl.program_id(1)
-    opening = (part == 0) & (block == 0)
     for k, total in enumerate(group_sum(lambda at: early_ref[:, at : at + HD])):
         early_out[:, k * HD : (k + 1) * HD] = total.astype(early_out.dtype)
 
-    @pl.when(opening)
+    @pl.when((part == 0) & (block == 0))
     def _():
         first_out[0] = late_ref[...]
-
-    @pl.when(jnp.logical_not(opening))
-    def _():
-        for k, total in enumerate(group_sum(lambda at: late_ref[:, at : at + HD])):
-            late_out[0, :, k * HD : (k + 1) * HD] = total.astype(late_out.dtype)
 
     @pl.when((part == 0) & (block > 0))
     def _():
@@ -79,6 +73,8 @@
     @pl.when(part == 1)
     def _():
         second_out[0] = late_ref[...]
+        for k, total in enumerate(group_sum(lambda at: late_ref[:, at : at + HD])):
+            late_out[0, :, k * HD : (k + 1) * HD] = total.astype(late_out.dtype)
 
 
 def group_sums(early, late, blocks):
@@ -87,7 +83,7 @@
     step = rows // blocks // 2
     wide = pl.BlockSpec((step, width), lambda j, i: (2 * j + i, 0))
     narrow = pl.BlockSpec((step, inner), lambda j, i: (2 * j + i, 0))
-    later = pl.BlockSpec((1, step, inner), lambda j, i: (jnp.maximum(2 * j + i - 1, 0), 0, 0))
+    later = pl.BlockSpec((1, step, inner), lambda j, i: (j, 0, 0))
     shape = (1, step, width)
     first = pl.BlockSpec(shape, lambda j, i: (0, 0, 0))
     rest = pl.BlockSpec(shape, lambda j, i: (jnp.maximum(j - 1, 0), 0, 0))
@@ -99,7 +95,7 @@
         out_specs=[narrow, later, first, rest, second],
         out_shape=[
             jax.ShapeDtypeStruct((rows, inner), early.dtype),
-            jax.ShapeDtypeStruct((2 * blocks - 1, step, inner), late.dtype),
+            jax.ShapeDtypeStruct((blocks, step, inner), late.dtype),
         ]
         + [
             jax.ShapeDtypeStruct((count, step, width), late.dtype)
@@ -159,20 +155,23 @@
         write_grouped(m * rows, value, own, grouped_ref, pieces)
 
 
-def late_pieces_kernel(chips, x_ref, match_ref, first_ref, sums_ref, grouped_ref, *pieces):
+def late_pieces_kernel(
+    chips, x_ref, match_ref, first_ref, rest_ref, sums_ref, grouped_ref, *pieces
+):
     write_normed(chips, x_ref, pieces)
     half = first_ref.shape[1]
     blocks = match_ref.shape[0]
     own = x_ref.shape[1] // chips // pieces[0].shape[-1]
-    first = group_sum(lambda at: first_ref[0, :, at : at + HD])
-    first = jnp.concatenate(first, axis=-1).astype(x_ref.dtype)
-
-    def sums_of(at):
-        return first if at == 0 else sums_ref[at - 1]
-
+    raws = [(first_ref, 0)] + [(rest_ref, j) for j in range(blocks - 1)]
+    firsts = []
+    for ref, j in raws:
+        sums = group_sum(lambda at: ref[j, :, at : at + HD])
+        firsts.append(jnp.concatenate(sums, axis=-1).astype(x_ref.dtype))
     for part in range(2):
         for m in range(blocks):
-            value = arranged(match_ref, m, lambda j: sums_of(2 * j + part), blocks)
+            value = arranged(
+                match_ref, m, lambda j: firsts[j] if part == 0 else sums_ref[j], blocks
+            )
             at = (2 * m + part) * half
             write_grouped(at, value.astype(x_ref.dtype), own, grouped_ref, pieces)
 
@@ -419,7 +418,11 @@
     )
     got_early = exchanged(sent_early)
     grouped_late, *sent_late = pieces_of(
-        late_pieces_kernel, x_late, (match_late, raw_late[0], sums_late), inner, members
+        late_pieces_kernel,
+        x_late,
+        (match_late, raw_late[0], raw_late[1], sums_late),
+        inner,
+        members,
     )
     got_late = exchanged(sent_late)
 

time: 79.4 us -> 80.5 us (1.014)
  waiting for transfers between devices: 38.5 us -> 39.7 us
    ppermute x8, waiting for transfers between devices: 30 us -> 31.9 us  [passed_along(): lax.ppermute(shard, axis, [(i, (i + by) % count) for i in range(count)])]
where the time goes in v7:
time: 80.5 us; the launch traced here: 80.3 us
  waiting for transfers between devices  39.7 us (49%)
  starting transfers between devices  22 us (27%)
  Pallas kernels  14.8 us (18%)
  local copies, waits for them, and re-layouts  2.98 us (4%)
    ppermute x8, waiting for transfers between devices, passed_along(): lax.ppermute(shard, axis, [(i, (i + by) % count) for i in range(count)])  31.9 us
    ppermute x8, starting transfers between devices, passed_along(): lax.ppermute(shard, axis, [(i, (i + by) % count) for i in range(count)])  14.8 us
    pallas_call x5, Pallas kernels, called(): pl.pallas_call(kernel, in_specs=more.get('in_specs', [whole_vmem()] * len...  11 us
    ppermute x6, waiting for transfers between devices, exchanged(): got.append(lax.ppermute(pieces[c], 'dp', to))  7.8 us
    ppermute x6, starting transfers between devices, exchanged(): got.append(lax.ppermute(pieces[c], 'dp', to))  7.11 us
    pallas_call x3, Pallas kernels, finished(): pl.pallas_call(functools.partial(finish_kernel, parts, places), in_specs=...  2.54 us
    unnamed x6, local copies, waits for them, and re-layouts  2.09 us
  transfers between devices with their start and end apart: 15, of which 5 were waited for; matrix products, arithmetic and copies ran while one was open for 1% of the time, Pallas kernels for 16%

profile of v7, /device:TPU:0, one launch (start us, length us, event | category | flops | bytes accessed | tf_op | source)
XLA Modules:
  0.0 80.3 jit_solution(6900275435032002748)
XLA Ops:
  0.6 3.1 %collective-permute-start = (bf16[64,4096]{1,0:T(8,128)(2,1)}, bf16[64,4096]{1,0:T(8,128)(2,1)S(1)}, u32[]{:S(2)}, u32[]{:S(2)}) collective-permute-start(bf16[64,4096]{1,0:T(8,128)(2,1)} %bitcast.26), channel_id=1, source_target_pairs={{0,8},{8,16},{16,24},{24,0},{1,9},{9,17},{17,25},{25,1},{2,10},{10... | collective-permute-start | bytes 1572872 | tf_op jit(solution)/shard_map/ppermute | solution.py:25
  3.7 1.0 %copy-done = bf16[1,64,4096]{2,1,0:T(8,128)(2,1)S(1)} copy-done((bf16[1,64,4096]{2,1,0:T(8,128)(2,1)S(1)}, bf16[1,64,4096]{2,1,0:T(8,128)(2,1)}, u32[]{:S(2)}) %copy-start) | copy-done | bytes 524312
  4.8 1.0 %copy-done.1 = bf16[1,64,4096]{2,1,0:T(8,128)(2,1)S(1)} copy-done((bf16[1,64,4096]{2,1,0:T(8,128)(2,1)S(1)}, bf16[1,64,4096]{2,1,0:T(8,128)(2,1)}, u32[]{:S(2)}) %copy-start.1) | copy-done | bytes 524312
  5.8 0.2 group_sums.1
  6.1 2.1 %collective-permute-start.1 = (bf16[1,16,4096]{2,1,0:T(8,128)(2,1)S(1)}, bf16[1,16,4096]{2,1,0:T(8,128)(2,1)S(1)}, u32[]{:S(2)}, u32[]{:S(2)}) collective-permute-start(bf16[1,16,4096]{2,1,0:T(8,128)(2,1)S(1)} %get-tuple-element.26), channel_id=1, source_target_pairs={{0,24},{8,0},{16,8},{24,16},{1,25},{9,1},{17,9},{25,17},{2,26},{10... | collective-permute-start | bytes 393224 | tf_op jit(solution)/shard_map/ppermute | solution.py:25
  8.2 2.0 %collective-permute-start.2 = (bf16[1,16,4096]{2,1,0:T(8,128)(2,1)S(1)}, bf16[1,16,4096]{2,1,0:T(8,128)(2,1)S(1)}, u32[]{:S(2)}, u32[]{:S(2)}) collective-permute-start(bf16[1,16,4096]{2,1,0:T(8,128)(2,1)S(1)} %get-tuple-element.27), channel_id=1, source_target_pairs={{0,24},{8,0},{16,8},{24,16},{1,25},{9,1},{17,9},{25,17},{2,26},{10... | collective-permute-start | bytes 393224 | tf_op jit(solution)/shard_map/ppermute | solution.py:25
  10.2 0.4 collective-permute-start.3
  10.6 0.4 collective-permute-start.4
  11.1 0.8 slice_bitcast_fusion
  11.8 12.5 %collective-permute-done.3.sums_ref = bf16[2,16,512]{2,1,0:T(8,128)(2,1)S(1)} collective-permute-done((bf16[2,16,512]{2,1,0:T(8,128)(2,1)S(1)}, bf16[2,16,512]{2,1,0:T(8,128)(2,1)S(1)}, u32[]{:S(2)}, u32[]{:S(2)}) %collective-permute-start.3) | collective-permute-done | bytes 32800 | tf_op jit(solution)/shard_map/ppermute | solution.py:25
  24.3 0.6 collective-permute-start.5
  25.0 0.3 shard_map.101
  25.2 1.6 %collective-permute-start.11 = (bf16[3,64,512]{2,1,0:T(8,128)(2,1)S(1)}, bf16[3,64,512]{2,1,0:T(8,128)(2,1)S(1)}, u32[]{:S(2)}, u32[]{:S(2)}) collective-permute-start(bf16[3,64,512]{2,1,0:T(8,128)(2,1)S(1)} %get-tuple-element.42), channel_id=1, source_target_pairs={{0,2},{1,3},{2,0},{3,1},{4,6},{5,7},{6,4},{7,5},{8,10},{9,11},{10,... | collective-permute-start | bytes 589832 | tf_op jit(solution)/shard_map/ppermute | solution.py:411
  26.8 1.5 %collective-permute-start.12 = (bf16[3,64,512]{2,1,0:T(8,128)(2,1)S(1)}, bf16[3,64,512]{2,1,0:T(8,128)(2,1)S(1)}, u32[]{:S(2)}, u32[]{:S(2)}) collective-permute-start(bf16[3,64,512]{2,1,0:T(8,128)(2,1)S(1)} %get-tuple-element.43), channel_id=1, source_target_pairs={{0,4},{1,5},{2,6},{3,7},{4,0},{5,1},{6,2},{7,3},{8,12},{9,13},{10,... | collective-permute-start | bytes 589832 | tf_op jit(solution)/shard_map/ppermute | solution.py:411
  28.3 0.5 collective-permute-start.13
  28.8 8.1 %collective-permute-done.5 = bf16[64,512]{1,0:T(8,128)(2,1)S(1)} collective-permute-done((bf16[64,512]{1,0:T(8,128)(2,1)S(1)}, bf16[64,512]{1,0:T(8,128)(2,1)S(1)}, u32[]{:S(2)}, u32[]{:S(2)}) %collective-permute-start.5) | collective-permute-done | bytes 65568 | tf_op jit(solution)/shard_map/ppermute | solution.py:25
  37.0 0.2 shard_map.103
  37.2 2.5 %collective-permute-start.10 = (bf16[3,64,512]{2,1,0:T(8,128)(2,1)S(1)}, bf16[3,64,512]{2,1,0:T(8,128)(2,1)S(1)}, u32[]{:S(2)}, u32[]{:S(2)}) collective-permute-start(bf16[3,64,512]{2,1,0:T(8,128)(2,1)S(1)} %get-tuple-element.40), channel_id=1, source_target_pairs={{0,6},{1,7},{2,4},{3,5},{4,2},{5,3},{6,0},{7,1},{8,14},{9,15},{10,... | collective-permute-start | bytes 589832 | tf_op jit(solution)/shard_map/ppermute | solution.py:411
  39.7 0.5 collective-permute-start.8
  40.3 0.5 collective-permute-start.9
  40.8 5.2 %collective-permute-done.10.refs_3_ = bf16[3,64,512]{2,1,0:T(8,128)(2,1)S(1)} collective-permute-done((bf16[3,64,512]{2,1,0:T(8,128)(2,1)S(1)}, bf16[3,64,512]{2,1,0:T(8,128)(2,1)S(1)}, u32[]{:S(2)}, u32[]{:S(2)}) %collective-permute-start.10) | collective-permute-done | bytes 196640 | tf_op jit(solution)/shard_map/ppermute | solution.py:411
  46.0 2.6 %collective-permute-done.8.refs_1_ = bf16[3,64,512]{2,1,0:T(8,128)(2,1)S(1)} collective-permute-done((bf16[3,64,512]{2,1,0:T(8,128)(2,1)S(1)}, bf16[3,64,512]{2,1,0:T(8,128)(2,1)S(1)}, u32[]{:S(2)}, u32[]{:S(2)}) %collective-permute-start.8) | collective-permute-done | bytes 196640 | tf_op jit(solution)/shard_map/ppermute | solution.py:411
  48.6 0.7 shard_map.105
  49.4 0.6 collective-permute-start.7
  50.0 5.5 %collective-permute-start.6 = (bf16[2,16,4096]{2,1,0:T(8,128)(2,1)S(1)}, bf16[2,16,4096]{2,1,0:T(8,128)(2,1)S(1)}, u32[]{:S(2)}, u32[]{:S(2)}) collective-permute-start(bf16[2,16,4096]{2,1,0:T(8,128)(2,1)S(1)} %get-tuple-element.35), channel_id=1, source_target_pairs={{0,24},{8,0},{16,8},{24,16},{1,25},{9,1},{17,9},{25,17},{2,26},{10... | collective-permute-start | bytes 786440 | tf_op jit(solution)/shard_map/ppermute | solution.py:25
  55.6 4.9 %shard_map.102 = (bf16[64,4096]{1,0:T(8,128)(2,1)}, f32[64,4096]{1,0:T(8,128)S(1)}) custom-call(bf16[64,4096]{1,0:T(8,128)(2,1)S(1)} %collective-permute-done.x_ref, bf16[64,512]{1,0:T(8,128)(2,1)S(1)} %get-tuple-element.29.grouped_ref, bf16[4096,512]{1,0:T(8,128)(2,1)} %bitcast.21), custom_call_target="tpu_custom_call" | custom-call | flops 536870912 | bytes 6356992 | tf_op jit(solution)/shard_map/pallas_call | solution.py:34
  60.4 0.8 %finished.3.refs_1_ = bf16[64,4096]{1,0:T(8,128)(2,1)} custom-call(s32[2,2,128]{2,1,0:T(2,128)S(1)} %broadcast_in_dim.14.match_ref, f32[64,4096]{1,0:T(8,128)S(1)} %get-tuple-element.34.through_ref, bf16[1,16,4096]{2,1,0:T(8,128)(2,1)S(1)} %collective-permute-done.1.first_ref.refs_0_, bf16[1,16,4096]{2,1,0:T(8,128)(2,1)S(1)} %collective-permute-done.2.rest_ref.refs_1_), custom_call_target="tpu_custom_call" | custom-call | flops 262144 | bytes 1048576 | tf_op jit(solution)/shard_map/finished/pallas_call | solution.py:360
  61.2 11.3 %collective-permute-done.6.refs_0_ = bf16[2,16,4096]{2,1,0:T(8,128)(2,1)S(1)} collective-permute-done((bf16[2,16,4096]{2,1,0:T(8,128)(2,1)S(1)}, bf16[2,16,4096]{2,1,0:T(8,128)(2,1)S(1)}, u32[]{:S(2)}, u32[]{:S(2)}) %collective-permute-start.6) | collective-permute-done | bytes 262176 | tf_op jit(solution)/shard_map/ppermute | solution.py:25
  72.6 0.8 %finished.4 = bf16[64,4096]{1,0:T(8,128)(2,1)} custom-call(s32[2,2,128]{2,1,0:T(2,128)S(1)} %broadcast_in_dim.14.match_ref, f32[64,4096]{1,0:T(8,128)S(1)} %get-tuple-element.34.through_ref, bf16[2,16,4096]{2,1,0:T(8,128)(2,1)S(1)} %collective-permute-done.6.refs_0_, bf16[64,4096]{1,0:T(8,128)(2,1)} %finished.3.refs_1_), custom_call_target="tpu_custom_call", output_to_operand_aliasing={{}: (3, {})} | custom-call | flops 262144 | bytes 1048576 | tf_op jit(solution)/shard_map/finished/pallas_call | solution.py:360
  73.4 4.9 %shard_map.104 = (bf16[64,4096]{1,0:T(8,128)(2,1)}, f32[64,4096]{1,0:T(8,128)S(1)}) custom-call(bf16[64,4096]{1,0:T(8,128)(2,1)S(1)} %collective-permute-done.4.x_ref, bf16[64,512]{1,0:T(8,128)(2,1)S(1)} %get-tuple-element.32.grouped_ref, bf16[4096,512]{1,0:T(8,128)(2,1)} %bitcast.22), custom_call_target="tpu_custom_call" | custom-call | flops 536870912 | bytes 6356992 | tf_op jit(solution)/shard_map/pallas_call | solution.py:34
  78.3 0.9 %finished.5 = bf16[64,4096]{1,0:T(8,128)(2,1)} custom-call(s32[2,2,128]{2,1,0:T(2,128)S(1)} %broadcast_in_dim.31.match_ref, f32[64,4096]{1,0:T(8,128)S(1)} %get-tuple-element.36.through_ref, bf16[4,16,4096]{2,1,0:T(8,128)(2,1)S(1)} %bitcast.16), custom_call_target="tpu_custom_call" | custom-call | flops 524288 | bytes 2097152 | tf_op jit(solution)/shard_map/finished/pallas_call | solution.py:360
  79.2 1.0 %combine.1 = f32[512,512]{1,0:T(8,128)} custom-call(f32[512,512]{1,0:T(8,128)S(1)} %get-tuple-element.45.keep_ref, f32[512,512]{1,0:T(8,128)S(1)} %collective-permute-done.14.got_ref), custom_call_target="tpu_custom_call" | custom-call | flops 524288 | bytes 3145728 | tf_op jit(solution)/shard_map/combine/pallas_call | solution.py:243
  (19 shorter events, 0.3 us)
Async XLA Ops:
  0.6 24.3 %collective-permute-start = (bf16[64,4096]{1,0:T(8,128)(2,1)}, bf16[64,4096]{1,0:T(8,128)(2,1)S(1)}, u32[]{:S(2)}, u32[]{:S(2)}) collective-permute-start(bf16[64,4096]{1,0:T(8,128)(2,1)} %bitcast.26), channel_id=1, source_target_pairs={{0,8},{8,16},{16,24},{24,0},{1,9},{9,17},{17,25},{25,1},{2,10},{10... | collective-permute-start | bytes 1572872 | tf_op jit(solution)/shard_map/ppermute | solution.py:25
  3.7 1.0 %copy-start = (bf16[1,64,4096]{2,1,0:T(8,128)(2,1)S(1)}, bf16[1,64,4096]{2,1,0:T(8,128)(2,1)}, u32[]{:S(2)}) copy-start(bf16[1,64,4096]{2,1,0:T(8,128)(2,1)} %param.8) | copy-start | bytes 1572868
  4.8 1.0 %copy-start.1 = (bf16[1,64,4096]{2,1,0:T(8,128)(2,1)S(1)}, bf16[1,64,4096]{2,1,0:T(8,128)(2,1)}, u32[]{:S(2)}) copy-start(bf16[1,64,4096]{2,1,0:T(8,128)(2,1)} %param.9) | copy-start | bytes 1572868
  5.8 43.6 %copy-start.2 = (bf16[1,64,4096]{2,1,0:T(8,128)(2,1)S(1)}, bf16[1,64,4096]{2,1,0:T(8,128)(2,1)}, u32[]{:S(2)}) copy-start(bf16[1,64,4096]{2,1,0:T(8,128)(2,1)} %param.9) | copy-start | bytes 1572868
  6.1 18.8 %collective-permute-start.1 = (bf16[1,16,4096]{2,1,0:T(8,128)(2,1)S(1)}, bf16[1,16,4096]{2,1,0:T(8,128)(2,1)S(1)}, u32[]{:S(2)}, u32[]{:S(2)}) collective-permute-start(bf16[1,16,4096]{2,1,0:T(8,128)(2,1)S(1)} %get-tuple-element.26), channel_id=1, source_target_pairs={{0,24},{8,0},{16,8},{24,16},{1,25},{9,1},{17,9},{25,17},{2,26},{10... | collective-permute-start | bytes 393224 | tf_op jit(solution)/shard_map/ppermute | solution.py:25
  8.2 16.7 %collective-permute-start.2 = (bf16[1,16,4096]{2,1,0:T(8,128)(2,1)S(1)}, bf16[1,16,4096]{2,1,0:T(8,128)(2,1)S(1)}, u32[]{:S(2)}, u32[]{:S(2)}) collective-permute-start(bf16[1,16,4096]{2,1,0:T(8,128)(2,1)S(1)} %get-tuple-element.27), channel_id=1, source_target_pairs={{0,24},{8,0},{16,8},{24,16},{1,25},{9,1},{17,9},{25,17},{2,26},{10... | collective-permute-start | bytes 393224 | tf_op jit(solution)/shard_map/ppermute | solution.py:25
  10.2 14.1 %collective-permute-start.3 = (bf16[2,16,512]{2,1,0:T(8,128)(2,1)S(1)}, bf16[2,16,512]{2,1,0:T(8,128)(2,1)S(1)}, u32[]{:S(2)}, u32[]{:S(2)}) collective-permute-start(bf16[2,16,512]{2,1,0:T(8,128)(2,1)S(1)} %get-tuple-element.28), channel_id=1, source_target_pairs={{0,24},{8,0},{16,8},{24,16},{1,25},{9,1},{17,9},{25,17},{2,26},{10... | collective-permute-start | bytes 98312 | tf_op jit(solution)/shard_map/ppermute | solution.py:25
  10.6 26.3 %collective-permute-start.4 = (bf16[64,4096]{1,0:T(8,128)(2,1)}, bf16[64,4096]{1,0:T(8,128)(2,1)S(1)}, u32[]{:S(2)}, u32[]{:S(2)}) collective-permute-start(bf16[64,4096]{1,0:T(8,128)(2,1)} %bitcast.27), channel_id=1, source_target_pairs={{0,24},{8,0},{16,8},{24,16},{1,25},{9,1},{17,9},{25,17},{2,26},{10... | collective-permute-start | bytes 1572872 | tf_op jit(solution)/shard_map/ppermute | solution.py:25
  24.3 12.6 %collective-permute-start.5 = (bf16[64,512]{1,0:T(8,128)(2,1)S(1)}, bf16[64,512]{1,0:T(8,128)(2,1)S(1)}, u32[]{:S(2)}, u32[]{:S(2)}) collective-permute-start(bf16[64,512]{1,0:T(8,128)(2,1)S(1)} %get-tuple-element.31), channel_id=1, source_target_pairs={{0,8},{8,16},{16,24},{24,0},{1,9},{9,17},{17,25},{25,1},{2,10},{10... | collective-permute-start | bytes 196616 | tf_op jit(solution)/shard_map/ppermute | solution.py:25
  25.2 15.0 %collective-permute-start.11 = (bf16[3,64,512]{2,1,0:T(8,128)(2,1)S(1)}, bf16[3,64,512]{2,1,0:T(8,128)(2,1)S(1)}, u32[]{:S(2)}, u32[]{:S(2)}) collective-permute-start(bf16[3,64,512]{2,1,0:T(8,128)(2,1)S(1)} %get-tuple-element.42), channel_id=1, source_target_pairs={{0,2},{1,3},{2,0},{3,1},{4,6},{5,7},{6,4},{7,5},{8,10},{9,11},{10,... | collective-permute-start | bytes 589832 | tf_op jit(solution)/shard_map/ppermute | solution.py:411
  26.8 14.0 %collective-permute-start.12 = (bf16[3,64,512]{2,1,0:T(8,128)(2,1)S(1)}, bf16[3,64,512]{2,1,0:T(8,128)(2,1)S(1)}, u32[]{:S(2)}, u32[]{:S(2)}) collective-permute-start(bf16[3,64,512]{2,1,0:T(8,128)(2,1)S(1)} %get-tuple-element.43), channel_id=1, source_target_pairs={{0,4},{1,5},{2,6},{3,7},{4,0},{5,1},{6,2},{7,3},{8,12},{9,13},{10,... | collective-permute-start | bytes 589832 | tf_op jit(solution)/shard_map/ppermute | solution.py:411
  28.3 12.5 %collective-permute-start.13 = (bf16[3,64,512]{2,1,0:T(8,128)(2,1)S(1)}, bf16[3,64,512]{2,1,0:T(8,128)(2,1)S(1)}, u32[]{:S(2)}, u32[]{:S(2)}) collective-permute-start(bf16[3,64,512]{2,1,0:T(8,128)(2,1)S(1)} %get-tuple-element.44), channel_id=1, source_target_pairs={{0,6},{1,7},{2,4},{3,5},{4,2},{5,3},{6,0},{7,1},{8,14},{9,15},{10,... | collective-permute-start | bytes 589832 | tf_op jit(solution)/shard_map/ppermute | solution.py:411
  37.2 8.7 %collective-permute-start.10 = (bf16[3,64,512]{2,1,0:T(8,128)(2,1)S(1)}, bf16[3,64,512]{2,1,0:T(8,128)(2,1)S(1)}, u32[]{:S(2)}, u32[]{:S(2)}) collective-permute-start(bf16[3,64,512]{2,1,0:T(8,128)(2,1)S(1)} %get-tuple-element.40), channel_id=1, source_target_pairs={{0,6},{1,7},{2,4},{3,5},{4,2},{5,3},{6,0},{7,1},{8,14},{9,15},{10,... | collective-permute-start | bytes 589832 | tf_op jit(solution)/shard_map/ppermute | solution.py:411
  39.7 8.8 %collective-permute-start.8 = (bf16[3,64,512]{2,1,0:T(8,128)(2,1)S(1)}, bf16[3,64,512]{2,1,0:T(8,128)(2,1)S(1)}, u32[]{:S(2)}, u32[]{:S(2)}) collective-permute-start(bf16[3,64,512]{2,1,0:T(8,128)(2,1)S(1)} %get-tuple-element.38), channel_id=1, source_target_pairs={{0,2},{1,3},{2,0},{3,1},{4,6},{5,7},{6,4},{7,5},{8,10},{9,11},{10,... | collective-permute-start | bytes 589832 | tf_op jit(solution)/shard_map/ppermute | solution.py:411
  40.3 8.3 %collective-permute-start.9 = (bf16[3,64,512]{2,1,0:T(8,128)(2,1)S(1)}, bf16[3,64,512]{2,1,0:T(8,128)(2,1)S(1)}, u32[]{:S(2)}, u32[]{:S(2)}) collective-permute-start(bf16[3,64,512]{2,1,0:T(8,128)(2,1)S(1)} %get-tuple-element.39), channel_id=1, source_target_pairs={{0,4},{1,5},{2,6},{3,7},{4,0},{5,1},{6,2},{7,3},{8,12},{9,13},{10,... | collective-permute-start | bytes 589832 | tf_op jit(solution)/shard_map/ppermute | solution.py:411
  49.3 29.9 %collective-permute-start.14 = (f32[512,512]{1,0:T(8,128)S(1)}, f32[512,512]{1,0:T(8,128)S(1)}, u32[]{:S(2)}, u32[]{:S(2)}) collective-permute-start(f32[512,512]{1,0:T(8,128)S(1)} %get-tuple-element.46), channel_id=1, source_target_pairs={{0,1},{1,0},{2,3},{3,2},{4,5},{5,4},{6,7},{7,6},{8,9},{9,8},{10,11... | collective-permute-start | bytes 3145736 | tf_op jit(solution)/shard_map/ppermute | solution.py:433
  49.4 28.9 %collective-permute-start.7 = (bf16[64,4096]{1,0:T(8,128)(2,1)S(1)}, bf16[64,4096]{1,0:T(8,128)(2,1)S(1)}, u32[]{:S(2)}, u32[]{:S(2)}) collective-permute-start(bf16[64,4096]{1,0:T(8,128)(2,1)S(1)} %bitcast.19), channel_id=1, source_target_pairs={{0,8},{8,16},{16,24},{24,0},{1,9},{9,17},{17,25},{25,1},{2,10},{10... | collective-permute-start | bytes 1572872 | tf_op jit(solution)/shard_map/ppermute | solution.py:25
  50.0 22.5 %collective-permute-start.6 = (bf16[2,16,4096]{2,1,0:T(8,128)(2,1)S(1)}, bf16[2,16,4096]{2,1,0:T(8,128)(2,1)S(1)}, u32[]{:S(2)}, u32[]{:S(2)}) collective-permute-start(bf16[2,16,4096]{2,1,0:T(8,128)(2,1)S(1)} %get-tuple-element.35), channel_id=1, source_target_pairs={{0,24},{8,0},{16,8},{24,16},{1,25},{9,1},{17,9},{25,17},{2,26},{10... | collective-permute-start | bytes 786440 | tf_op jit(solution)/shard_map/ppermute | solution.py:25

commit v8 on v7

--- a/solution.py
+++ b/solution.py
@@ -186,13 +186,14 @@
     return called(functools.partial(kernel, chips), (x, *operands), outputs, flops=4 * rows * width)
 
 
-def product_kernel(chips, inner, *refs):
+def product_kernel(chips, inner, other, *refs):
     early, late = refs[:chips], refs[chips : 2 * chips]
-    keep_ref, send_ref = refs[2 * chips :]
+    out_ref = refs[2 * chips]
     unit = early[0].shape[-1]
-    half = keep_ref.shape[0] // unit
+    half = out_ref.shape[0] // unit
     own = 2 * half
     core = lax.axis_index("dp") % 2
+    dest = 1 - core if other else core
     over_tokens = (((0,), (0,)), ((), ()))
 
     def stacked(at):
@@ -200,27 +201,26 @@
 
     for g in range(inner // unit):
         grouped = stacked(own + g)
-        for dest, out_ref in ((core, keep_ref), (1 - core, send_ref)):
-            for b in range(half):
-                out_ref[b * unit : (b + 1) * unit, g * unit : (g + 1) * unit] = lax.dot_general(
-                    stacked(dest * half + b),
-                    grouped,
-                    over_tokens,
-                    preferred_element_type=jnp.float32,
-                )
-
-
-def products(early, late, width, inner, members):
+        for b in range(half):
+            out_ref[b * unit : (b + 1) * unit, g * unit : (g + 1) * unit] = lax.dot_general(
+                stacked(dest * half + b),
+                grouped,
+                over_tokens,
+                preferred_element_type=jnp.float32,
+            )
+
+
+def products(early, late, width, inner, members, other):
     chips = members // 2
     rows = late[0].shape[1]
-    out = jax.ShapeDtypeStruct((width // members, inner), jnp.float32)
-    return called(
-        functools.partial(product_kernel, chips, inner),
+    (out,) = called(
+        functools.partial(product_kernel, chips, inner, other),
         (*early, *late),
-        [out, out],
-        flops=8 * chips * rows * (width // members) * inner,
+        [jax.ShapeDtypeStruct((width // members, inner), jnp.float32)],
+        flops=4 * chips * rows * (width // members) * inner,
         vmem=8,
     )
+    return out
 
 
 def combine_kernel(factor, keep_ref, got_ref, out_ref, held, sent):
@@ -429,7 +429,8 @@
     next_early, through_early = span(x_early, grouped_early, weight)
     next_late, through_late = span(x_late, grouped_late, weight)
 
-    keep, send = products(got_early, got_late, width, inner, members)
+    send = products(got_early, got_late, width, inner, members, True)
+    keep = products(got_early, got_late, width, inner, members, False)
     got = lax.ppermute(send, "dp", [(i, i ^ 1) for i in range(members)])
     summed = combined(keep, got, float(2 * rows * members) ** (-0.5))
 

time: 80.5 us -> 80.7 us (level)
    pallas_call x5 -> x6, Pallas kernels: 11 us -> 11.2 us  [called(): pl.pallas_call(kernel, in_specs=more.get('in_specs', [whole_vmem()] * len...]
  transfers between devices with their start and end apart: 15 -> 15, of which waited for: 5 -> 5; matrix products, arithmetic and copies ran while one was open for 1% -> 1% of each run, Pallas kernels for 16% -> 17%
where the time goes in v8:
time: 80.7 us; the launch traced here: 80.5 us
  waiting for transfers between devices  39.7 us (49%)
  starting transfers between devices  22 us (27%)
  Pallas kernels  15 us (19%)
  local copies, waits for them, and re-layouts  2.98 us (4%)
    ppermute x8, waiting for transfers between devices, passed_along(): lax.ppermute(shard, axis, [(i, (i + by) % count) for i in range(count)])  31.9 us
    ppermute x8, starting transfers between devices, passed_along(): lax.ppermute(shard, axis, [(i, (i + by) % count) for i in range(count)])  14.8 us
    pallas_call x6, Pallas kernels, called(): pl.pallas_call(kernel, in_specs=more.get('in_specs', [whole_vmem()] * len...  11.2 us
    ppermute x6, waiting for transfers between devices, exchanged(): got.append(lax.ppermute(pieces[c], 'dp', to))  7.8 us
    ppermute x6, starting transfers between devices, exchanged(): got.append(lax.ppermute(pieces[c], 'dp', to))  7.11 us
    pallas_call x3, Pallas kernels, finished(): pl.pallas_call(functools.partial(finish_kernel, parts, places), in_specs=...  2.54 us
    unnamed x6, local copies, waits for them, and re-layouts  2.09 us
  transfers between devices with their start and end apart: 15, of which 5 were waited for; matrix products, arithmetic and copies ran while one was open for 1% of the time, Pallas kernels for 17%

profile of v8, /device:TPU:0, one launch (start us, length us, event | category | flops | bytes accessed | tf_op | source)
XLA Modules:
  0.0 80.5 jit_solution(106543549677014984)
XLA Ops:
  0.6 3.1 %collective-permute-start = (bf16[64,4096]{1,0:T(8,128)(2,1)}, bf16[64,4096]{1,0:T(8,128)(2,1)S(1)}, u32[]{:S(2)}, u32[]{:S(2)}) collective-permute-start(bf16[64,4096]{1,0:T(8,128)(2,1)} %bitcast.26), channel_id=1, source_target_pairs={{0,8},{8,16},{16,24},{24,0},{1,9},{9,17},{17,25},{25,1},{2,10},{10... | collective-permute-start | bytes 1572872 | tf_op jit(solution)/shard_map/ppermute | solution.py:25
  3.7 1.0 %copy-done = bf16[1,64,4096]{2,1,0:T(8,128)(2,1)S(1)} copy-done((bf16[1,64,4096]{2,1,0:T(8,128)(2,1)S(1)}, bf16[1,64,4096]{2,1,0:T(8,128)(2,1)}, u32[]{:S(2)}) %copy-start) | copy-done | bytes 524312
  4.8 1.0 %copy-done.1 = bf16[1,64,4096]{2,1,0:T(8,128)(2,1)S(1)} copy-done((bf16[1,64,4096]{2,1,0:T(8,128)(2,1)S(1)}, bf16[1,64,4096]{2,1,0:T(8,128)(2,1)}, u32[]{:S(2)}) %copy-start.1) | copy-done | bytes 524312
  6.1 2.1 %collective-permute-start.1 = (bf16[1,16,4096]{2,1,0:T(8,128)(2,1)S(1)}, bf16[1,16,4096]{2,1,0:T(8,128)(2,1)S(1)}, u32[]{:S(2)}, u32[]{:S(2)}) collective-permute-start(bf16[1,16,4096]{2,1,0:T(8,128)(2,1)S(1)} %get-tuple-element.24), channel_id=1, source_target_pairs={{0,24},{8,0},{16,8},{24,16},{1,25},{9,1},{17,9},{25,17},{2,26},{10... | collective-permute-start | bytes 393224 | tf_op jit(solution)/shard_map/ppermute | solution.py:25
  8.2 2.0 %collective-permute-start.2 = (bf16[1,16,4096]{2,1,0:T(8,128)(2,1)S(1)}, bf16[1,16,4096]{2,1,0:T(8,128)(2,1)S(1)}, u32[]{:S(2)}, u32[]{:S(2)}) collective-permute-start(bf16[1,16,4096]{2,1,0:T(8,128)(2,1)S(1)} %get-tuple-element.25), channel_id=1, source_target_pairs={{0,24},{8,0},{16,8},{24,16},{1,25},{9,1},{17,9},{25,17},{2,26},{10... | collective-permute-start | bytes 393224 | tf_op jit(solution)/shard_map/ppermute | solution.py:25
  10.2 0.4 collective-permute-start.3
  10.6 0.4 collective-permute-start.4
  11.1 0.8 slice_bitcast_fusion
  11.8 12.5 %collective-permute-done.3.sums_ref = bf16[2,16,512]{2,1,0:T(8,128)(2,1)S(1)} collective-permute-done((bf16[2,16,512]{2,1,0:T(8,128)(2,1)S(1)}, bf16[2,16,512]{2,1,0:T(8,128)(2,1)S(1)}, u32[]{:S(2)}, u32[]{:S(2)}) %collective-permute-start.3) | collective-permute-done | bytes 32800 | tf_op jit(solution)/shard_map/ppermute | solution.py:25
  24.3 0.6 collective-permute-start.5
  25.0 0.3 shard_map.101
  25.2 1.6 %collective-permute-start.11 = (bf16[3,64,512]{2,1,0:T(8,128)(2,1)S(1)}, bf16[3,64,512]{2,1,0:T(8,128)(2,1)S(1)}, u32[]{:S(2)}, u32[]{:S(2)}) collective-permute-start(bf16[3,64,512]{2,1,0:T(8,128)(2,1)S(1)} %get-tuple-element.40), channel_id=1, source_target_pairs={{0,2},{1,3},{2,0},{3,1},{4,6},{5,7},{6,4},{7,5},{8,10},{9,11},{10,... | collective-permute-start | bytes 589832 | tf_op jit(solution)/shard_map/ppermute | solution.py:411
  26.8 1.5 %collective-permute-start.12 = (bf16[3,64,512]{2,1,0:T(8,128)(2,1)S(1)}, bf16[3,64,512]{2,1,0:T(8,128)(2,1)S(1)}, u32[]{:S(2)}, u32[]{:S(2)}) collective-permute-start(bf16[3,64,512]{2,1,0:T(8,128)(2,1)S(1)} %get-tuple-element.41), channel_id=1, source_target_pairs={{0,4},{1,5},{2,6},{3,7},{4,0},{5,1},{6,2},{7,3},{8,12},{9,13},{10,... | collective-permute-start | bytes 589832 | tf_op jit(solution)/shard_map/ppermute | solution.py:411
  28.3 0.5 collective-permute-start.13
  28.8 8.1 %collective-permute-done.5 = bf16[64,512]{1,0:T(8,128)(2,1)S(1)} collective-permute-done((bf16[64,512]{1,0:T(8,128)(2,1)S(1)}, bf16[64,512]{1,0:T(8,128)(2,1)S(1)}, u32[]{:S(2)}, u32[]{:S(2)}) %collective-permute-start.5) | collective-permute-done | bytes 65568 | tf_op jit(solution)/shard_map/ppermute | solution.py:25
  37.0 0.2 shard_map.103
  37.2 2.5 %collective-permute-start.10 = (bf16[3,64,512]{2,1,0:T(8,128)(2,1)S(1)}, bf16[3,64,512]{2,1,0:T(8,128)(2,1)S(1)}, u32[]{:S(2)}, u32[]{:S(2)}) collective-permute-start(bf16[3,64,512]{2,1,0:T(8,128)(2,1)S(1)} %get-tuple-element.38), channel_id=1, source_target_pairs={{0,6},{1,7},{2,4},{3,5},{4,2},{5,3},{6,0},{7,1},{8,14},{9,15},{10,... | collective-permute-start | bytes 589832 | tf_op jit(solution)/shard_map/ppermute | solution.py:411
  39.7 0.5 collective-permute-start.8
  40.3 0.5 collective-permute-start.9
  40.8 5.2 %collective-permute-done.10.refs_3_ = bf16[3,64,512]{2,1,0:T(8,128)(2,1)S(1)} collective-permute-done((bf16[3,64,512]{2,1,0:T(8,128)(2,1)S(1)}, bf16[3,64,512]{2,1,0:T(8,128)(2,1)S(1)}, u32[]{:S(2)}, u32[]{:S(2)}) %collective-permute-start.10) | collective-permute-done | bytes 196640 | tf_op jit(solution)/shard_map/ppermute | solution.py:411
  46.0 2.6 %collective-permute-done.8.refs_1_ = bf16[3,64,512]{2,1,0:T(8,128)(2,1)S(1)} collective-permute-done((bf16[3,64,512]{2,1,0:T(8,128)(2,1)S(1)}, bf16[3,64,512]{2,1,0:T(8,128)(2,1)S(1)}, u32[]{:S(2)}, u32[]{:S(2)}) %collective-permute-start.8) | collective-permute-done | bytes 196640 | tf_op jit(solution)/shard_map/ppermute | solution.py:411
  48.6 0.5 shard_map.106
  49.1 0.6 collective-permute-start.7
  49.8 5.5 %collective-permute-start.6 = (bf16[2,16,4096]{2,1,0:T(8,128)(2,1)S(1)}, bf16[2,16,4096]{2,1,0:T(8,128)(2,1)S(1)}, u32[]{:S(2)}, u32[]{:S(2)}) collective-permute-start(bf16[2,16,4096]{2,1,0:T(8,128)(2,1)S(1)} %get-tuple-element.33), channel_id=1, source_target_pairs={{0,24},{8,0},{16,8},{24,16},{1,25},{9,1},{17,9},{25,17},{2,26},{10... | collective-permute-start | bytes 786440 | tf_op jit(solution)/shard_map/ppermute | solution.py:25
  55.3 4.9 %shard_map.102 = (bf16[64,4096]{1,0:T(8,128)(2,1)}, f32[64,4096]{1,0:T(8,128)S(1)}) custom-call(bf16[64,4096]{1,0:T(8,128)(2,1)S(1)} %collective-permute-done.x_ref, bf16[64,512]{1,0:T(8,128)(2,1)S(1)} %get-tuple-element.27.grouped_ref, bf16[4096,512]{1,0:T(8,128)(2,1)} %bitcast.21), custom_call_target="tpu_custom_call" | custom-call | flops 536870912 | bytes 6356992 | tf_op jit(solution)/shard_map/pallas_call | solution.py:34
  60.2 0.8 %finished.3.refs_1_ = bf16[64,4096]{1,0:T(8,128)(2,1)} custom-call(s32[2,2,128]{2,1,0:T(2,128)S(1)} %broadcast_in_dim.14.match_ref, f32[64,4096]{1,0:T(8,128)S(1)} %get-tuple-element.32.through_ref, bf16[1,16,4096]{2,1,0:T(8,128)(2,1)S(1)} %collective-permute-done.1.first_ref.refs_0_, bf16[1,16,4096]{2,1,0:T(8,128)(2,1)S(1)} %collective-permute-done.2.rest_ref.refs_1_), custom_call_target="tpu_custom_call" | custom-call | flops 262144 | bytes 1048576 | tf_op jit(solution)/shard_map/finished/pallas_call | solution.py:360
  61.0 11.3 %collective-permute-done.6.refs_0_ = bf16[2,16,4096]{2,1,0:T(8,128)(2,1)S(1)} collective-permute-done((bf16[2,16,4096]{2,1,0:T(8,128)(2,1)S(1)}, bf16[2,16,4096]{2,1,0:T(8,128)(2,1)S(1)}, u32[]{:S(2)}, u32[]{:S(2)}) %collective-permute-start.6) | collective-permute-done | bytes 262176 | tf_op jit(solution)/shard_map/ppermute | solution.py:25
  72.3 0.8 %finished.4 = bf16[64,4096]{1,0:T(8,128)(2,1)} custom-call(s32[2,2,128]{2,1,0:T(2,128)S(1)} %broadcast_in_dim.14.match_ref, f32[64,4096]{1,0:T(8,128)S(1)} %get-tuple-element.32.through_ref, bf16[2,16,4096]{2,1,0:T(8,128)(2,1)S(1)} %collective-permute-done.6.refs_0_, bf16[64,4096]{1,0:T(8,128)(2,1)} %finished.3.refs_1_), custom_call_target="tpu_custom_call", output_to_operand_aliasing={{}: (3, {})} | custom-call | flops 262144 | bytes 1048576 | tf_op jit(solution)/shard_map/finished/pallas_call | solution.py:360
  73.1 4.9 %shard_map.104 = (bf16[64,4096]{1,0:T(8,128)(2,1)}, f32[64,4096]{1,0:T(8,128)S(1)}) custom-call(bf16[64,4096]{1,0:T(8,128)(2,1)S(1)} %collective-permute-done.4.x_ref, bf16[64,512]{1,0:T(8,128)(2,1)S(1)} %get-tuple-element.30.grouped_ref, bf16[4096,512]{1,0:T(8,128)(2,1)} %bitcast.22), custom_call_target="tpu_custom_call" | custom-call | flops 536870912 | bytes 6356992 | tf_op jit(solution)/shard_map/pallas_call | solution.py:34
  78.0 0.9 %finished.5 = bf16[64,4096]{1,0:T(8,128)(2,1)} custom-call(s32[2,2,128]{2,1,0:T(2,128)S(1)} %broadcast_in_dim.31.match_ref, f32[64,4096]{1,0:T(8,128)S(1)} %get-tuple-element.34.through_ref, bf16[4,16,4096]{2,1,0:T(8,128)(2,1)S(1)} %bitcast.16), custom_call_target="tpu_custom_call" | custom-call | flops 524288 | bytes 2097152 | tf_op jit(solution)/shard_map/finished/pallas_call | solution.py:360
  78.9 0.5 shard_map.105.keep_ref
  79.4 1.0 %combine.1 = f32[512,512]{1,0:T(8,128)} custom-call(f32[512,512]{1,0:T(8,128)S(1)} %shard_map.105.keep_ref, f32[512,512]{1,0:T(8,128)S(1)} %collective-permute-done.14.got_ref), custom_call_target="tpu_custom_call" | custom-call | flops 524288 | bytes 3145728 | tf_op jit(solution)/shard_map/combine/pallas_call | solution.py:243
  (20 shorter events, 0.5 us)
Async XLA Ops:
  0.6 24.3 %collective-permute-start = (bf16[64,4096]{1,0:T(8,128)(2,1)}, bf16[64,4096]{1,0:T(8,128)(2,1)S(1)}, u32[]{:S(2)}, u32[]{:S(2)}) collective-permute-start(bf16[64,4096]{1,0:T(8,128)(2,1)} %bitcast.26), channel_id=1, source_target_pairs={{0,8},{8,16},{16,24},{24,0},{1,9},{9,17},{17,25},{25,1},{2,10},{10... | collective-permute-start | bytes 1572872 | tf_op jit(solution)/shard_map/ppermute | solution.py:25
  3.7 1.0 %copy-start = (bf16[1,64,4096]{2,1,0:T(8,128)(2,1)S(1)}, bf16[1,64,4096]{2,1,0:T(8,128)(2,1)}, u32[]{:S(2)}) copy-start(bf16[1,64,4096]{2,1,0:T(8,128)(2,1)} %param.8) | copy-start | bytes 1572868
  4.8 1.0 %copy-start.1 = (bf16[1,64,4096]{2,1,0:T(8,128)(2,1)S(1)}, bf16[1,64,4096]{2,1,0:T(8,128)(2,1)}, u32[]{:S(2)}) copy-start(bf16[1,64,4096]{2,1,0:T(8,128)(2,1)} %param.9) | copy-start | bytes 1572868
  5.8 43.3 %copy-start.2 = (bf16[1,64,4096]{2,1,0:T(8,128)(2,1)S(1)}, bf16[1,64,4096]{2,1,0:T(8,128)(2,1)}, u32[]{:S(2)}) copy-start(bf16[1,64,4096]{2,1,0:T(8,128)(2,1)} %param.9) | copy-start | bytes 1572868
  6.1 18.8 %collective-permute-start.1 = (bf16[1,16,4096]{2,1,0:T(8,128)(2,1)S(1)}, bf16[1,16,4096]{2,1,0:T(8,128)(2,1)S(1)}, u32[]{:S(2)}, u32[]{:S(2)}) collective-permute-start(bf16[1,16,4096]{2,1,0:T(8,128)(2,1)S(1)} %get-tuple-element.24), channel_id=1, source_target_pairs={{0,24},{8,0},{16,8},{24,16},{1,25},{9,1},{17,9},{25,17},{2,26},{10... | collective-permute-start | bytes 393224 | tf_op jit(solution)/shard_map/ppermute | solution.py:25
  8.2 16.7 %collective-permute-start.2 = (bf16[1,16,4096]{2,1,0:T(8,128)(2,1)S(1)}, bf16[1,16,4096]{2,1,0:T(8,128)(2,1)S(1)}, u32[]{:S(2)}, u32[]{:S(2)}) collective-permute-start(bf16[1,16,4096]{2,1,0:T(8,128)(2,1)S(1)} %get-tuple-element.25), channel_id=1, source_target_pairs={{0,24},{8,0},{16,8},{24,16},{1,25},{9,1},{17,9},{25,17},{2,26},{10... | collective-permute-start | bytes 393224 | tf_op jit(solution)/shard_map/ppermute | solution.py:25
  10.2 14.1 %collective-permute-start.3 = (bf16[2,16,512]{2,1,0:T(8,128)(2,1)S(1)}, bf16[2,16,512]{2,1,0:T(8,128)(2,1)S(1)}, u32[]{:S(2)}, u32[]{:S(2)}) collective-permute-start(bf16[2,16,512]{2,1,0:T(8,128)(2,1)S(1)} %get-tuple-element.26), channel_id=1, source_target_pairs={{0,24},{8,0},{16,8},{24,16},{1,25},{9,1},{17,9},{25,17},{2,26},{10... | collective-permute-start | bytes 98312 | tf_op jit(solution)/shard_map/ppermute | solution.py:25
  10.6 26.3 %collective-permute-start.4 = (bf16[64,4096]{1,0:T(8,128)(2,1)}, bf16[64,4096]{1,0:T(8,128)(2,1)S(1)}, u32[]{:S(2)}, u32[]{:S(2)}) collective-permute-start(bf16[64,4096]{1,0:T(8,128)(2,1)} %bitcast.27), channel_id=1, source_target_pairs={{0,24},{8,0},{16,8},{24,16},{1,25},{9,1},{17,9},{25,17},{2,26},{10... | collective-permute-start | bytes 1572872 | tf_op jit(solution)/shard_map/ppermute | solution.py:25
  24.3 12.6 %collective-permute-start.5 = (bf16[64,512]{1,0:T(8,128)(2,1)S(1)}, bf16[64,512]{1,0:T(8,128)(2,1)S(1)}, u32[]{:S(2)}, u32[]{:S(2)}) collective-permute-start(bf16[64,512]{1,0:T(8,128)(2,1)S(1)} %get-tuple-element.29), channel_id=1, source_target_pairs={{0,8},{8,16},{16,24},{24,0},{1,9},{9,17},{17,25},{25,1},{2,10},{10... | collective-permute-start | bytes 196616 | tf_op jit(solution)/shard_map/ppermute | solution.py:25
  25.2 15.0 %collective-permute-start.11 = (bf16[3,64,512]{2,1,0:T(8,128)(2,1)S(1)}, bf16[3,64,512]{2,1,0:T(8,128)(2,1)S(1)}, u32[]{:S(2)}, u32[]{:S(2)}) collective-permute-start(bf16[3,64,512]{2,1,0:T(8,128)(2,1)S(1)} %get-tuple-element.40), channel_id=1, source_target_pairs={{0,2},{1,3},{2,0},{3,1},{4,6},{5,7},{6,4},{7,5},{8,10},{9,11},{10,... | collective-permute-start | bytes 589832 | tf_op jit(solution)/shard_map/ppermute | solution.py:411
  26.8 14.0 %collective-permute-start.12 = (bf16[3,64,512]{2,1,0:T(8,128)(2,1)S(1)}, bf16[3,64,512]{2,1,0:T(8,128)(2,1)S(1)}, u32[]{:S(2)}, u32[]{:S(2)}) collective-permute-start(bf16[3,64,512]{2,1,0:T(8,128)(2,1)S(1)} %get-tuple-element.41), channel_id=1, source_target_pairs={{0,4},{1,5},{2,6},{3,7},{4,0},{5,1},{6,2},{7,3},{8,12},{9,13},{10,... | collective-permute-start | bytes 589832 | tf_op jit(solution)/shard_map/ppermute | solution.py:411
  28.3 12.5 %collective-permute-start.13 = (bf16[3,64,512]{2,1,0:T(8,128)(2,1)S(1)}, bf16[3,64,512]{2,1,0:T(8,128)(2,1)S(1)}, u32[]{:S(2)}, u32[]{:S(2)}) collective-permute-start(bf16[3,64,512]{2,1,0:T(8,128)(2,1)S(1)} %get-tuple-element.42), channel_id=1, source_target_pairs={{0,6},{1,7},{2,4},{3,5},{4,2},{5,3},{6,0},{7,1},{8,14},{9,15},{10,... | collective-permute-start | bytes 589832 | tf_op jit(solution)/shard_map/ppermute | solution.py:411
  37.2 8.7 %collective-permute-start.10 = (bf16[3,64,512]{2,1,0:T(8,128)(2,1)S(1)}, bf16[3,64,512]{2,1,0:T(8,128)(2,1)S(1)}, u32[]{:S(2)}, u32[]{:S(2)}) collective-permute-start(bf16[3,64,512]{2,1,0:T(8,128)(2,1)S(1)} %get-tuple-element.38), channel_id=1, source_target_pairs={{0,6},{1,7},{2,4},{3,5},{4,2},{5,3},{6,0},{7,1},{8,14},{9,15},{10,... | collective-permute-start | bytes 589832 | tf_op jit(solution)/shard_map/ppermute | solution.py:411
  39.7 8.8 %collective-permute-start.8 = (bf16[3,64,512]{2,1,0:T(8,128)(2,1)S(1)}, bf16[3,64,512]{2,1,0:T(8,128)(2,1)S(1)}, u32[]{:S(2)}, u32[]{:S(2)}) collective-permute-start(bf16[3,64,512]{2,1,0:T(8,128)(2,1)S(1)} %get-tuple-element.36), channel_id=1, source_target_pairs={{0,2},{1,3},{2,0},{3,1},{4,6},{5,7},{6,4},{7,5},{8,10},{9,11},{10,... | collective-permute-start | bytes 589832 | tf_op jit(solution)/shard_map/ppermute | solution.py:411
  40.3 8.3 %collective-permute-start.9 = (bf16[3,64,512]{2,1,0:T(8,128)(2,1)S(1)}, bf16[3,64,512]{2,1,0:T(8,128)(2,1)S(1)}, u32[]{:S(2)}, u32[]{:S(2)}) collective-permute-start(bf16[3,64,512]{2,1,0:T(8,128)(2,1)S(1)} %get-tuple-element.37), channel_id=1, source_target_pairs={{0,4},{1,5},{2,6},{3,7},{4,0},{5,1},{6,2},{7,3},{8,12},{9,13},{10,... | collective-permute-start | bytes 589832 | tf_op jit(solution)/shard_map/ppermute | solution.py:411
  49.1 30.4 %collective-permute-start.14 = (f32[512,512]{1,0:T(8,128)S(1)}, f32[512,512]{1,0:T(8,128)S(1)}, u32[]{:S(2)}, u32[]{:S(2)}) collective-permute-start(f32[512,512]{1,0:T(8,128)S(1)} %shard_map.106), channel_id=1, source_target_pairs={{0,1},{1,0},{2,3},{3,2},{4,5},{5,4},{6,7},{7,6},{8,9},{9,8},{10,11... | collective-permute-start | bytes 3145736 | tf_op jit(solution)/shard_map/ppermute | solution.py:434
  49.1 28.9 %collective-permute-start.7 = (bf16[64,4096]{1,0:T(8,128)(2,1)S(1)}, bf16[64,4096]{1,0:T(8,128)(2,1)S(1)}, u32[]{:S(2)}, u32[]{:S(2)}) collective-permute-start(bf16[64,4096]{1,0:T(8,128)(2,1)S(1)} %bitcast.19), channel_id=1, source_target_pairs={{0,8},{8,16},{16,24},{24,0},{1,9},{9,17},{17,25},{25,1},{2,10},{10... | collective-permute-start | bytes 1572872 | tf_op jit(solution)/shard_map/ppermute | solution.py:25
  49.8 22.5 %collective-permute-start.6 = (bf16[2,16,4096]{2,1,0:T(8,128)(2,1)S(1)}, bf16[2,16,4096]{2,1,0:T(8,128)(2,1)S(1)}, u32[]{:S(2)}, u32[]{:S(2)}) collective-permute-start(bf16[2,16,4096]{2,1,0:T(8,128)(2,1)S(1)} %get-tuple-element.33), channel_id=1, source_target_pairs={{0,24},{8,0},{16,8},{24,16},{1,25},{9,1},{17,9},{25,17},{2,26},{10... | collective-permute-start | bytes 786440 | tf_op jit(solution)/shard_map/ppermute | solution.py:25

commit v9 on v8

--- a/solution.py
+++ b/solution.py
@@ -106,7 +106,10 @@
         cost_estimate=pl.CostEstimate(
             flops=2 * rows * width, bytes_accessed=6 * rows * width, transcendentals=0
         ),
-    )(early, late)
+    )(
+        pltpu.with_memory_space_constraint(early, pltpu.HBM),
+        pltpu.with_memory_space_constraint(late, pltpu.HBM),
+    )
 
 
 def inverse_of(x):

time: 80.7 us -> 80.6 us (level)
  local copies, waits for them, and re-layouts: 2.98 us -> 0.9 us
  Pallas kernels: 15 us -> 17 us
    unnamed x6 -> x2, local copies, waits for them, and re-layouts: 2.09 us -> 0.01 us
    pallas_call x1, Pallas kernels: 0.24 us -> 2.24 us  [group_sums(): pl.pallas_call(group_kernel, grid=(blocks, 2), in_specs=[wide, wide], out...]
  transfers between devices with their start and end apart: 15 -> 15, of which waited for: 5 -> 5; matrix products, arithmetic and copies ran while one was open for 1% -> 1% of each run, Pallas kernels for 17% -> 19%
where the time goes in v9:
time: 80.6 us; the launch traced here: 80.5 us
  waiting for transfers between devices  39.8 us (49%)
  starting transfers between devices  22 us (27%)
  Pallas kernels  17 us (21%)
  local copies, waits for them, and re-layouts  0.9 us (1%)
    ppermute x8, waiting for transfers between devices, passed_along(): lax.ppermute(shard, axis, [(i, (i + by) % count) for i in range(count)])  32 us
    ppermute x8, starting transfers between devices, passed_along(): lax.ppermute(shard, axis, [(i, (i + by) % count) for i in range(count)])  14.8 us
    pallas_call x6, Pallas kernels, called(): pl.pallas_call(kernel, in_specs=more.get('in_specs', [whole_vmem()] * len...  11.2 us
    ppermute x6, waiting for transfers between devices, exchanged(): got.append(lax.ppermute(pieces[c], 'dp', to))  7.8 us
    ppermute x6, starting transfers between devices, exchanged(): got.append(lax.ppermute(pieces[c], 'dp', to))  7.11 us
    pallas_call x3, Pallas kernels, finished(): pl.pallas_call(functools.partial(finish_kernel, parts, places), in_specs=...  2.54 us
    pallas_call x1, Pallas kernels, group_sums(): pl.pallas_call(group_kernel, grid=(blocks, 2), in_specs=[wide, wide], out...  2.24 us
  transfers between devices with their start and end apart: 15, of which 5 were waited for; matrix products, arithmetic and copies ran while one was open for 1% of the time, Pallas kernels for 19%

profile of v9, /device:TPU:0, one launch (start us, length us, event | category | flops | bytes accessed | tf_op | source)
XLA Modules:
  0.0 80.5 jit_solution(13743016901977613935)
XLA Ops:
  0.6 3.1 %collective-permute-start = (bf16[64,4096]{1,0:T(8,128)(2,1)}, bf16[64,4096]{1,0:T(8,128)(2,1)S(1)}, u32[]{:S(2)}, u32[]{:S(2)}) collective-permute-start(bf16[64,4096]{1,0:T(8,128)(2,1)} %bitcast.26), channel_id=1, source_target_pairs={{0,8},{8,16},{16,24},{24,0},{1,9},{9,17},{17,25},{25,1},{2,10},{10... | collective-permute-start | bytes 1572872 | tf_op jit(solution)/shard_map/ppermute | solution.py:25
  3.7 2.2 %group_sums.1 = (bf16[64,512]{1,0:T(8,128)(2,1)S(1)}, bf16[2,16,512]{2,1,0:T(8,128)(2,1)S(1)}, bf16[1,16,4096]{2,1,0:T(8,128)(2,1)S(1)}, bf16[1,16,4096]{2,1,0:T(8,128)(2,1)S(1)}, bf16[2,16,4096]{2,1,0:T(8,128)(2,1)S(1)}) custom-call(bf16[64,4096]{1,0:T(8,128)(2,1)} %bitcast.24, bf16[64,4096]{1,0:T(8,128)(2,1)} %bitcast.23), custom_call_target="tpu_custom_call" | custom-call | flops 524288 | bytes 1572864 | tf_op jit(solution)/shard_map/group_sums/pallas_call | solution.py:91
  6.0 2.2 %collective-permute-start.1 = (bf16[1,16,4096]{2,1,0:T(8,128)(2,1)S(1)}, bf16[1,16,4096]{2,1,0:T(8,128)(2,1)S(1)}, u32[]{:S(2)}, u32[]{:S(2)}) collective-permute-start(bf16[1,16,4096]{2,1,0:T(8,128)(2,1)S(1)} %get-tuple-element.24), channel_id=1, source_target_pairs={{0,24},{8,0},{16,8},{24,16},{1,25},{9,1},{17,9},{25,17},{2,26},{10... | collective-permute-start | bytes 393224 | tf_op jit(solution)/shard_map/ppermute | solution.py:25
  8.1 1.9 %collective-permute-start.2 = (bf16[1,16,4096]{2,1,0:T(8,128)(2,1)S(1)}, bf16[1,16,4096]{2,1,0:T(8,128)(2,1)S(1)}, u32[]{:S(2)}, u32[]{:S(2)}) collective-permute-start(bf16[1,16,4096]{2,1,0:T(8,128)(2,1)S(1)} %get-tuple-element.25), channel_id=1, source_target_pairs={{0,24},{8,0},{16,8},{24,16},{1,25},{9,1},{17,9},{25,17},{2,26},{10... | collective-permute-start | bytes 393224 | tf_op jit(solution)/shard_map/ppermute | solution.py:25
  10.1 0.4 collective-permute-start.3
  10.5 0.4 collective-permute-start.4
  11.0 0.8 slice_bitcast_fusion
  11.8 12.6 %collective-permute-done.3.sums_ref = bf16[2,16,512]{2,1,0:T(8,128)(2,1)S(1)} collective-permute-done((bf16[2,16,512]{2,1,0:T(8,128)(2,1)S(1)}, bf16[2,16,512]{2,1,0:T(8,128)(2,1)S(1)}, u32[]{:S(2)}, u32[]{:S(2)}) %collective-permute-start.3) | collective-permute-done | bytes 32800 | tf_op jit(solution)/shard_map/ppermute | solution.py:25
  24.3 0.6 collective-permute-start.5
  25.0 0.3 shard_map.101
  25.3 1.6 %collective-permute-start.11 = (bf16[3,64,512]{2,1,0:T(8,128)(2,1)S(1)}, bf16[3,64,512]{2,1,0:T(8,128)(2,1)S(1)}, u32[]{:S(2)}, u32[]{:S(2)}) collective-permute-start(bf16[3,64,512]{2,1,0:T(8,128)(2,1)S(1)} %get-tuple-element.40), channel_id=1, source_target_pairs={{0,2},{1,3},{2,0},{3,1},{4,6},{5,7},{6,4},{7,5},{8,10},{9,11},{10,... | collective-permute-start | bytes 589832 | tf_op jit(solution)/shard_map/ppermute | solution.py:414
  26.8 1.5 %collective-permute-start.12 = (bf16[3,64,512]{2,1,0:T(8,128)(2,1)S(1)}, bf16[3,64,512]{2,1,0:T(8,128)(2,1)S(1)}, u32[]{:S(2)}, u32[]{:S(2)}) collective-permute-start(bf16[3,64,512]{2,1,0:T(8,128)(2,1)S(1)} %get-tuple-element.41), channel_id=1, source_target_pairs={{0,4},{1,5},{2,6},{3,7},{4,0},{5,1},{6,2},{7,3},{8,12},{9,13},{10,... | collective-permute-start | bytes 589832 | tf_op jit(solution)/shard_map/ppermute | solution.py:414
  28.3 0.5 collective-permute-start.13
  28.8 8.1 %collective-permute-done.5 = bf16[64,512]{1,0:T(8,128)(2,1)S(1)} collective-permute-done((bf16[64,512]{1,0:T(8,128)(2,1)S(1)}, bf16[64,512]{1,0:T(8,128)(2,1)S(1)}, u32[]{:S(2)}, u32[]{:S(2)}) %collective-permute-start.5) | collective-permute-done | bytes 65568 | tf_op jit(solution)/shard_map/ppermute | solution.py:25
  37.0 0.2 shard_map.103
  37.2 2.5 %collective-permute-start.10 = (bf16[3,64,512]{2,1,0:T(8,128)(2,1)S(1)}, bf16[3,64,512]{2,1,0:T(8,128)(2,1)S(1)}, u32[]{:S(2)}, u32[]{:S(2)}) collective-permute-start(bf16[3,64,512]{2,1,0:T(8,128)(2,1)S(1)} %get-tuple-element.38), channel_id=1, source_target_pairs={{0,6},{1,7},{2,4},{3,5},{4,2},{5,3},{6,0},{7,1},{8,14},{9,15},{10,... | collective-permute-start | bytes 589832 | tf_op jit(solution)/shard_map/ppermute | solution.py:414
  39.7 0.5 collective-permute-start.8
  40.3 0.5 collective-permute-start.9
  40.8 5.2 %collective-permute-done.10.refs_3_ = bf16[3,64,512]{2,1,0:T(8,128)(2,1)S(1)} collective-permute-done((bf16[3,64,512]{2,1,0:T(8,128)(2,1)S(1)}, bf16[3,64,512]{2,1,0:T(8,128)(2,1)S(1)}, u32[]{:S(2)}, u32[]{:S(2)}) %collective-permute-start.10) | collective-permute-done | bytes 196640 | tf_op jit(solution)/shard_map/ppermute | solution.py:414
  46.0 2.6 %collective-permute-done.8.refs_1_ = bf16[3,64,512]{2,1,0:T(8,128)(2,1)S(1)} collective-permute-done((bf16[3,64,512]{2,1,0:T(8,128)(2,1)S(1)}, bf16[3,64,512]{2,1,0:T(8,128)(2,1)S(1)}, u32[]{:S(2)}, u32[]{:S(2)}) %collective-permute-start.8) | collective-permute-done | bytes 196640 | tf_op jit(solution)/shard_map/ppermute | solution.py:414
  48.6 0.5 shard_map.106
  49.1 0.1 collective-permute-start.14
  49.2 0.6 collective-permute-start.7
  49.8 5.5 %collective-permute-start.6 = (bf16[2,16,4096]{2,1,0:T(8,128)(2,1)S(1)}, bf16[2,16,4096]{2,1,0:T(8,128)(2,1)S(1)}, u32[]{:S(2)}, u32[]{:S(2)}) collective-permute-start(bf16[2,16,4096]{2,1,0:T(8,128)(2,1)S(1)} %get-tuple-element.33), channel_id=1, source_target_pairs={{0,24},{8,0},{16,8},{24,16},{1,25},{9,1},{17,9},{25,17},{2,26},{10... | collective-permute-start | bytes 786440 | tf_op jit(solution)/shard_map/ppermute | solution.py:25
  55.3 4.9 %shard_map.102 = (bf16[64,4096]{1,0:T(8,128)(2,1)}, f32[64,4096]{1,0:T(8,128)S(1)}) custom-call(bf16[64,4096]{1,0:T(8,128)(2,1)S(1)} %collective-permute-done.x_ref, bf16[64,512]{1,0:T(8,128)(2,1)S(1)} %get-tuple-element.27.grouped_ref, bf16[4096,512]{1,0:T(8,128)(2,1)} %bitcast.18), custom_call_target="tpu_custom_call" | custom-call | flops 536870912 | bytes 6356992 | tf_op jit(solution)/shard_map/pallas_call | solution.py:34
  60.2 0.8 %finished.3.refs_1_ = bf16[64,4096]{1,0:T(8,128)(2,1)} custom-call(s32[2,2,128]{2,1,0:T(2,128)S(1)} %broadcast_in_dim.14.match_ref, f32[64,4096]{1,0:T(8,128)S(1)} %get-tuple-element.32.through_ref, bf16[1,16,4096]{2,1,0:T(8,128)(2,1)S(1)} %collective-permute-done.1.first_ref.refs_0_, bf16[1,16,4096]{2,1,0:T(8,128)(2,1)S(1)} %collective-permute-done.2.rest_ref.refs_1_), custom_call_target="tpu_custom_call" | custom-call | flops 262144 | bytes 1048576 | tf_op jit(solution)/shard_map/finished/pallas_call | solution.py:363
  61.0 11.3 %collective-permute-done.6.refs_0_ = bf16[2,16,4096]{2,1,0:T(8,128)(2,1)S(1)} collective-permute-done((bf16[2,16,4096]{2,1,0:T(8,128)(2,1)S(1)}, bf16[2,16,4096]{2,1,0:T(8,128)(2,1)S(1)}, u32[]{:S(2)}, u32[]{:S(2)}) %collective-permute-start.6) | collective-permute-done | bytes 262176 | tf_op jit(solution)/shard_map/ppermute | solution.py:25
  72.3 0.8 %finished.4 = bf16[64,4096]{1,0:T(8,128)(2,1)} custom-call(s32[2,2,128]{2,1,0:T(2,128)S(1)} %broadcast_in_dim.14.match_ref, f32[64,4096]{1,0:T(8,128)S(1)} %get-tuple-element.32.through_ref, bf16[2,16,4096]{2,1,0:T(8,128)(2,1)S(1)} %collective-permute-done.6.refs_0_, bf16[64,4096]{1,0:T(8,128)(2,1)} %finished.3.refs_1_), custom_call_target="tpu_custom_call", output_to_operand_aliasing={{}: (3, {})} | custom-call | flops 262144 | bytes 1048576 | tf_op jit(solution)/shard_map/finished/pallas_call | solution.py:363
  73.1 4.9 %shard_map.104 = (bf16[64,4096]{1,0:T(8,128)(2,1)}, f32[64,4096]{1,0:T(8,128)S(1)}) custom-call(bf16[64,4096]{1,0:T(8,128)(2,1)S(1)} %collective-permute-done.4.x_ref, bf16[64,512]{1,0:T(8,128)(2,1)S(1)} %get-tuple-element.30.grouped_ref, bf16[4096,512]{1,0:T(8,128)(2,1)} %bitcast.19), custom_call_target="tpu_custom_call" | custom-call | flops 536870912 | bytes 6356992 | tf_op jit(solution)/shard_map/pallas_call | solution.py:34
  78.0 0.9 %finished.5 = bf16[64,4096]{1,0:T(8,128)(2,1)} custom-call(s32[2,2,128]{2,1,0:T(2,128)S(1)} %broadcast_in_dim.31.match_ref, f32[64,4096]{1,0:T(8,128)S(1)} %get-tuple-element.34.through_ref, bf16[4,16,4096]{2,1,0:T(8,128)(2,1)S(1)} %bitcast.16), custom_call_target="tpu_custom_call" | custom-call | flops 524288 | bytes 2097152 | tf_op jit(solution)/shard_map/finished/pallas_call | solution.py:363
  78.9 0.5 shard_map.105.keep_ref
  79.4 1.0 %combine.1 = f32[512,512]{1,0:T(8,128)} custom-call(f32[512,512]{1,0:T(8,128)S(1)} %shard_map.105.keep_ref, f32[512,512]{1,0:T(8,128)S(1)} %collective-permute-done.14.got_ref), custom_call_target="tpu_custom_call" | custom-call | flops 524288 | bytes 3145728 | tf_op jit(solution)/shard_map/combine/pallas_call | solution.py:246
  (16 shorter events, 0.2 us)
Async XLA Ops:
  0.6 48.5 %copy-start = (bf16[1,64,4096]{2,1,0:T(8,128)(2,1)S(1)}, bf16[1,64,4096]{2,1,0:T(8,128)(2,1)}, u32[]{:S(2)}) copy-start(bf16[1,64,4096]{2,1,0:T(8,128)(2,1)} %param.9) | copy-start | bytes 1572868
  0.6 24.3 %collective-permute-start = (bf16[64,4096]{1,0:T(8,128)(2,1)}, bf16[64,4096]{1,0:T(8,128)(2,1)S(1)}, u32[]{:S(2)}, u32[]{:S(2)}) collective-permute-start(bf16[64,4096]{1,0:T(8,128)(2,1)} %bitcast.26), channel_id=1, source_target_pairs={{0,8},{8,16},{16,24},{24,0},{1,9},{9,17},{17,25},{25,1},{2,10},{10... | collective-permute-start | bytes 1572872 | tf_op jit(solution)/shard_map/ppermute | solution.py:25
  6.0 18.9 %collective-permute-start.1 = (bf16[1,16,4096]{2,1,0:T(8,128)(2,1)S(1)}, bf16[1,16,4096]{2,1,0:T(8,128)(2,1)S(1)}, u32[]{:S(2)}, u32[]{:S(2)}) collective-permute-start(bf16[1,16,4096]{2,1,0:T(8,128)(2,1)S(1)} %get-tuple-element.24), channel_id=1, source_target_pairs={{0,24},{8,0},{16,8},{24,16},{1,25},{9,1},{17,9},{25,17},{2,26},{10... | collective-permute-start | bytes 393224 | tf_op jit(solution)/shard_map/ppermute | solution.py:25
  8.1 16.7 %collective-permute-start.2 = (bf16[1,16,4096]{2,1,0:T(8,128)(2,1)S(1)}, bf16[1,16,4096]{2,1,0:T(8,128)(2,1)S(1)}, u32[]{:S(2)}, u32[]{:S(2)}) collective-permute-start(bf16[1,16,4096]{2,1,0:T(8,128)(2,1)S(1)} %get-tuple-element.25), channel_id=1, source_target_pairs={{0,24},{8,0},{16,8},{24,16},{1,25},{9,1},{17,9},{25,17},{2,26},{10... | collective-permute-start | bytes 393224 | tf_op jit(solution)/shard_map/ppermute | solution.py:25
  10.1 14.2 %collective-permute-start.3 = (bf16[2,16,512]{2,1,0:T(8,128)(2,1)S(1)}, bf16[2,16,512]{2,1,0:T(8,128)(2,1)S(1)}, u32[]{:S(2)}, u32[]{:S(2)}) collective-permute-start(bf16[2,16,512]{2,1,0:T(8,128)(2,1)S(1)} %get-tuple-element.26), channel_id=1, source_target_pairs={{0,24},{8,0},{16,8},{24,16},{1,25},{9,1},{17,9},{25,17},{2,26},{10... | collective-permute-start | bytes 98312 | tf_op jit(solution)/shard_map/ppermute | solution.py:25
  10.5 26.4 %collective-permute-start.4 = (bf16[64,4096]{1,0:T(8,128)(2,1)}, bf16[64,4096]{1,0:T(8,128)(2,1)S(1)}, u32[]{:S(2)}, u32[]{:S(2)}) collective-permute-start(bf16[64,4096]{1,0:T(8,128)(2,1)} %bitcast.27), channel_id=1, source_target_pairs={{0,24},{8,0},{16,8},{24,16},{1,25},{9,1},{17,9},{25,17},{2,26},{10... | collective-permute-start | bytes 1572872 | tf_op jit(solution)/shard_map/ppermute | solution.py:25
  24.3 12.6 %collective-permute-start.5 = (bf16[64,512]{1,0:T(8,128)(2,1)S(1)}, bf16[64,512]{1,0:T(8,128)(2,1)S(1)}, u32[]{:S(2)}, u32[]{:S(2)}) collective-permute-start(bf16[64,512]{1,0:T(8,128)(2,1)S(1)} %get-tuple-element.29), channel_id=1, source_target_pairs={{0,8},{8,16},{16,24},{24,0},{1,9},{9,17},{17,25},{25,1},{2,10},{10... | collective-permute-start | bytes 196616 | tf_op jit(solution)/shard_map/ppermute | solution.py:25
  25.3 15.0 %collective-permute-start.11 = (bf16[3,64,512]{2,1,0:T(8,128)(2,1)S(1)}, bf16[3,64,512]{2,1,0:T(8,128)(2,1)S(1)}, u32[]{:S(2)}, u32[]{:S(2)}) collective-permute-start(bf16[3,64,512]{2,1,0:T(8,128)(2,1)S(1)} %get-tuple-element.40), channel_id=1, source_target_pairs={{0,2},{1,3},{2,0},{3,1},{4,6},{5,7},{6,4},{7,5},{8,10},{9,11},{10,... | collective-permute-start | bytes 589832 | tf_op jit(solution)/shard_map/ppermute | solution.py:414
  26.8 14.0 %collective-permute-start.12 = (bf16[3,64,512]{2,1,0:T(8,128)(2,1)S(1)}, bf16[3,64,512]{2,1,0:T(8,128)(2,1)S(1)}, u32[]{:S(2)}, u32[]{:S(2)}) collective-permute-start(bf16[3,64,512]{2,1,0:T(8,128)(2,1)S(1)} %get-tuple-element.41), channel_id=1, source_target_pairs={{0,4},{1,5},{2,6},{3,7},{4,0},{5,1},{6,2},{7,3},{8,12},{9,13},{10,... | collective-permute-start | bytes 589832 | tf_op jit(solution)/shard_map/ppermute | solution.py:414
  28.3 12.5 %collective-permute-start.13 = (bf16[3,64,512]{2,1,0:T(8,128)(2,1)S(1)}, bf16[3,64,512]{2,1,0:T(8,128)(2,1)S(1)}, u32[]{:S(2)}, u32[]{:S(2)}) collective-permute-start(bf16[3,64,512]{2,1,0:T(8,128)(2,1)S(1)} %get-tuple-element.42), channel_id=1, source_target_pairs={{0,6},{1,7},{2,4},{3,5},{4,2},{5,3},{6,0},{7,1},{8,14},{9,15},{10,... | collective-permute-start | bytes 589832 | tf_op jit(solution)/shard_map/ppermute | solution.py:414
  37.2 8.7 %collective-permute-start.10 = (bf16[3,64,512]{2,1,0:T(8,128)(2,1)S(1)}, bf16[3,64,512]{2,1,0:T(8,128)(2,1)S(1)}, u32[]{:S(2)}, u32[]{:S(2)}) collective-permute-start(bf16[3,64,512]{2,1,0:T(8,128)(2,1)S(1)} %get-tuple-element.38), channel_id=1, source_target_pairs={{0,6},{1,7},{2,4},{3,5},{4,2},{5,3},{6,0},{7,1},{8,14},{9,15},{10,... | collective-permute-start | bytes 589832 | tf_op jit(solution)/shard_map/ppermute | solution.py:414
  39.7 8.8 %collective-permute-start.8 = (bf16[3,64,512]{2,1,0:T(8,128)(2,1)S(1)}, bf16[3,64,512]{2,1,0:T(8,128)(2,1)S(1)}, u32[]{:S(2)}, u32[]{:S(2)}) collective-permute-start(bf16[3,64,512]{2,1,0:T(8,128)(2,1)S(1)} %get-tuple-element.36), channel_id=1, source_target_pairs={{0,2},{1,3},{2,0},{3,1},{4,6},{5,7},{6,4},{7,5},{8,10},{9,11},{10,... | collective-permute-start | bytes 589832 | tf_op jit(solution)/shard_map/ppermute | solution.py:414
  40.3 8.3 %collective-permute-start.9 = (bf16[3,64,512]{2,1,0:T(8,128)(2,1)S(1)}, bf16[3,64,512]{2,1,0:T(8,128)(2,1)S(1)}, u32[]{:S(2)}, u32[]{:S(2)}) collective-permute-start(bf16[3,64,512]{2,1,0:T(8,128)(2,1)S(1)} %get-tuple-element.37), channel_id=1, source_target_pairs={{0,4},{1,5},{2,6},{3,7},{4,0},{5,1},{6,2},{7,3},{8,12},{9,13},{10,... | collective-permute-start | bytes 589832 | tf_op jit(solution)/shard_map/ppermute | solution.py:414
  49.1 30.4 %collective-permute-start.14 = (f32[512,512]{1,0:T(8,128)S(1)}, f32[512,512]{1,0:T(8,128)S(1)}, u32[]{:S(2)}, u32[]{:S(2)}) collective-permute-start(f32[512,512]{1,0:T(8,128)S(1)} %shard_map.106), channel_id=1, source_target_pairs={{0,1},{1,0},{2,3},{3,2},{4,5},{5,4},{6,7},{7,6},{8,9},{9,8},{10,11... | collective-permute-start | bytes 3145736 | tf_op jit(solution)/shard_map/ppermute | solution.py:437
  49.2 28.8 %collective-permute-start.7 = (bf16[64,4096]{1,0:T(8,128)(2,1)S(1)}, bf16[64,4096]{1,0:T(8,128)(2,1)S(1)}, u32[]{:S(2)}, u32[]{:S(2)}) collective-permute-start(bf16[64,4096]{1,0:T(8,128)(2,1)S(1)} %bitcast.25), channel_id=1, source_target_pairs={{0,8},{8,16},{16,24},{24,0},{1,9},{9,17},{17,25},{25,1},{2,10},{10... | collective-permute-start | bytes 1572872 | tf_op jit(solution)/shard_map/ppermute | solution.py:25
  49.8 22.5 %collective-permute-start.6 = (bf16[2,16,4096]{2,1,0:T(8,128)(2,1)S(1)}, bf16[2,16,4096]{2,1,0:T(8,128)(2,1)S(1)}, u32[]{:S(2)}, u32[]{:S(2)}) collective-permute-start(bf16[2,16,4096]{2,1,0:T(8,128)(2,1)S(1)} %get-tuple-element.33), channel_id=1, source_target_pairs={{0,24},{8,0},{16,8},{24,16},{1,25},{9,1},{17,9},{25,17},{2,26},{10... | collective-permute-start | bytes 786440 | tf_op jit(solution)/shard_map/ppermute | solution.py:25
